TPU v7x, 256 devices: a whole 4x4x8 slice. The times are simulated.
256 devices in a mesh: section: 4 (over y), row: 4 (over x), col: 16 (over z, core).
Axes of the slice: x: 4, y: 4, z: 8, core: 2. Of those that a mesh axis runs over, the one named last changes fastest.
Arguments:
- hidden: bfloat16 [4, 256, 2, 3072], P(None, ('row', 'col')), may hold values from -6 to 6
- patch_counts: int32 [2, 4], replicated, may hold values from 128 to 256, as said below
- timestep: int32 [1], replicated, may hold values from 0 to 999
- time_table: float32 [1000, 512], replicated, may hold values from -6 to 6
- ada_weight: bfloat16 [4, 512, 18432], P('section', None, ('row', 'col')), may hold values from -0.25 to 0.25
- qkv_weight: bfloat16 [4, 3072, 9216], P('section', None, 'col'), may hold values from -0.109375 to 0.109375
- out_weight: bfloat16 [4, 3072, 3072], P('section', 'col'), may hold values from -0.109375 to 0.109375
- qk_gain: float32 [4, 2, 64], P('section'), may hold values from 1 to 3
- stale_kv: bfloat16 [4, 1024, 2, 48, 128], P('section', None, None, 'col'), may hold values from -8 to 8
- stale_inputs: bfloat16 [4, 64, 2, 3072], P('section', ('row', 'col')), may hold values from -6 to 6
- recompute_slots: int32 [2, 64], replicated, may hold values from 0 to 1023, as said below
Outputs:
- layer_outputs: bfloat16 [4, 4, 256, 2, 3072], P('section', None, ('row', 'col'))
Inputs may be any that keep to these rules, and one draw needn't show every extreme that they name: `patch_counts`: in every request one patch holds exactly 256 live tokens and another exactly 128. `recompute_slots`: the slots of one request are distinct.
All inputs are finite; a program needn't handle non-finite values.
Results may differ from a plain program's by a relative error of at most 0.035.
Values may be sent and summed in bfloat16 or wider, within the bound.
No kernel may reach another device: no remote copies, remote signals or barrier semaphores. Data moves between devices by JAX's collectives and lax.ppermute only.
A program may use at most 64 MiB of HBM per device.

v0:
```python
import jax
import jax.numpy as jnp
import numpy as np
from jax import lax
from jax.experimental import pallas as pl
from jax.experimental.pallas import tpu as pltpu
from jax.sharding import Mesh
from jax.sharding import PartitionSpec as P

HD = 64
D = 3072
TXT = 226
GH = 30
GW = 45
PLEN = 256
GROUP = 128
REC_GROUP = 32
BF = jnp.bfloat16
F32 = jnp.float32
COL = ("z", "core")
ROW = ("req", "half")
ROW_AXES = ("req", "half", "z", "core")


SMEM = pl.BlockSpec(memory_space=pltpu.SMEM)
VMEM = pl.BlockSpec(memory_space=pltpu.VMEM)
HBM = pl.BlockSpec(memory_space=pltpu.HBM)


def call(kernel, out_shape, in_specs, name, out_specs=None, scratch=(), aliases=None):
    if out_specs is None:
        out_specs = jax.tree.map(lambda _: VMEM, out_shape)
    return pl.pallas_call(
        kernel,
        out_shape=out_shape,
        in_specs=in_specs,
        out_specs=out_specs,
        scratch_shapes=list(scratch),
        input_output_aliases=aliases or {},
        compiler_params=pltpu.CompilerParams(vmem_limit_bytes=24 * 1024 * 1024),
        name=name,
    )


def iota(shape, dim):
    return lax.broadcasted_iota(jnp.int32, shape, dim)


def shape_of(shape, dtype):
    return jax.ShapeDtypeStruct(shape, dtype)


def frequencies():
    parts = []
    for size in (HD // 4, HD * 3 // 8, HD * 3 // 8):
        rate = 1.0 / np.float32(10000.0) ** (
            np.arange(0, size, 2).astype(np.float32) / np.float32(size)
        )
        parts.append(np.repeat(rate.astype(np.float32), 2))
    rate = np.concatenate(parts)
    return np.concatenate([rate, rate])[None, :].astype(np.float32)


def offset_in_patch(index, half):
    return (2 * ((index >> 2) & 1) + half) * 64 + 4 * (index >> 3) + (index & 3)


def prepare_kernel(scalars, row_ref, ada_ref, rate_ref, rec_ref, mod_out, cos_out, sin_out, text_out):
    half = scalars[0]
    time_row = row_ref[pl.ds(scalars[5], 1), :]
    embedding = (time_row / (1.0 + jnp.exp(-time_row))).astype(BF)
    embedding = jnp.broadcast_to(embedding, (8, embedding.shape[1]))
    part = lax.dot_general(
        embedding, ada_ref[...], (((1,), (1,)), ((), ())), preferred_element_type=F32
    )[0:1]
    high = part.astype(BF)
    mod_out[0:1, :] = high
    mod_out[1:2, :] = (part - high.astype(F32)).astype(BF)

    rate = rate_ref[...]

    def tables(position, rows, at):
        text = position < TXT
        index = jnp.maximum(position - TXT, 0).astype(F32)
        frame = jnp.floor((index + 0.5) * (1.0 / (GH * GW)))
        line = jnp.floor((index + 0.5) * (1.0 / GW))
        width = index - line * GW
        height = line - jnp.floor((line + 0.5) * (1.0 / GH)) * GH
        lane = iota((rows, 128), 1) & (HD - 1)
        coordinate = jnp.where(lane < HD // 4, frame, jnp.where(lane < HD // 4 + HD * 3 // 8, height, width))
        phase = coordinate * rate
        cos_out[at : at + rows, :] = jnp.where(text, 1.0, jnp.cos(phase))
        sin_out[at : at + rows, :] = jnp.where(text, 0.0, jnp.sin(phase))
        text_out[at : at + rows, :] = jnp.where(text, 1.0, 0.0)

    tables(offset_in_patch(iota((GROUP, 128), 0), half) + scalars[6], GROUP, 0)
    slot = rec_ref[...]
    start = jnp.where(
        slot < PLEN,
        scalars[1],
        jnp.where(slot < 2 * PLEN, scalars[2], jnp.where(slot < 3 * PLEN, scalars[3], scalars[4])),
    )
    tables(start + (slot & (PLEN - 1)), REC_GROUP, GROUP)


def normalize(x_ref, mod_ref, layer, text_ref, norm_ref):
    chunks = D // 128
    rows = x_ref.shape[0]
    text = text_ref[...] > 0.5

    def over_chunks(step, start):
        return lax.fori_loop(0, chunks, lambda k, carry: step(pl.ds(pl.multiple_of(k * 128, 128), 128), carry), start, unroll=6)

    def add(lanes, total):
        return total + x_ref[:, lanes].astype(F32)

    mean = jnp.sum(over_chunks(add, jnp.zeros((rows, 128), F32)), axis=1, keepdims=True) * (1.0 / D)

    def add_square(lanes, total):
        centered = x_ref[:, lanes].astype(F32) - mean
        return total + centered * centered

    total = jnp.sum(over_chunks(add_square, jnp.zeros((rows, 128), F32)), axis=1, keepdims=True)
    factor = lax.rsqrt(total * (1.0 / D) + 1e-5)

    def write(lanes, carry):
        shift = jnp.where(text, mod_ref[layer, 3:4, lanes], mod_ref[layer, 0:1, lanes])
        scale = jnp.where(text, mod_ref[layer, 4:5, lanes], mod_ref[layer, 1:2, lanes])
        centered = x_ref[:, lanes].astype(F32) - mean
        norm_ref[:, lanes] = (centered * factor * (1.0 + scale) + shift).astype(BF)
        return carry

    over_chunks(write, 0)


def heads_from(mixed, gain_ref, cos_ref, sin_ref, q_out, kv_out):
    rows = mixed.shape[0]
    lane = iota((128, 128), 1)
    block = jnp.where((iota((128, 128), 0) >> 6) == (lane >> 6), 1.0 / HD, 0.0).astype(BF)

    def group_mean(values):
        high = values.astype(BF)
        low = (values - high.astype(F32)).astype(BF)
        return jnp.dot(high, block, preferred_element_type=F32) + jnp.dot(
            low, block, preferred_element_type=F32
        )

    low_half = iota((rows, 128), 1) < HD
    even = (iota((rows, 128), 1) & 1) == 0
    cosine, sine = cos_ref[...], sin_ref[...]
    gain_q = gain_ref[0:1, :]
    gain_k = gain_ref[1:2, :]
    gains = (
        jnp.where(low_half, gain_q, gain_k),
        jnp.broadcast_to(gain_q, (rows, 128)),
        jnp.broadcast_to(gain_k, (rows, 128)),
        jnp.where(low_half, gain_q, gain_k),
    )
    plain, turned = [], []
    for k in range(4):
        values = mixed[:, 128 * k : 128 * k + 128]
        plain.append(values)
        centered = values - group_mean(values)
        scaled = centered * lax.rsqrt(group_mean(centered * centered) + 1e-6) * gains[k]
        partner = jnp.where(even, -pltpu.roll(scaled, 127, 1), pltpu.roll(scaled, 1, 1))
        turned.append(scaled * cosine + partner * sine)
    last = jnp.concatenate([mixed[:, 512:576], jnp.zeros((rows, 64), F32)], axis=1)
    keys_values = (
        pltpu.roll(jnp.where(low_half, plain[1], turned[0]), 64, 1).astype(BF),
        jnp.where(low_half, turned[2], plain[2]).astype(BF),
        pltpu.roll(jnp.where(low_half, last, turned[3]), 64, 1).astype(BF),
    )
    for copy in range(kv_out.shape[0]):
        for head in range(3):
            kv_out[copy, :, 128 * head : 128 * head + 128] = keys_values[head]
    if q_out is None:
        return
    zero = jnp.zeros((rows, 128), F32)
    q_out[:, 0:128] = (jnp.where(low_half, turned[0], zero) * 0.125).astype(BF)
    q_out[:, 128:256] = (jnp.where(low_half, pltpu.roll(turned[1], 64, 1), zero) * 0.125).astype(BF)
    q_out[:, 256:384] = (jnp.where(low_half, turned[3], zero) * 0.125).astype(BF)


def times_weights(norm, weights):
    return lax.dot_general(norm, weights, (((1,), (1,)), ((), ())), preferred_element_type=F32)


def rec_kernel(scalars, x_ref, mod_ref, gain_ref, cos_ref, sin_ref, text_ref, w_ref, kv_out, norm_ref, w_vmem, sem):
    fetch = pltpu.make_async_copy(w_ref, w_vmem, sem)
    fetch.start()
    normalize(x_ref, mod_ref, scalars[7], text_ref, norm_ref)
    fetch.wait()
    heads_from(times_weights(norm_ref[...], w_vmem[...]), gain_ref, cos_ref, sin_ref, None, kv_out)


def qkv_kernel_of(layer):
    def qkv_kernel(x_ref, mod_ref, gain_ref, cos_ref, sin_ref, text_ref, packed_ref, q_out, kv_out, weights_out, norm_ref, w_vmem, sems):
        def fetch(k):
            to = w_vmem.at[pl.ds(288 * (k % 2), 288), pl.ds(384 * (k // 2), 384)]
            return pltpu.make_async_copy(packed_ref.at[k, pl.ds(0, 288), :], to, sems.at[k])

        def pass_on(k):
            to = weights_out.at[pl.ds(96 * (k % 2), 96), pl.ds(384 * (k // 2), 384)]
            return pltpu.make_async_copy(packed_ref.at[k, pl.ds(288, 96), :], to, sems.at[16 + k])

        for k in range(16):
            fetch(k).start()
        for k in range(16):
            pass_on(k).start()
        normalize(x_ref, mod_ref, layer, text_ref, norm_ref)
        mixed = jnp.zeros((GROUP, 576), F32)
        for piece in range(4):
            for k in range(4 * piece, 4 * piece + 4):
                fetch(k).wait()
            lanes = slice(768 * piece, 768 * piece + 768)
            mixed = mixed + times_weights(norm_ref[:, lanes], w_vmem[:, lanes])
        heads_from(mixed, gain_ref, cos_ref, sin_ref, q_out, kv_out)
        for k in range(16):
            pass_on(k).wait()

    return qkv_kernel


def pack_kernel(scalars, w_ref, out_ref, base_ref, packed, sems):
    row = scalars[8]
    copies = []
    for k in range(4):
        lanes = pl.ds(pl.multiple_of(row * 768 + 384 * (k // 2), 128), 384)
        copies += [
            (w_ref.at[pl.ds(288 * (k % 2), 288), lanes], packed.at[k, pl.ds(0, 288), :]),
            (out_ref.at[pl.ds(96 * (k % 2), 96), lanes], packed.at[k, pl.ds(288, 96), :]),
            (base_ref.at[k], packed.at[k, pl.ds(384, 128), :]),
        ]
    copies = [pltpu.make_async_copy(a, b, sems.at[n]) for n, (a, b) in enumerate(copies)]
    for copy in copies:
        copy.start()
    for copy in copies:
        copy.wait()


def attend(scalars, q_ref, cache_ref, keep_out, send_out):
    patch, core = scalars[7], scalars[9]
    key = iota((8, 1024), 1)
    key_patch = key >> 8
    within = key & (PLEN - 1)
    fresh_offset = (2 * ((within >> 2) & 1) + (within >> 7)) * 64 + 4 * ((within >> 3) & 15) + (within & 3)
    offset = jnp.where(key_patch <= patch, fresh_offset, within)
    count = jnp.where(
        key_patch == 0,
        scalars[11],
        jnp.where(key_patch == 1, scalars[12], jnp.where(key_patch == 2, scalars[13], scalars[14])),
    )
    live = (offset < count)[0:1]
    outs = []
    for head in range(3):
        lanes = slice(128 * head, 128 * head + 128)
        keys_values = cache_ref[:, lanes]
        scores = lax.dot_general(
            q_ref[:, lanes], keys_values, (((1,), (1,)), ((), ())), preferred_element_type=F32
        )
        weights = jnp.where(live, jnp.exp(scores), 0.0)
        total = jnp.sum(weights, axis=1, keepdims=True)
        mixed = jnp.dot(weights.astype(BF), keys_values, preferred_element_type=F32)
        outs.append(mixed / total)
    low = iota((GROUP, 128), 1) < HD
    first = jnp.where(low, pltpu.roll(outs[0], 64, 1), outs[1]).astype(BF)
    second = jnp.where(low, pltpu.roll(outs[2], 64, 1), 0.0).astype(BF)
    for z in range(8):
        to = slice(8 * z, 8 * z + 8)
        even, odd = slice(16 * z, 16 * z + 8), slice(16 * z + 8, 16 * z + 16)
        for value, lanes in ((first, slice(0, 128)), (second, slice(128, 256))):
            keep_out[to, lanes] = jnp.where(core == 0, value[even], value[odd])
            send_out[to, lanes] = jnp.where(core == 0, value[odd], value[even])


def attend_kernel_of(layer):
    def attend_kernel(
        scalars, q_ref, fresh_ref, rec_ref, target_ref, packed_ref, own_hbm, other_hbm,
        keep_out, send_out, weights_out, base_ref, cache_ref, rec_vmem, sems,
    ):
        section, req = scalars[7], scalars[15]
        rec_copies = [
            pltpu.make_async_copy(
                rec_ref.at[2 * layer + h], rec_vmem.at[pl.ds(REC_GROUP * h, REC_GROUP), :], sems.at[18 + h]
            )
            for h in range(2)
        ]
        for copy in rec_copies:
            copy.start()
        from_base = []
        for k in range(16):
            rows = pl.ds(pl.multiple_of(384 + 64 * req, 64), 64)
            from_base.append(
                pltpu.make_async_copy(packed_ref.at[k, rows, :], base_ref.at[pl.ds(64 * k, 64), :], sems.at[k])
            )
        weights = [
            pltpu.make_async_copy(own_hbm, weights_out.at[0], sems.at[16]),
            pltpu.make_async_copy(other_hbm, weights_out.at[1], sems.at[17]),
        ]
        for copy in from_base + weights:
            copy.start()
        rec_vmem[64:, :] = jnp.zeros((64, 384), BF)
        match = iota((1024, 128), 0) == target_ref[0:1, :]
        chosen = jnp.where(match, 1.0, 0.0)
        hit = jnp.sum(chosen, axis=1, keepdims=True) > 0.5
        for copy in rec_copies:
            copy.wait()
        placed = jnp.dot(chosen.astype(BF), rec_vmem[...], preferred_element_type=F32)
        for copy in from_base:
            copy.wait()
        for patch in range(4):
            rows = slice(PLEN * patch, PLEN * patch + PLEN)

            @pl.when(patch <= section)
            def _(patch=patch, rows=rows):
                cache_ref[rows, :] = jnp.concatenate([fresh_ref[2 * patch], fresh_ref[2 * patch + 1]], axis=0)

            @pl.when(patch > section)
            def _(rows=rows):
                cache_ref[rows, :] = jnp.where(hit[rows], placed[rows], base_ref[rows, :].astype(F32)).astype(BF)

        attend(scalars, q_ref, cache_ref, keep_out, send_out)
        for copy in weights:
            copy.wait()

    return attend_kernel


def project_kernel(keep_ref, got_ref, weights_ref, out_ref):
    out = jnp.dot(keep_ref[:, 0:192], weights_ref[0], preferred_element_type=F32)
    out = out + jnp.dot(got_ref[:, 0:192], weights_ref[1], preferred_element_type=F32)
    out_ref[...] = out.astype(BF)


def residual_kernel_of(layer):
    def residual_kernel(scalars, parts_ref, x_ref, mod_ref, out_ref):
        row = iota((8, 128), 0)
        offset = (2 * (row >> 2) + scalars[0]) * 64 + 4 * scalars[10] + (row & 3)
        text = (offset + scalars[6]) < TXT
        for k in range(D // 128):
            lanes = slice(128 * k, 128 * k + 128)
            total = parts_ref[0, :, lanes].astype(F32)
            for source in range(1, 8):
                total = total + parts_ref[source, :, lanes].astype(F32)
            gate = jnp.where(text, mod_ref[layer, 5:6, lanes], mod_ref[layer, 2:3, lanes])
            out_ref[:, lanes] = (x_ref[:, lanes].astype(F32) + gate * total).astype(BF)

    return residual_kernel


def time_block(timestep, time_table):
    return lax.dynamic_slice(time_table, ((timestep[0] // 8) * 8, 0), (8, time_table.shape[1]))


def swapped(value, axis):
    return lax.ppermute(value, axis, [(0, 1), (1, 0)])


def local(
    hidden,
    patch_counts,
    timestep,
    time_table,
    ada_weight,
    qkv_weight,
    out_weight,
    qk_gain,
    stale_kv,
    stale_inputs,
    recompute_slots,
):
    section = lax.axis_index("section")
    req = lax.axis_index("req")
    half = lax.axis_index("half")
    core = lax.axis_index("core")
    col = lax.axis_index("z") * 2 + core
    first_req = req == 0
    sections = lax.axis_size("section")
    patches = hidden.shape[0]

    def of_request(value, axis):
        both = [lax.index_in_dim(value, r, axis, keepdims=False) for r in range(2)]
        return jnp.where(first_req, both[0], both[1]), jnp.where(first_req, both[1], both[0])

    def by_request(value, got):
        own = [lax.index_in_dim(value, r, 1, keepdims=False) for r in range(2)]
        far = [lax.index_in_dim(got, r, 1, keepdims=False) for r in range(2)]
        return jnp.where(
            first_req, jnp.concatenate([own[0], far[0]], axis=0), jnp.concatenate([far[1], own[1]], axis=0)
        )

    patch_rows = lax.dynamic_index_in_dim(hidden, section, 0, keepdims=False)
    tokens = by_request(patch_rows, swapped(patch_rows, "req"))
    rec_tokens = by_request(stale_inputs[0], swapped(stale_inputs[0], "req"))

    counts, _ = of_request(patch_counts, 0)
    starts = jnp.stack([jnp.int32(0), counts[0], counts[0] + counts[1], counts[0] + counts[1] + counts[2]])
    slots, _ = of_request(recompute_slots, 0)
    slots = slots.reshape(2, 2, 16)
    by_half = [slots[:, h].T.reshape(REC_GROUP) for h in range(2)]
    target_own = jnp.where(half == 0, by_half[0], by_half[1])
    targets = jnp.concatenate(by_half + [jnp.full((64,), -1, jnp.int32)])
    targets = jnp.broadcast_to(targets[None, :], (8, 128))

    own_start = lax.dynamic_index_in_dim(starts, section, 0, keepdims=True)
    row_index = req * 2 + half
    scalars = jnp.concatenate(
        [half[None], starts, timestep % 8, own_start, jnp.stack([section, row_index, core, col]), counts, req[None]]
    ).astype(jnp.int32)
    table_rows = shape_of((GROUP + REC_GROUP, 128), F32)
    mod_part, cosine, sine, text = call(
        prepare_kernel,
        (shape_of((2, 288), BF), table_rows, table_rows, table_rows),
        [SMEM, VMEM, VMEM, VMEM, VMEM],
        "prepare",
    )(
        scalars,
        time_block(timestep, time_table),
        ada_weight[0].T,
        jnp.asarray(frequencies()),
        jnp.broadcast_to(target_own[:, None], (REC_GROUP, 128)),
    )

    stale_rows = lax.dynamic_slice_in_dim(stale_kv[0], row_index * 256, 256, 0)
    stale_rows = jnp.transpose(stale_rows.reshape(4, 64, 2, 384), (0, 2, 1, 3)).reshape(4, 128, 384)
    weights_qkv = qkv_weight[0].T
    packed = call(
        pack_kernel,
        shape_of((4, 512, 384), BF),
        [SMEM, HBM, HBM, HBM],
        "pack",
        out_specs=HBM,
        scratch=[pltpu.SemaphoreType.DMA((12,))],
    )(scalars, weights_qkv, out_weight[0], stale_rows)
    chunks = lax.all_to_all(packed, "section", 0, 0)
    layers = [
        lax.all_gather(chunks[layer], ("req", "half", "section"), axis=0, tiled=False) for layer in range(sections)
    ]

    payload = jnp.concatenate(
        [
            tokens,
            rec_tokens.reshape(8, 768),
            jnp.pad(mod_part.reshape(8, 72), ((0, 0), (0, 56))),
        ],
        axis=1,
    )
    gathered = lax.all_gather(payload, COL, axis=0, tiled=True)
    rec_rows = gathered[:, D : D + 768].reshape(REC_GROUP, D)
    pieces = gathered[:, D + 768 : D + 840].reshape(16, 2, 288).astype(F32)
    summed = pieces[:, 0] + pieces[:, 1]
    gain_row = jnp.pad(qk_gain[0].reshape(1, 128), ((0, 0), (0, 160)))
    rows = lax.all_gather(jnp.concatenate([summed, gain_row], axis=0), ("section",) + ROW, axis=0, tiled=False)
    modulation = rows[:, :16].reshape(sections, 6, D)
    all_gains = rows.reshape(sections, 4, 17, 288)[:, 0, 16, :128].reshape(sections, 2, HD)
    all_gains = jnp.concatenate([all_gains, all_gains], axis=2)
    own_gains = jnp.concatenate([qk_gain[0], qk_gain[0]], axis=1)

    peers = ("section", "half")
    copies = lax.axis_size(peers)

    rec_fresh = call(
        rec_kernel,
        shape_of((copies, REC_GROUP, 384), BF),
        [SMEM] + [VMEM] * 6 + [HBM],
        "rec",
        scratch=[pltpu.VMEM((REC_GROUP, D), BF), pltpu.VMEM((576, D), BF), pltpu.SemaphoreType.DMA],
    )(scalars, rec_rows, modulation, own_gains, cosine[GROUP:], sine[GROUP:], text[GROUP:], weights_qkv)
    rec_all = lax.all_to_all(rec_fresh, peers, 0, 0)
    cosine, sine, text = cosine[:GROUP], sine[:GROUP], text[:GROUP]

    half_rows = shape_of((64, 256), BF)
    group, rec_all = lax.optimization_barrier((gathered[:, :D], rec_all))
    current, outs = tokens, []
    for layer in range(sections):
        packed = pltpu.with_memory_space_constraint(layers[layer], pltpu.HBM)
        if layer > 0:
            group = lax.all_gather(current, COL, axis=0, tiled=True)
        queries, fresh, out_own = call(
            qkv_kernel_of(layer),
            (shape_of((GROUP, 384), BF), shape_of((copies, GROUP, 384), BF), shape_of((192, D), BF)),
            [VMEM] * 6 + [HBM],
            "qkv",
            out_specs=(VMEM, VMEM, HBM),
            scratch=[pltpu.VMEM((GROUP, D), BF), pltpu.VMEM((576, D), BF), pltpu.SemaphoreType.DMA((32,))],
        )(group, modulation, all_gains[layer], cosine, sine, text, packed)
        out_other = swapped(out_own, "core")
        fresh = lax.all_to_all(fresh, peers, 0, 0)
        keep, send, weights_out = call(
            attend_kernel_of(layer),
            (half_rows, half_rows, shape_of((2, 192, D), BF)),
            [SMEM] + [VMEM] * 2 + [HBM, VMEM, HBM, HBM, HBM],
            "attend",
            scratch=[
                pltpu.VMEM((1024, 384), BF),
                pltpu.VMEM((1024, 384), BF),
                pltpu.VMEM((128, 384), BF),
                pltpu.SemaphoreType.DMA((20,)),
            ],
        )(scalars, queries, fresh, rec_all, targets, packed, out_own, out_other)
        projected = call(project_kernel, shape_of((64, D), BF), [VMEM] * 3, "project")(
            keep, swapped(send, "core"), weights_out
        )
        parts = lax.all_to_all(projected.reshape(8, 8, D), "z", 0, 0)
        current = call(residual_kernel_of(layer), shape_of((8, D), BF), [SMEM, VMEM, VMEM, VMEM], "residual")(
            scalars, parts, current, modulation
        )
        outs.append(current)

    leaving = jnp.stack(outs).reshape(sections * 2, 4, D)
    out = lax.all_to_all(leaving, ("section", "req"), 0, 0).reshape(patches, 2, 4, D)
    return jnp.transpose(out, (0, 2, 1, 3))[None]


def solution(mesh):
    sizes = tuple(mesh.devices.shape)
    fine = Mesh(
        mesh.devices.reshape(sizes[0], 2, sizes[1] // 2, sizes[2] // 2, 2),
        ("section", "req", "half", "z", "core"),
    )
    return jax.shard_map(
        local,
        mesh=fine,
        in_specs=(
            P(None, ROW_AXES, None, None),
            P(),
            P(),
            P(),
            P("section", None, ROW_AXES),
            P("section", None, COL),
            P("section", COL, None),
            P("section", None, None),
            P("section", None, None, COL, None),
            P("section", ROW_AXES, None, None),
            P(),
        ),
        out_specs=P("section", None, ROW_AXES, None, None),
        check_vma=False,
    )
```

profile of v0, /device:TPU:2, one launch (start us, length us, event | category | flops | bytes accessed | tf_op | source)
XLA Modules:
  0.0 425.9 jit_solution(6273918284357210508)
XLA Ops:
  7.4 0.8 broadcast_select_fusion.3
  8.1 0.8 fusion.14
  11.3 0.7 pad_add_fusion
  12.0 1.3 constant_dynamic-slice_fusion
  14.5 1.3 concatenate.31.scalars
  15.8 2.0 copy-done.2
  17.8 1.3 copy-done.4
  19.1 1.3 pack.1
  20.4 25.0 %all_to_all.55 = bf16[4,512,384]{2,1,0:T(8,128)(2,1)S(1)} all-to-all(bf16[4,512,384]{2,1,0:T(8,128)(2,1)S(1)} %pack.1), channel_id=1, replica_groups=mesh['section'=4,'req'=2,'half'=2,'z'=8,'core'=2] {'section'}, dimensions={0} | all-to-all | bytes 3145728 | tf_op jit(solution)/shard_map/all_to_all | solution.py:435
  45.4 1.2 fusion.11
  46.7 0.7 all-gather.9.cloned.1.call-update
  48.2 0.8 constant_dynamic-slice_fusion.2
  49.1 2.2 collective-permute-start
  51.3 1.4 collective-permute-start.1
  53.6 1.0 prepare.1
  54.7 1.8 collective-permute-done.1
  56.7 22.8 %all_gather.30 = bf16[128,3968]{1,0:T(8,128)(2,1)S(1)} all-gather(bf16[8,3968]{1,0:T(8,128)(2,1)S(1)} %fusion.1), channel_id=1, replica_groups=mesh['section'=4,'req'=2,'half'=2,'z'=8,'core'=2] {'z','core'}, dimensions={0}, use_global_device_ids=true | all-gather | bytes 1079296 | tf_op jit(solution)/shard_map/all_gather | solution.py:448
  79.7 24.3 %all-gather.1 = f32[16,17,288]{2,1,0:T(8,128)S(1)} all-gather(f32[1,17,288]{2,1,0:T(8,128)S(1)} %fusion.2), channel_id=2, replica_groups=mesh['section'=4,'req'=2,'half'=2,'z'=8,'core'=2] {'section','req','half'}, dimensions={0}, use_global_device_ids=true | all-gather | bytes 332928 | tf_op jit(solution)/shard_map/all_gather | solution.py:453
  104.4 2.1 copy-done.3
  106.5 3.9 rec.1
  110.4 4.6 %all-to-all-start = ((bf16[8,32,384]{2,1,0:T(8,128)(2,1)}), bf16[8,32,384]{2,1,0:T(8,128)(2,1)S(1)}, u32[]{:S(2)}, u32[]{:S(2)}) async-start(bf16[8,32,384]{2,1,0:T(8,128)(2,1)} %rec.1), calls=%async_computation | async-start | bytes 393216 | tf_op jit(solution)/shard_map/all_to_all | solution.py:469
  115.3 5.5 %all-to-all-done.rec_ref = bf16[8,32,384]{2,1,0:T(8,128)(2,1)S(1)} async-done(((bf16[8,32,384]{2,1,0:T(8,128)(2,1)}), bf16[8,32,384]{2,1,0:T(8,128)(2,1)S(1)}, u32[]{:S(2)}, u32[]{:S(2)}) %all-to-all-start) | async-done | bytes 196640 | tf_op jit(solution)/shard_map/all_to_all | solution.py:469
  120.8 38.0 %qkv.4 = (bf16[128,384]{1,0:T(8,128)(2,1)S(1)}, bf16[8,128,384]{2,1,0:T(8,128)(2,1)}, bf16[192,3072]{1,0:T(8,128)(2,1)}) custom-call(bf16[128,3072]{1,0:T(8,128)(2,1)S(1)} %slice.174.x_ref, f32[4,6,3072]{2,1,0:T(8,128)S(1)} %reshape.82.mod_ref, f32[2,128]{1,0:T(2,128)S(1)} %get-tuple-element.80.gain_ref, f32[128,128]{1,0:T(8,128)S(1)} %slice.154.cos_ref, ...), custom_call_target="tpu_custom_call" | custom-call | tf_op jit(solution)/shard_map/qkv/pallas_call | solution.py:479
  158.9 4.7 %all-to-all-start.2 = ((bf16[8,128,384]{2,1,0:T(8,128)(2,1)}), bf16[8,128,384]{2,1,0:T(8,128)(2,1)S(1)}, u32[]{:S(2)}, u32[]{:S(2)}) async-start(bf16[8,128,384]{2,1,0:T(8,128)(2,1)} %get-tuple-element.41), calls=%async_computation.2 | async-start | bytes 1572864 | tf_op jit(solution)/shard_map/all_to_all | solution.py:488
  163.7 18.5 %all-to-all-done.2.fresh_ref = bf16[8,128,384]{2,1,0:T(8,128)(2,1)S(1)} async-done(((bf16[8,128,384]{2,1,0:T(8,128)(2,1)}), bf16[8,128,384]{2,1,0:T(8,128)(2,1)S(1)}, u32[]{:S(2)}, u32[]{:S(2)}) %all-to-all-start.2) | async-done | bytes 786464 | tf_op jit(solution)/shard_map/all_to_all | solution.py:488
  182.1 3.1 attend.4
  185.4 1.1 collective-permute-done.3.got_ref
  187.1 19.7 %all_to_all.56.parts_ref = bf16[8,8,3072]{2,1,0:T(8,128)(2,1)S(1)} all-to-all(bf16[8,8,3072]{2,1,0:T(8,128)(2,1)S(1)} %bitcast.88), channel_id=1, replica_groups=mesh['section'=4,'req'=2,'half'=2,'z'=8,'core'=2] {'z'}, dimensions={0} | all-to-all | bytes 786432 | tf_op jit(solution)/shard_map/all_to_all | solution.py:504
  207.5 16.8 %all_gather.34.x_ref = bf16[128,3072]{1,0:T(8,128)(2,1)S(1)} all-gather(bf16[8,3072]{1,0:T(8,128)(2,1)S(1)} %residual.4.x_ref), channel_id=1, replica_groups=mesh['section'=4,'req'=2,'half'=2,'z'=8,'core'=2] {'z','core'}, dimensions={0}, use_global_device_ids=true | all-gather | bytes 835584 | tf_op jit(solution)/shard_map/all_gather | solution.py:478
  224.3 4.2 qkv.5
  228.9 26.2 %all_to_all.57.fresh_ref = bf16[8,128,384]{2,1,0:T(8,128)(2,1)S(1)} all-to-all(bf16[8,128,384]{2,1,0:T(8,128)(2,1)S(1)} %get-tuple-element.48), channel_id=1, replica_groups=mesh['section'=4,'req'=2,'half'=2,'z'=8,'core'=2] {'section','half'}, dimensions={0} | all-to-all | bytes 1572864 | tf_op jit(solution)/shard_map/all_to_all | solution.py:488
  255.2 3.0 attend.5
  258.3 1.2 collective-permute-done.5.got_ref
  260.0 17.7 %all_to_all.58.parts_ref = bf16[8,8,3072]{2,1,0:T(8,128)(2,1)S(1)} all-to-all(bf16[8,8,3072]{2,1,0:T(8,128)(2,1)S(1)} %bitcast.89), channel_id=1, replica_groups=mesh['section'=4,'req'=2,'half'=2,'z'=8,'core'=2] {'z'}, dimensions={0} | all-to-all | bytes 786432 | tf_op jit(solution)/shard_map/all_to_all | solution.py:504
  278.3 16.8 %all_gather.36.x_ref = bf16[128,3072]{1,0:T(8,128)(2,1)S(1)} all-gather(bf16[8,3072]{1,0:T(8,128)(2,1)S(1)} %residual.5.x_ref), channel_id=1, replica_groups=mesh['section'=4,'req'=2,'half'=2,'z'=8,'core'=2] {'z','core'}, dimensions={0}, use_global_device_ids=true | all-gather | bytes 835584 | tf_op jit(solution)/shard_map/all_gather | solution.py:478
  295.2 4.2 qkv.6
  299.8 20.7 %all_to_all.59.fresh_ref = bf16[8,128,384]{2,1,0:T(8,128)(2,1)S(1)} all-to-all(bf16[8,128,384]{2,1,0:T(8,128)(2,1)S(1)} %get-tuple-element.54), channel_id=1, replica_groups=mesh['section'=4,'req'=2,'half'=2,'z'=8,'core'=2] {'section','half'}, dimensions={0} | all-to-all | bytes 1572864 | tf_op jit(solution)/shard_map/all_to_all | solution.py:488
  320.5 3.0 attend.6
  323.6 1.2 collective-permute-done.7.got_ref
  325.4 17.7 %all_to_all.60.parts_ref = bf16[8,8,3072]{2,1,0:T(8,128)(2,1)S(1)} all-to-all(bf16[8,8,3072]{2,1,0:T(8,128)(2,1)S(1)} %bitcast.90), channel_id=1, replica_groups=mesh['section'=4,'req'=2,'half'=2,'z'=8,'core'=2] {'z'}, dimensions={0} | all-to-all | bytes 786432 | tf_op jit(solution)/shard_map/all_to_all | solution.py:504
  343.7 17.1 %all_gather.38.x_ref = bf16[128,3072]{1,0:T(8,128)(2,1)S(1)} all-gather(bf16[8,3072]{1,0:T(8,128)(2,1)S(1)} %residual.6.x_ref), channel_id=1, replica_groups=mesh['section'=4,'req'=2,'half'=2,'z'=8,'core'=2] {'z','core'}, dimensions={0}, use_global_device_ids=true | all-gather | bytes 835584 | tf_op jit(solution)/shard_map/all_gather | solution.py:478
  360.7 4.2 qkv.7
  365.4 16.9 %all_to_all.61.fresh_ref = bf16[8,128,384]{2,1,0:T(8,128)(2,1)S(1)} all-to-all(bf16[8,128,384]{2,1,0:T(8,128)(2,1)S(1)} %get-tuple-element.60), channel_id=1, replica_groups=mesh['section'=4,'req'=2,'half'=2,'z'=8,'core'=2] {'section','half'}, dimensions={0} | all-to-all | bytes 1572864 | tf_op jit(solution)/shard_map/all_to_all | solution.py:488
  382.3 3.0 attend.7
  385.4 1.2 collective-permute-done.9.got_ref
  387.2 18.7 %all_to_all.62.parts_ref = bf16[8,8,3072]{2,1,0:T(8,128)(2,1)S(1)} all-to-all(bf16[8,8,3072]{2,1,0:T(8,128)(2,1)S(1)} %bitcast.91), channel_id=1, replica_groups=mesh['section'=4,'req'=2,'half'=2,'z'=8,'core'=2] {'z'}, dimensions={0} | all-to-all | bytes 786432 | tf_op jit(solution)/shard_map/all_to_all | solution.py:504
  406.6 12.0 %all_to_all.63 = bf16[8,4,3072]{2,1,0:T(4,128)(2,1)S(1)} all-to-all(bf16[8,4,3072]{2,1,0:T(4,128)(2,1)S(1)} %reshape.90), channel_id=1, replica_groups=mesh['section'=4,'req'=2,'half'=2,'z'=8,'core'=2] {'section','req'}, dimensions={0} | all-to-all | bytes 393216 | tf_op jit(solution)/shard_map/all_to_all | solution.py:511
  418.6 0.8 copy.32
  (100 shorter events, 11.3 us)
Async XLA Ops:
  6.5 46.7 %copy-start = (f32[1000,512]{1,0:T(8,128)S(1)}, f32[1000,512]{1,0:T(8,128)}, u32[]{:S(2)}) copy-start(f32[1000,512]{1,0:T(8,128)} %param.15) | copy-start | bytes 6144004
  6.5 114.3 %all-gather.7.cloned.1.call-start = ((), (), s32[]{:S(2)}) async-start(), calls=%async_computation.11 | async-start | bytes 6684672 | tf_op jit(solution)/shard_map/all_gather | solution.py:437
  15.8 2.0 copy-start.2
  17.8 1.3 copy-start.4
  45.4 5.9 %copy-start.7 = (bf16[1,1,2,3072]{3,2,1,0:T(2,128)(2,1)S(1)}, bf16[1,1,2,3072]{3,2,1,0:T(2,128)(2,1)}, u32[]{:S(2)}) copy-start(bf16[1,1,2,3072]{3,2,1,0:T(2,128)(2,1)} %param.21) | copy-start | bytes 36868
  45.4 7.3 %copy-start.8 = (s32[2,64]{1,0:T(2,128)S(1)}, s32[2,64]{1,0:T(2,128)}, u32[]{:S(2)}) copy-start(s32[2,64]{1,0:T(2,128)} %param.22) | copy-start | bytes 1540
  46.6 6.7 %copy-start.9 = (f32[1,2,64]{2,1,0:T(2,128)S(1)}, f32[1,2,64]{2,1,0:T(2,128)}, u32[]{:S(2)}) copy-start(f32[1,2,64]{2,1,0:T(2,128)} %param.19) | copy-start | bytes 1540
  46.6 6.9 %copy-start.5 = (bf16[1,512,288]{1,2,0:T(8,128)(2,1)S(1)}, bf16[1,512,288]{1,2,0:T(8,128)(2,1)}, u32[]{:S(2)}) copy-start(bf16[1,512,288]{1,2,0:T(8,128)(2,1)} %param.16) | copy-start | bytes 884740
  46.6 6.9 %copy-start.6 = (f32[1,128]{1,0:T(1,128)S(1)}, f32[1,128]{1,0:T(1,128)}, u32[]{:S(2)}) copy-start(f32[1,128]{1,0:T(1,128)} %constant.84.clone.rate_ref) | copy-start | bytes 1540
  46.7 177.6 %all-gather.9.cloned.1.call-start = ((), (), s32[]{:S(2)}) async-start(), calls=%async_computation.12 | async-start | bytes 6684672 | tf_op jit(solution)/shard_map/all_gather | solution.py:437
  47.4 247.8 %all-gather.11.cloned.1.call-start = ((), (), s32[]{:S(2)}) async-start(), calls=%async_computation.13 | async-start | bytes 6684672 | tf_op jit(solution)/shard_map/all_gather | solution.py:437
  48.1 312.6 %all-gather.13.cloned.1.call-start = ((), (), s32[]{:S(2)}) async-start(), calls=%async_computation.14 | async-start | bytes 6684672 | tf_op jit(solution)/shard_map/all_gather | solution.py:437
  49.1 7.5 %collective-permute-start = (bf16[4,2,3072]{2,0,1:T(4,128)(2,1)S(1)}, bf16[4,2,3072]{2,0,1:T(4,128)(2,1)S(1)}, u32[]{:S(2)}, u32[]{:S(2)}) collective-permute-start(bf16[4,2,3072]{2,0,1:T(4,128)(2,1)S(1)} %bitcast.102), channel_id=1, source_target_pairs={{0,32},{32,0},{1,33},{33,1},{2,34},{34,2},{3,35},{35,3},{4,36},{36... | collective-permute-start | bytes 147464 | tf_op jit(solution)/shard_map/ppermute | solution.py:356
  51.3 5.2 %collective-permute-start.1 = (bf16[1,2,3072]{2,1,0:T(2,128)(2,1)S(1)}, bf16[1,2,3072]{2,1,0:T(2,128)(2,1)S(1)}, u32[]{:S(2)}, u32[]{:S(2)}) collective-permute-start(bf16[1,2,3072]{2,1,0:T(2,128)(2,1)S(1)} %bitcast.105), channel_id=1, source_target_pairs={{0,32},{32,0},{1,33},{33,1},{2,34},{34,2},{3,35},{35,3},{4,36},{36... | collective-permute-start | bytes 36872 | tf_op jit(solution)/shard_map/ppermute | solution.py:356
  104.4 2.1 copy-start.3
  110.4 10.4 %all-to-all-start = ((bf16[8,32,384]{2,1,0:T(8,128)(2,1)}), bf16[8,32,384]{2,1,0:T(8,128)(2,1)S(1)}, u32[]{:S(2)}, u32[]{:S(2)}) async-start(bf16[8,32,384]{2,1,0:T(8,128)(2,1)} %rec.1), calls=%async_computation | async-start | bytes 393216 | tf_op jit(solution)/shard_map/all_to_all | solution.py:469
  158.8 23.3 %collective-permute-start.2 = (bf16[192,3072]{1,0:T(8,128)(2,1)}, bf16[192,3072]{1,0:T(8,128)(2,1)}, u32[]{:S(2)}, u32[]{:S(2)}) collective-permute-start(bf16[192,3072]{1,0:T(8,128)(2,1)} %get-tuple-element.43.own_hbm), channel_id=1, source_target_pairs={{0,1},{1,0},{2,3},{3,2},{4,5},{5,4},{6,7},{7,6},{8,9},{9,8},{10,11... | collective-permute-start | bytes 3538952 | tf_op jit(solution)/shard_map/ppermute | solution.py:356
  158.9 23.2 %all-to-all-start.2 = ((bf16[8,128,384]{2,1,0:T(8,128)(2,1)}), bf16[8,128,384]{2,1,0:T(8,128)(2,1)S(1)}, u32[]{:S(2)}, u32[]{:S(2)}) async-start(bf16[8,128,384]{2,1,0:T(8,128)(2,1)} %get-tuple-element.41), calls=%async_computation.2 | async-start | bytes 1572864 | tf_op jit(solution)/shard_map/all_to_all | solution.py:488
  185.2 1.3 collective-permute-start.3
  228.5 26.7 %collective-permute-start.4 = (bf16[192,3072]{1,0:T(8,128)(2,1)S(1)}, bf16[192,3072]{1,0:T(8,128)(2,1)S(1)}, u32[]{:S(2)}, u32[]{:S(2)}) collective-permute-start(bf16[192,3072]{1,0:T(8,128)(2,1)S(1)} %get-tuple-element.49.own_hbm), channel_id=1, source_target_pairs={{0,1},{1,0},{2,3},{3,2},{4,5},{5,4},{6,7},{7,6},{8,9},{9,8},{10,11... | collective-permute-start | bytes 3538952 | tf_op jit(solution)/shard_map/ppermute | solution.py:356
  258.2 1.3 collective-permute-start.5
  299.4 21.1 %collective-permute-start.6 = (bf16[192,3072]{1,0:T(8,128)(2,1)S(1)}, bf16[192,3072]{1,0:T(8,128)(2,1)S(1)}, u32[]{:S(2)}, u32[]{:S(2)}) collective-permute-start(bf16[192,3072]{1,0:T(8,128)(2,1)S(1)} %get-tuple-element.55.own_hbm), channel_id=1, source_target_pairs={{0,1},{1,0},{2,3},{3,2},{4,5},{5,4},{6,7},{7,6},{8,9},{9,8},{10,11... | collective-permute-start | bytes 3538952 | tf_op jit(solution)/shard_map/ppermute | solution.py:356
  323.5 1.3 collective-permute-start.7
  364.9 17.4 %collective-permute-start.8 = (bf16[192,3072]{1,0:T(8,128)(2,1)S(1)}, bf16[192,3072]{1,0:T(8,128)(2,1)S(1)}, u32[]{:S(2)}, u32[]{:S(2)}) collective-permute-start(bf16[192,3072]{1,0:T(8,128)(2,1)S(1)} %get-tuple-element.61.own_hbm), channel_id=1, source_target_pairs={{0,1},{1,0},{2,3},{3,2},{4,5},{5,4},{6,7},{7,6},{8,9},{9,8},{10,11... | collective-permute-start | bytes 3538952 | tf_op jit(solution)/shard_map/ppermute | solution.py:356
  385.3 1.3 collective-permute-start.9
  387.2 32.2 %copy-start.1 = (f32[1000,512]{1,0:T(8,128)S(1)}, f32[1000,512]{1,0:T(8,128)}, u32[]{:S(2)}) copy-start(f32[1000,512]{1,0:T(8,128)} %param.15) | copy-start | bytes 6144004
Sparse Core Ops, SparseCore 0:
  46.8 70.3 all-gather.6
  119.7 75.8 all-gather.8
  198.0 74.5 all-gather.10
  275.0 67.3 all-gather.12
where the time goes:
time: 427 us; the launch traced here: 426 us
  blocking collectives  272 us (64%)
  Pallas kernels  73.6 us (17%)
  waiting for transfers between devices  31.9 us (7%)
  between operations  16.3 us (4%)
  starting transfers between devices  14.9 us (3%)
  local copies, waits for them, and re-layouts  14.2 us (3%)
    all_to_all x4, blocking collectives, local(): parts = lax.all_to_all(projected.reshape(8, 8, D), 'z', 0, 0)  73.8 us
    all_to_all x3, blocking collectives, local(): fresh = lax.all_to_all(fresh, peers, 0, 0)  63.9 us
    all_gather x3, blocking collectives, local(): group = lax.all_gather(current, COL, axis=0, tiled=True)  50.8 us
    pallas_call x4, Pallas kernels, local(): call(qkv_kernel_of(layer), (shape_of((GROUP, 384), BF), shape_of((copies,...  50.6 us
    all_to_all x1, blocking collectives, local(): chunks = lax.all_to_all(packed, 'section', 0, 0)  25 us
    all_gather x1, blocking collectives, local(): lax.all_gather(jnp.concatenate([summed, gain_row], axis=0), ('section',)...  24.3 us
    all_gather x1, blocking collectives, local(): gathered = lax.all_gather(payload, COL, axis=0, tiled=True)  22.8 us
    all_to_all x1, waiting for transfers between devices, local(): fresh = lax.all_to_all(fresh, peers, 0, 0)  18.5 us
  transfers between devices with their start and end apart: 16, of which 7 were waited for; matrix products, arithmetic and copies ran while one was open for 1% of the time, Pallas kernels for 15%

commit v1 on v0

--- a/solution.py
+++ b/solution.py
@@ -15,6 +15,7 @@
 PLEN = 256
 GROUP = 128
 REC_GROUP = 32
+STALE = 384
 BF = jnp.bfloat16
 F32 = jnp.float32
 COL = ("z", "core")
@@ -172,7 +173,7 @@
     )
     for copy in range(kv_out.shape[0]):
         for head in range(3):
-            kv_out[copy, :, 128 * head : 128 * head + 128] = keys_values[head]
+            kv_out[copy, 0:rows, 128 * head : 128 * head + 128] = keys_values[head]
     if q_out is None:
         return
     zero = jnp.zeros((rows, 128), F32)
@@ -194,7 +195,7 @@
 
 
 def qkv_kernel_of(layer):
-    def qkv_kernel(x_ref, mod_ref, gain_ref, cos_ref, sin_ref, text_ref, packed_ref, q_out, kv_out, weights_out, norm_ref, w_vmem, sems):
+    def qkv_kernel(x_ref, mod_ref, gain_ref, cos_ref, sin_ref, text_ref, rec_ref, packed_ref, q_out, kv_out, weights_out, norm_ref, w_vmem, sems):
         def fetch(k):
             to = w_vmem.at[pl.ds(288 * (k % 2), 288), pl.ds(384 * (k // 2), 384)]
             return pltpu.make_async_copy(packed_ref.at[k, pl.ds(0, 288), :], to, sems.at[k])
@@ -215,21 +216,22 @@
             lanes = slice(768 * piece, 768 * piece + 768)
             mixed = mixed + times_weights(norm_ref[:, lanes], w_vmem[:, lanes])
         heads_from(mixed, gain_ref, cos_ref, sin_ref, q_out, kv_out)
+        if layer == 0:
+            for copy in range(kv_out.shape[0]):
+                kv_out[copy, GROUP:, :] = rec_ref[0]
         for k in range(16):
             pass_on(k).wait()
 
     return qkv_kernel
 
 
-def pack_kernel(scalars, w_ref, out_ref, base_ref, packed, sems):
-    row = scalars[8]
+def pack_kernel(row_ref, w_ref, out_ref, packed, sems):
     copies = []
     for k in range(4):
-        lanes = pl.ds(pl.multiple_of(row * 768 + 384 * (k // 2), 128), 384)
+        lanes = pl.ds(pl.multiple_of(row_ref[0] * 768 + 384 * (k // 2), 128), 384)
         copies += [
             (w_ref.at[pl.ds(288 * (k % 2), 288), lanes], packed.at[k, pl.ds(0, 288), :]),
             (out_ref.at[pl.ds(96 * (k % 2), 96), lanes], packed.at[k, pl.ds(288, 96), :]),
-            (base_ref.at[k], packed.at[k, pl.ds(384, 128), :]),
         ]
     copies = [pltpu.make_async_copy(a, b, sems.at[n]) for n, (a, b) in enumerate(copies)]
     for copy in copies:
@@ -275,27 +277,29 @@
 
 def attend_kernel_of(layer):
     def attend_kernel(
-        scalars, q_ref, fresh_ref, rec_ref, target_ref, packed_ref, own_hbm, other_hbm,
+        scalars, q_ref, fresh_ref, target_ref, rec_ref, stale_ref, own_hbm, other_hbm,
         keep_out, send_out, weights_out, base_ref, cache_ref, rec_vmem, sems,
     ):
-        section, req = scalars[7], scalars[15]
+        section = scalars[7]
         rec_copies = [
             pltpu.make_async_copy(
-                rec_ref.at[2 * layer + h], rec_vmem.at[pl.ds(REC_GROUP * h, REC_GROUP), :], sems.at[18 + h]
+                rec_ref.at[2 * layer + h, pl.ds(GROUP, REC_GROUP), :],
+                rec_vmem.at[pl.ds(REC_GROUP * h, REC_GROUP), :],
+                sems.at[4 + h],
             )
             for h in range(2)
         ]
         for copy in rec_copies:
             copy.start()
-        from_base = []
-        for k in range(16):
-            rows = pl.ds(pl.multiple_of(384 + 64 * req, 64), 64)
-            from_base.append(
-                pltpu.make_async_copy(packed_ref.at[k, rows, :], base_ref.at[pl.ds(64 * k, 64), :], sems.at[k])
+        from_base = [
+            pltpu.make_async_copy(
+                stale_ref.at[2 * layer + h], base_ref.at[pl.ds(PLEN + STALE * h, STALE), :], sems.at[h]
             )
+            for h in range(2)
+        ]
         weights = [
-            pltpu.make_async_copy(own_hbm, weights_out.at[0], sems.at[16]),
-            pltpu.make_async_copy(other_hbm, weights_out.at[1], sems.at[17]),
+            pltpu.make_async_copy(own_hbm, weights_out.at[0], sems.at[2]),
+            pltpu.make_async_copy(other_hbm, weights_out.at[1], sems.at[3]),
         ]
         for copy in from_base + weights:
             copy.start()
@@ -313,7 +317,12 @@
 
             @pl.when(patch <= section)
             def _(patch=patch, rows=rows):
-                cache_ref[rows, :] = jnp.concatenate([fresh_ref[2 * patch], fresh_ref[2 * patch + 1]], axis=0)
+                cache_ref[rows, :] = jnp.concatenate(
+                    [fresh_ref[2 * patch, 0:GROUP, :], fresh_ref[2 * patch + 1, 0:GROUP, :]], axis=0
+                )
+
+            if patch == 0:
+                continue
 
             @pl.when(patch > section)
             def _(rows=rows):
@@ -378,6 +387,30 @@
     sections = lax.axis_size("section")
     patches = hidden.shape[0]
 
+    row_index = req * 2 + half
+    weights_qkv = pltpu.with_memory_space_constraint(qkv_weight[0].T, pltpu.HBM)
+    packed = call(
+        pack_kernel,
+        shape_of((4, 384, 384), BF),
+        [SMEM, HBM, HBM],
+        "pack",
+        out_specs=HBM,
+        scratch=[pltpu.SemaphoreType.DMA((8,))],
+    )(
+        row_index[None].astype(jnp.int32),
+        weights_qkv,
+        pltpu.with_memory_space_constraint(out_weight[0], pltpu.HBM),
+    )
+    chunks = lax.all_to_all(packed, "section", 0, 0)
+    layers = [
+        lax.all_gather(chunks[layer], ("req", "half", "section"), axis=0, tiled=False) for layer in range(sections)
+    ]
+    peers = ("section", "half")
+    copies = lax.axis_size(peers)
+    stale_share = lax.dynamic_slice(stale_kv, (0, PLEN + STALE * half, req, 0, 0), (1, STALE, 1, 3, 128))
+    stale_share = stale_share.reshape(1, STALE, 384)
+    stale_all = lax.all_to_all(jnp.broadcast_to(stale_share, (copies, STALE, 384)), peers, 0, 0)
+
     def of_request(value, axis):
         both = [lax.index_in_dim(value, r, axis, keepdims=False) for r in range(2)]
         return jnp.where(first_req, both[0], both[1]), jnp.where(first_req, both[1], both[0])
@@ -403,7 +436,6 @@
     targets = jnp.broadcast_to(targets[None, :], (8, 128))
 
     own_start = lax.dynamic_index_in_dim(starts, section, 0, keepdims=True)
-    row_index = req * 2 + half
     scalars = jnp.concatenate(
         [half[None], starts, timestep % 8, own_start, jnp.stack([section, row_index, core, col]), counts, req[None]]
     ).astype(jnp.int32)
@@ -421,22 +453,6 @@
         jnp.broadcast_to(target_own[:, None], (REC_GROUP, 128)),
     )
 
-    stale_rows = lax.dynamic_slice_in_dim(stale_kv[0], row_index * 256, 256, 0)
-    stale_rows = jnp.transpose(stale_rows.reshape(4, 64, 2, 384), (0, 2, 1, 3)).reshape(4, 128, 384)
-    weights_qkv = qkv_weight[0].T
-    packed = call(
-        pack_kernel,
-        shape_of((4, 512, 384), BF),
-        [SMEM, HBM, HBM, HBM],
-        "pack",
-        out_specs=HBM,
-        scratch=[pltpu.SemaphoreType.DMA((12,))],
-    )(scalars, weights_qkv, out_weight[0], stale_rows)
-    chunks = lax.all_to_all(packed, "section", 0, 0)
-    layers = [
-        lax.all_gather(chunks[layer], ("req", "half", "section"), axis=0, tiled=False) for layer in range(sections)
-    ]
-
     payload = jnp.concatenate(
         [
             tokens,
@@ -450,54 +466,55 @@
     pieces = gathered[:, D + 768 : D + 840].reshape(16, 2, 288).astype(F32)
     summed = pieces[:, 0] + pieces[:, 1]
     gain_row = jnp.pad(qk_gain[0].reshape(1, 128), ((0, 0), (0, 160)))
-    rows = lax.all_gather(jnp.concatenate([summed, gain_row], axis=0), ("section",) + ROW, axis=0, tiled=False)
+    rows = jnp.concatenate([summed, gain_row], axis=0)[None]
+    everyone = ("section",) + ROW
+    rows = lax.all_to_all(jnp.broadcast_to(rows, (lax.axis_size(everyone), 17, 288)), everyone, 0, 0)
     modulation = rows[:, :16].reshape(sections, 6, D)
     all_gains = rows.reshape(sections, 4, 17, 288)[:, 0, 16, :128].reshape(sections, 2, HD)
     all_gains = jnp.concatenate([all_gains, all_gains], axis=2)
     own_gains = jnp.concatenate([qk_gain[0], qk_gain[0]], axis=1)
 
-    peers = ("section", "half")
-    copies = lax.axis_size(peers)
-
     rec_fresh = call(
         rec_kernel,
-        shape_of((copies, REC_GROUP, 384), BF),
+        shape_of((1, REC_GROUP, 384), BF),
         [SMEM] + [VMEM] * 6 + [HBM],
         "rec",
         scratch=[pltpu.VMEM((REC_GROUP, D), BF), pltpu.VMEM((576, D), BF), pltpu.SemaphoreType.DMA],
     )(scalars, rec_rows, modulation, own_gains, cosine[GROUP:], sine[GROUP:], text[GROUP:], weights_qkv)
-    rec_all = lax.all_to_all(rec_fresh, peers, 0, 0)
     cosine, sine, text = cosine[:GROUP], sine[:GROUP], text[:GROUP]
 
     half_rows = shape_of((64, 256), BF)
-    group, rec_all = lax.optimization_barrier((gathered[:, :D], rec_all))
-    current, outs = tokens, []
+    current, group, outs, first_fresh = tokens, gathered[:, :D], [], None
     for layer in range(sections):
         packed = pltpu.with_memory_space_constraint(layers[layer], pltpu.HBM)
         if layer > 0:
             group = lax.all_gather(current, COL, axis=0, tiled=True)
         queries, fresh, out_own = call(
             qkv_kernel_of(layer),
-            (shape_of((GROUP, 384), BF), shape_of((copies, GROUP, 384), BF), shape_of((192, D), BF)),
-            [VMEM] * 6 + [HBM],
+            (
+                shape_of((GROUP, 384), BF),
+                shape_of((copies, GROUP + (REC_GROUP if layer == 0 else 0), 384), BF),
+                shape_of((192, D), BF),
+            ),
+            [VMEM] * 7 + [HBM],
             "qkv",
-            out_specs=(VMEM, VMEM, HBM),
             scratch=[pltpu.VMEM((GROUP, D), BF), pltpu.VMEM((576, D), BF), pltpu.SemaphoreType.DMA((32,))],
-        )(group, modulation, all_gains[layer], cosine, sine, text, packed)
+        )(group, modulation, all_gains[layer], cosine, sine, text, rec_fresh, packed)
         out_other = swapped(out_own, "core")
         fresh = lax.all_to_all(fresh, peers, 0, 0)
+        first_fresh = fresh if layer == 0 else first_fresh
         keep, send, weights_out = call(
             attend_kernel_of(layer),
             (half_rows, half_rows, shape_of((2, 192, D), BF)),
-            [SMEM] + [VMEM] * 2 + [HBM, VMEM, HBM, HBM, HBM],
+            [SMEM] + [VMEM] * 3 + [HBM] * 4,
             "attend",
             scratch=[
                 pltpu.VMEM((1024, 384), BF),
                 pltpu.VMEM((1024, 384), BF),
                 pltpu.VMEM((128, 384), BF),
-                pltpu.SemaphoreType.DMA((20,)),
+                pltpu.SemaphoreType.DMA((6,)),
             ],
-        )(scalars, queries, fresh, rec_all, targets, packed, out_own, out_other)
+        )(scalars, queries, fresh, targets, first_fresh, stale_all, out_own, out_other)
         projected = call(project_kernel, shape_of((64, D), BF), [VMEM] * 3, "project")(
             keep, swapped(send, "core"), weights_out
         )

time: 427 us -> 418 us (0.979)
  Pallas kernels: 73.6 us -> 41.6 us
  local copies, waits for them, and re-layouts: 14.2 us -> 45.7 us
  blocking collectives: 272 us -> 244 us
  waiting for transfers between devices: 31.9 us -> 43.8 us
  starting transfers between devices: 14.9 us -> 21.3 us
    pallas_call x4, Pallas kernels: 50.6 us -> 18 us  [local(): call(qkv_kernel_of(layer), (shape_of((GROUP, 384), BF), shape_of((copies,...]
    all_gather x1 -> x0, blocking collectives: 24.3 us -> none  [local(): lax.all_gather(jnp.concatenate([summed, gain_row], axis=0), ('section',)...]
    unnamed x21 -> x108, local copies, waits for them, and re-layouts: 5.37 us -> 22.9 us
    all_to_all x1 -> x2, waiting for transfers between devices: 5.48 us -> 16.1 us  [the longest x1 14.9 us: local(): lax.all_to_all(jnp.broadcast_to(rows, (lax.axis_size(everyone), 17, 288))...]
    all_to_all x1 -> x2, starting transfers between devices: 4.63 us -> 10.4 us  [the longest x1 5.38 us: local(): lax.all_to_all(jnp.broadcast_to(rows, (lax.axis_size(everyone), 17, 288))...]
  transfers between devices with their start and end apart: 16 -> 17, of which waited for: 7 -> 7; matrix products, arithmetic and copies ran while one was open for 1% -> 6% of each run, Pallas kernels for 15% -> 8%
where the time goes in v1:
time: 418 us; the launch traced here: 416 us
  blocking collectives  244 us (58%)
  local copies, waits for them, and re-layouts  45.7 us (11%)
  waiting for transfers between devices  43.8 us (10%)
  Pallas kernels  41.6 us (10%)
  starting transfers between devices  21.3 us (5%)
  between operations  16.3 us (4%)
    all_to_all x4, blocking collectives, local(): parts = lax.all_to_all(projected.reshape(8, 8, D), 'z', 0, 0)  77.2 us
    all_to_all x3, blocking collectives, local(): fresh = lax.all_to_all(fresh, peers, 0, 0)  62.1 us
    all_gather x3, blocking collectives, local(): group = lax.all_gather(current, COL, axis=0, tiled=True)  50.7 us
    unnamed x108, local copies, waits for them, and re-layouts  22.9 us
    all_gather x1, blocking collectives, local(): gathered = lax.all_gather(payload, COL, axis=0, tiled=True)  22.8 us
    all_to_all x1, waiting for transfers between devices, local(): fresh = lax.all_to_all(fresh, peers, 0, 0)  21 us
    all_to_all x1, blocking collectives, local(): chunks = lax.all_to_all(packed, 'section', 0, 0)  20.8 us
    pallas_call x4, Pallas kernels, local(): call(qkv_kernel_of(layer), (shape_of((GROUP, 384), BF), shape_of((copies,...  18 us
  transfers between devices with their start and end apart: 17, of which 7 were waited for; matrix products, arithmetic and copies ran while one was open for 6% of the time, Pallas kernels for 8%

profile of v1, /device:TPU:2, one launch (start us, length us, event | category | flops | bytes accessed | tf_op | source)
XLA Modules:
  0.0 415.6 jit_solution(7347962844774092801)
XLA Ops:
  6.5 1.6 pack.1
  8.1 20.8 %all_to_all.60 = bf16[4,384,384]{2,1,0:T(8,128)(2,1)S(1)} all-to-all(bf16[4,384,384]{2,1,0:T(8,128)(2,1)S(1)} %pack.1), channel_id=1, replica_groups=mesh['section'=4,'req'=2,'half'=2,'z'=8,'core'=2] {'section'}, dimensions={0} | all-to-all | bytes 2359296 | tf_op jit(solution)/shard_map/all_to_all | solution.py:404
  28.9 1.1 fusion.10
  32.4 2.2 collective-permute-start
  34.6 1.4 collective-permute-start.1
  41.3 1.4 concatenate.31.scalars
  42.7 1.0 prepare.1
  44.8 22.8 %all_gather.24 = bf16[128,3968]{1,0:T(8,128)(2,1)S(1)} all-gather(bf16[8,3968]{1,0:T(8,128)(2,1)S(1)} %fusion.1), channel_id=1, replica_groups=mesh['section'=4,'req'=2,'half'=2,'z'=8,'core'=2] {'z','core'}, dimensions={0}, use_global_device_ids=true | all-gather | bytes 1079296 | tf_op jit(solution)/shard_map/all_gather | solution.py:464
  67.8 1.0 broadcast_in_dim.41
  68.8 5.4 %all-to-all-start = ((f32[16,17,288]{2,1,0:T(8,128)}), f32[16,17,288]{2,1,0:T(8,128)S(1)}, u32[]{:S(2)}, u32[]{:S(2)}) async-start(f32[16,17,288]{2,1,0:T(8,128)} %broadcast_in_dim.41), calls=%async_computation | async-start | bytes 1179648 | tf_op jit(solution)/shard_map/all_to_all | solution.py:471
  74.8 1.7 constant_dynamic-slice_fusion
  77.6 14.9 %all-to-all-done = f32[16,17,288]{2,1,0:T(8,128)S(1)} async-done(((f32[16,17,288]{2,1,0:T(8,128)}), f32[16,17,288]{2,1,0:T(8,128)S(1)}, u32[]{:S(2)}, u32[]{:S(2)}) %all-to-all-start) | async-done | bytes 313376 | tf_op jit(solution)/shard_map/all_to_all | solution.py:471
  92.4 1.6 broadcast_in_dim.45
  94.1 5.0 %all-to-all-start.3 = ((bf16[8,384,384]{2,1,0:T(8,128)(2,1)}), bf16[8,384,384]{2,1,0:T(8,128)(2,1)S(1)}, u32[]{:S(2)}, u32[]{:S(2)}) async-start(bf16[8,384,384]{2,1,0:T(8,128)(2,1)} %broadcast_in_dim.45), calls=%async_computation.3 | async-start | bytes 4718592 | tf_op jit(solution)/shard_map/all_to_all | solution.py:412
  102.8 0.9 slice.182
  103.7 1.2 slice.174.x_ref
  105.7 1.8 slice.178
  107.5 1.3 reshape.76.mod_ref
  108.8 1.3 slice.179
  110.1 1.3 reshape_squeeze.7
  115.1 4.4 %rec.1.rec_ref = bf16[1,32,384]{2,1,0:T(8,128)(2,1)S(1)} custom-call(s32[16]{0:T(128)S(1)} %copy-done.37, bf16[32,3072]{1,0:T(8,128)(2,1)S(1)} %copy-done.15, f32[4,6,3072]{2,1,0:T(8,128)S(1)} %reshape.76.mod_ref, f32[2,128]{1,0:T(2,128)S(1)} %copy-done.39, f32[32,128]{1,0:T(8,128)S(1)} %slice.154.cos_ref, f32[32,128]{1,0:T(8,128)S(1)} %copy-done.34, ...), custom_call_target="tpu_custom_call" | custom-call | tf_op jit(solution)/shard_map/rec/pallas_call | solution.py:477
  124.0 5.2 %qkv.4 = (bf16[128,384]{1,0:T(8,128)(2,1)S(1)}, bf16[8,160,384]{2,1,0:T(8,128)(2,1)S(1)}, bf16[192,3072]{1,0:T(8,128)(2,1)}) custom-call(bf16[128,3072]{1,0:T(8,128)(2,1)S(1)} %slice.174.x_ref, f32[4,6,3072]{2,1,0:T(8,128)S(1)} %reshape.76.mod_ref, f32[2,128]{1,0:T(2,128)S(1)} %get-tuple-element.76.gain_ref, f32[128,128]{1,0:T(8,128)S(1)} %copy-done.2, ...), custom_call_target="tpu_custom_call" | custom-call | tf_op jit(solution)/shard_map/qkv/pallas_call | solution.py:492
  129.9 1.0 copy-done.14
  130.9 1.2 all-to-all-done.3.stale_ref
  132.1 5.4 %all-to-all-start.2 = ((bf16[8,160,384]{2,1,0:T(8,128)(2,1)}), bf16[8,160,384]{2,1,0:T(8,128)(2,1)}, u32[]{:S(2)}, u32[]{:S(2)}) async-start(bf16[8,160,384]{2,1,0:T(8,128)(2,1)} %copy-done.14), calls=%async_computation.2 | async-start | bytes 1966080 | tf_op jit(solution)/shard_map/all_to_all | solution.py:504
  137.5 21.0 %all-to-all-done.2.fresh_ref.rec_ref = bf16[8,160,384]{2,1,0:T(8,128)(2,1)} async-done(((bf16[8,160,384]{2,1,0:T(8,128)(2,1)}), bf16[8,160,384]{2,1,0:T(8,128)(2,1)}, u32[]{:S(2)}, u32[]{:S(2)}) %all-to-all-start.2) | async-done | bytes 983072 | tf_op jit(solution)/shard_map/all_to_all | solution.py:504
  158.6 3.5 attend.4
  162.3 1.2 collective-permute-done.3.got_ref
  164.1 17.7 %all_to_all.61.parts_ref = bf16[8,8,3072]{2,1,0:T(8,128)(2,1)S(1)} all-to-all(bf16[8,8,3072]{2,1,0:T(8,128)(2,1)S(1)} %bitcast.81), channel_id=1, replica_groups=mesh['section'=4,'req'=2,'half'=2,'z'=8,'core'=2] {'z'}, dimensions={0} | all-to-all | bytes 786432 | tf_op jit(solution)/shard_map/all_to_all | solution.py:521
  182.4 16.8 %all_gather.26.x_ref = bf16[128,3072]{1,0:T(8,128)(2,1)S(1)} all-gather(bf16[8,3072]{1,0:T(8,128)(2,1)S(1)} %residual.4.x_ref), channel_id=1, replica_groups=mesh['section'=4,'req'=2,'half'=2,'z'=8,'core'=2] {'z','core'}, dimensions={0}, use_global_device_ids=true | all-gather | bytes 835584 | tf_op jit(solution)/shard_map/all_gather | solution.py:491
  203.8 4.4 %qkv.5 = (bf16[128,384]{1,0:T(8,128)(2,1)S(1)}, bf16[8,128,384]{2,1,0:T(8,128)(2,1)S(1)}, bf16[192,3072]{1,0:T(8,128)(2,1)S(1)}) custom-call(bf16[128,3072]{1,0:T(8,128)(2,1)S(1)} %all_gather.26.x_ref, f32[4,6,3072]{2,1,0:T(8,128)S(1)} %reshape.76.mod_ref, f32[2,128]{1,0:T(2,128)S(1)} %copy-done.40, f32[128,128]{1,0:T(8,128)S(1)} %copy-done.3, ...), custom_call_target="tpu_custom_call" | custom-call | tf_op jit(solution)/shard_map/qkv/pallas_call | solution.py:492
  208.6 25.9 %all_to_all.62.fresh_ref = bf16[8,128,384]{2,1,0:T(8,128)(2,1)S(1)} all-to-all(bf16[8,128,384]{2,1,0:T(8,128)(2,1)S(1)} %get-tuple-element.44), channel_id=1, replica_groups=mesh['section'=4,'req'=2,'half'=2,'z'=8,'core'=2] {'section','half'}, dimensions={0} | all-to-all | bytes 1572864 | tf_op jit(solution)/shard_map/all_to_all | solution.py:504
  234.5 2.8 attend.5
  237.4 1.2 collective-permute-done.5.got_ref
  239.2 19.3 %all_to_all.63.parts_ref = bf16[8,8,3072]{2,1,0:T(8,128)(2,1)S(1)} all-to-all(bf16[8,8,3072]{2,1,0:T(8,128)(2,1)S(1)} %bitcast.82), channel_id=1, replica_groups=mesh['section'=4,'req'=2,'half'=2,'z'=8,'core'=2] {'z'}, dimensions={0} | all-to-all | bytes 786432 | tf_op jit(solution)/shard_map/all_to_all | solution.py:521
  259.1 16.8 %all_gather.28.x_ref = bf16[128,3072]{1,0:T(8,128)(2,1)S(1)} all-gather(bf16[8,3072]{1,0:T(8,128)(2,1)S(1)} %residual.5.x_ref), channel_id=1, replica_groups=mesh['section'=4,'req'=2,'half'=2,'z'=8,'core'=2] {'z','core'}, dimensions={0}, use_global_device_ids=true | all-gather | bytes 835584 | tf_op jit(solution)/shard_map/all_gather | solution.py:491
  279.9 4.2 %qkv.6 = (bf16[128,384]{1,0:T(8,128)(2,1)S(1)}, bf16[8,128,384]{2,1,0:T(8,128)(2,1)S(1)}, bf16[192,3072]{1,0:T(8,128)(2,1)S(1)}) custom-call(bf16[128,3072]{1,0:T(8,128)(2,1)S(1)} %all_gather.28.x_ref, f32[4,6,3072]{2,1,0:T(8,128)S(1)} %reshape.76.mod_ref, f32[2,128]{1,0:T(2,128)S(1)} %get-tuple-element.75.gain_ref, f32[128,128]{1,0:T(8,128)S(1)} %copy-done.4, ...), custom_call_target="tpu_custom_call" | custom-call | tf_op jit(solution)/shard_map/qkv/pallas_call | solution.py:492
  284.6 19.9 %all_to_all.64.fresh_ref = bf16[8,128,384]{2,1,0:T(8,128)(2,1)S(1)} all-to-all(bf16[8,128,384]{2,1,0:T(8,128)(2,1)S(1)} %get-tuple-element.50), channel_id=1, replica_groups=mesh['section'=4,'req'=2,'half'=2,'z'=8,'core'=2] {'section','half'}, dimensions={0} | all-to-all | bytes 1572864 | tf_op jit(solution)/shard_map/all_to_all | solution.py:504
  304.5 2.8 attend.6
  307.4 1.2 collective-permute-done.7.got_ref
  309.2 21.4 %all_to_all.65.parts_ref = bf16[8,8,3072]{2,1,0:T(8,128)(2,1)S(1)} all-to-all(bf16[8,8,3072]{2,1,0:T(8,128)(2,1)S(1)} %bitcast.83), channel_id=1, replica_groups=mesh['section'=4,'req'=2,'half'=2,'z'=8,'core'=2] {'z'}, dimensions={0} | all-to-all | bytes 786432 | tf_op jit(solution)/shard_map/all_to_all | solution.py:521
  331.2 17.1 %all_gather.30.x_ref = bf16[128,3072]{1,0:T(8,128)(2,1)S(1)} all-gather(bf16[8,3072]{1,0:T(8,128)(2,1)S(1)} %residual.6.x_ref), channel_id=1, replica_groups=mesh['section'=4,'req'=2,'half'=2,'z'=8,'core'=2] {'z','core'}, dimensions={0}, use_global_device_ids=true | all-gather | bytes 835584 | tf_op jit(solution)/shard_map/all_gather | solution.py:491
  352.1 4.2 %qkv.7 = (bf16[128,384]{1,0:T(8,128)(2,1)S(1)}, bf16[8,128,384]{2,1,0:T(8,128)(2,1)S(1)}, bf16[192,3072]{1,0:T(8,128)(2,1)S(1)}) custom-call(bf16[128,3072]{1,0:T(8,128)(2,1)S(1)} %all_gather.30.x_ref, f32[4,6,3072]{2,1,0:T(8,128)S(1)} %reshape.76.mod_ref, f32[2,128]{1,0:T(2,128)S(1)} %get-tuple-element.73.gain_ref, f32[128,128]{1,0:T(8,128)S(1)} %copy-done.5, ...), custom_call_target="tpu_custom_call" | custom-call | tf_op jit(solution)/shard_map/qkv/pallas_call | solution.py:492
  356.8 16.3 %all_to_all.66.fresh_ref = bf16[8,128,384]{2,1,0:T(8,128)(2,1)S(1)} all-to-all(bf16[8,128,384]{2,1,0:T(8,128)(2,1)S(1)} %get-tuple-element.56), channel_id=1, replica_groups=mesh['section'=4,'req'=2,'half'=2,'z'=8,'core'=2] {'section','half'}, dimensions={0} | all-to-all | bytes 1572864 | tf_op jit(solution)/shard_map/all_to_all | solution.py:504
  373.1 2.8 attend.7
  376.1 1.2 collective-permute-done.9.got_ref
  377.8 18.7 %all_to_all.67.parts_ref = bf16[8,8,3072]{2,1,0:T(8,128)(2,1)S(1)} all-to-all(bf16[8,8,3072]{2,1,0:T(8,128)(2,1)S(1)} %bitcast.84), channel_id=1, replica_groups=mesh['section'=4,'req'=2,'half'=2,'z'=8,'core'=2] {'z'}, dimensions={0} | all-to-all | bytes 786432 | tf_op jit(solution)/shard_map/all_to_all | solution.py:521
  397.3 10.9 %all_to_all.68 = bf16[8,4,3072]{2,1,0:T(4,128)(2,1)S(1)} all-to-all(bf16[8,4,3072]{2,1,0:T(4,128)(2,1)S(1)} %reshape.83), channel_id=1, replica_groups=mesh['section'=4,'req'=2,'half'=2,'z'=8,'core'=2] {'section','req'}, dimensions={0} | all-to-all | bytes 393216 | tf_op jit(solution)/shard_map/all_to_all | solution.py:528
  (188 shorter events, 41.0 us)
Async XLA Ops:
  6.5 33.3 %copy-start = (f32[1000,512]{1,0:T(8,128)S(1)}, f32[1000,512]{1,0:T(8,128)}, u32[]{:S(2)}) copy-start(f32[1000,512]{1,0:T(8,128)} %param.15) | copy-start | bytes 6144004
  6.5 114.2 %all-gather.5.cloned.1.call-start = ((), (), s32[]{:S(2)}) async-start(), calls=%async_computation.12 | async-start | bytes 5013504 | tf_op jit(solution)/shard_map/all_gather | solution.py:406
  28.9 5.8 %copy-start.44 = (bf16[1,1,2,3072]{3,2,1,0:T(2,128)(2,1)S(1)}, bf16[1,1,2,3072]{3,2,1,0:T(2,128)(2,1)}, u32[]{:S(2)}) copy-start(bf16[1,1,2,3072]{3,2,1,0:T(2,128)(2,1)} %param.21) | copy-start | bytes 36868
  28.9 7.9 %copy-start.51 = (s32[2,64]{1,0:T(2,128)S(1)}, s32[2,64]{1,0:T(2,128)}, u32[]{:S(2)}) copy-start(s32[2,64]{1,0:T(2,128)} %param.22) | copy-start | bytes 1540
  28.9 8.4 %copy-start.50 = (s32[2,4]{1,0:T(2,128)S(1)}, s32[2,4]{1,0:T(2,128)}, u32[]{:S(2)}) copy-start(s32[2,4]{1,0:T(2,128)} %param.13) | copy-start | bytes 100
  28.9 13.9 %copy-start.31 = (bf16[1,512,288]{1,2,0:T(8,128)(2,1)S(1)}, bf16[1,512,288]{1,2,0:T(8,128)(2,1)}, u32[]{:S(2)}) copy-start(bf16[1,512,288]{1,2,0:T(8,128)(2,1)} %param.16) | copy-start | bytes 884740
  28.9 13.9 %copy-start.41 = (f32[1,128]{1,0:T(1,128)S(1)}, f32[1,128]{1,0:T(1,128)}, u32[]{:S(2)}) copy-start(f32[1,128]{1,0:T(1,128)} %constant.86.clone.rate_ref) | copy-start | bytes 1540
  28.9 15.0 %copy-start.52 = (f32[1,2,64]{2,1,0:T(2,128)S(1)}, f32[1,2,64]{2,1,0:T(2,128)}, u32[]{:S(2)}) copy-start(f32[1,2,64]{2,1,0:T(2,128)} %param.19) | copy-start | bytes 1540
  30.1 169.8 %all-gather.7.cloned.1.call-start = ((), (), s32[]{:S(2)}) async-start(), calls=%async_computation.13 | async-start | bytes 5013504 | tf_op jit(solution)/shard_map/all_gather | solution.py:406
  30.8 245.8 %all-gather.9.cloned.1.call-start = ((), (), s32[]{:S(2)}) async-start(), calls=%async_computation.14 | async-start | bytes 5013504 | tf_op jit(solution)/shard_map/all_gather | solution.py:406
  32.4 11.6 %collective-permute-start = (bf16[4,2,3072]{2,0,1:T(4,128)(2,1)S(1)}, bf16[4,2,3072]{2,0,1:T(4,128)(2,1)S(1)}, u32[]{:S(2)}, u32[]{:S(2)}) collective-permute-start(bf16[4,2,3072]{2,0,1:T(4,128)(2,1)S(1)} %bitcast.96), channel_id=1, source_target_pairs={{0,32},{32,0},{1,33},{33,1},{2,34},{34,2},{3,35},{35,3},{4,36},{36... | collective-permute-start | bytes 147464 | tf_op jit(solution)/shard_map/ppermute | solution.py:365
  34.6 9.3 %collective-permute-start.1 = (bf16[1,2,3072]{2,1,0:T(2,128)(2,1)S(1)}, bf16[1,2,3072]{2,1,0:T(2,128)(2,1)S(1)}, u32[]{:S(2)}, u32[]{:S(2)}) collective-permute-start(bf16[1,2,3072]{2,1,0:T(2,128)(2,1)S(1)} %bitcast.99), channel_id=1, source_target_pairs={{0,32},{32,0},{1,33},{33,1},{2,34},{34,2},{3,35},{35,3},{4,36},{36... | collective-permute-start | bytes 36872 | tf_op jit(solution)/shard_map/ppermute | solution.py:365
  37.0 5.7 %copy-start.46 = (s32[32]{0:T(128)}, s32[32]{0:T(128)S(1)}, u32[]{:S(2)}) copy-start(s32[32]{0:T(128)S(1)} %reshape.73) | copy-start | bytes 388
  37.2 5.5 %copy-start.48 = (s32[32]{0:T(128)}, s32[32]{0:T(128)S(1)}, u32[]{:S(2)}) copy-start(s32[32]{0:T(128)S(1)} %reshape.74) | copy-start | bytes 388
  42.6 26.2 %copy-start.36 = (s32[16]{0:T(128)}, s32[16]{0:T(128)S(1)}, u32[]{:S(2)}) copy-start(s32[16]{0:T(128)S(1)} %concatenate.31.scalars) | copy-start | bytes 196
  67.6 26.5 %copy-start.42 = (bf16[128,3968]{1,0:T(8,128)(2,1)}, bf16[128,3968]{1,0:T(8,128)(2,1)S(1)}, u32[]{:S(2)}) copy-start(bf16[128,3968]{1,0:T(8,128)(2,1)S(1)} %all_gather.24) | copy-start | bytes 3047428
  68.8 23.6 %all-to-all-start = ((f32[16,17,288]{2,1,0:T(8,128)}), f32[16,17,288]{2,1,0:T(8,128)S(1)}, u32[]{:S(2)}, u32[]{:S(2)}) async-start(f32[16,17,288]{2,1,0:T(8,128)} %broadcast_in_dim.41), calls=%async_computation | async-start | bytes 1179648 | tf_op jit(solution)/shard_map/all_to_all | solution.py:471
  74.2 274.7 %all-gather.11.cloned.1.call-start = ((), (), s32[]{:S(2)}) async-start(), calls=%async_computation.15 | async-start | bytes 5013504 | tf_op jit(solution)/shard_map/all_gather | solution.py:406
  92.4 1.6 copy-start.43
  94.1 38.0 %all-to-all-start.3 = ((bf16[8,384,384]{2,1,0:T(8,128)(2,1)}), bf16[8,384,384]{2,1,0:T(8,128)(2,1)S(1)}, u32[]{:S(2)}, u32[]{:S(2)}) async-start(bf16[8,384,384]{2,1,0:T(8,128)(2,1)} %broadcast_in_dim.45), calls=%async_computation.3 | async-start | bytes 4718592 | tf_op jit(solution)/shard_map/all_to_all | solution.py:412
  111.4 0.9 copy-start.15
  115.1 5.0 %copy-start.45 = (f32[4,2,64]{2,1,0:T(2,128)S(1)}, f32[4,2,64]{2,1,0:T(2,128)}, u32[]{:S(2)}) copy-start(f32[4,2,64]{2,1,0:T(2,128)} %reshape_squeeze.7) | copy-start | bytes 6148
  120.7 0.8 copy-start.2
  122.4 0.8 copy-start.10
  129.9 1.0 copy-start.14
  129.9 7.6 %copy-start.47 = (s32[32]{0:T(128)S(1)}, s32[32]{0:T(128)}, u32[]{:S(2)}) copy-start(s32[32]{0:T(128)} %copy-done.46) | copy-start | bytes 388
  129.9 7.6 %copy-start.49 = (s32[32]{0:T(128)S(1)}, s32[32]{0:T(128)}, u32[]{:S(2)}) copy-start(s32[32]{0:T(128)} %copy-done.48) | copy-start | bytes 388
  129.9 28.7 %copy-start.38 = (s32[16]{0:T(128)S(1)}, s32[16]{0:T(128)}, u32[]{:S(2)}) copy-start(s32[16]{0:T(128)} %copy-done.36) | copy-start | bytes 196
  130.8 27.7 %copy-start.33 = (bf16[128,384]{1,0:T(8,128)(2,1)S(1)}, bf16[128,384]{1,0:T(8,128)(2,1)}, u32[]{:S(2)}) copy-start(bf16[128,384]{1,0:T(8,128)(2,1)} %copy-done.32) | copy-start | bytes 294916
  130.8 27.7 %collective-permute-start.2 = (bf16[192,3072]{1,0:T(8,128)(2,1)}, bf16[192,3072]{1,0:T(8,128)(2,1)}, u32[]{:S(2)}, u32[]{:S(2)}) collective-permute-start(bf16[192,3072]{1,0:T(8,128)(2,1)} %get-tuple-element.39.own_hbm), channel_id=1, source_target_pairs={{0,1},{1,0},{2,3},{3,2},{4,5},{5,4},{6,7},{7,6},{8,9},{9,8},{10,11... | collective-permute-start | bytes 3538952 | tf_op jit(solution)/shard_map/ppermute | solution.py:365
  132.1 26.5 %all-to-all-start.2 = ((bf16[8,160,384]{2,1,0:T(8,128)(2,1)}), bf16[8,160,384]{2,1,0:T(8,128)(2,1)}, u32[]{:S(2)}, u32[]{:S(2)}) async-start(bf16[8,160,384]{2,1,0:T(8,128)(2,1)} %copy-done.14), calls=%async_computation.2 | async-start | bytes 1966080 | tf_op jit(solution)/shard_map/all_to_all | solution.py:504
  162.1 1.5 collective-permute-start.3
  163.5 18.2 %copy-start.30 = (bf16[8,3072]{1,0:T(8,128)(2,1)S(1)}, bf16[8,3072]{1,0:T(8,128)(2,1)}, u32[]{:S(2)}) copy-start(bf16[8,3072]{1,0:T(8,128)(2,1)} %copy-done.29) | copy-start | bytes 147460
  199.9 0.8 copy-start.3
  208.2 26.3 %collective-permute-start.4 = (bf16[192,3072]{1,0:T(8,128)(2,1)S(1)}, bf16[192,3072]{1,0:T(8,128)(2,1)S(1)}, u32[]{:S(2)}, u32[]{:S(2)}) collective-permute-start(bf16[192,3072]{1,0:T(8,128)(2,1)S(1)} %get-tuple-element.45.own_hbm), channel_id=1, source_target_pairs={{0,1},{1,0},{2,3},{3,2},{4,5},{5,4},{6,7},{7,6},{8,9},{9,8},{10,11... | collective-permute-start | bytes 3538952 | tf_op jit(solution)/shard_map/ppermute | solution.py:365
  237.3 1.3 collective-permute-start.5
  238.6 19.9 %copy-start.17 = (bf16[8,3072]{1,0:T(8,128)(2,1)S(1)}, bf16[8,3072]{1,0:T(8,128)(2,1)}, u32[]{:S(2)}) copy-start(bf16[8,3072]{1,0:T(8,128)(2,1)} %copy-done.16) | copy-start | bytes 147460
  276.6 0.8 copy-start.4
  284.0 20.4 %collective-permute-start.6 = (bf16[192,3072]{1,0:T(8,128)(2,1)S(1)}, bf16[192,3072]{1,0:T(8,128)(2,1)S(1)}, u32[]{:S(2)}, u32[]{:S(2)}) collective-permute-start(bf16[192,3072]{1,0:T(8,128)(2,1)S(1)} %get-tuple-element.51.own_hbm), channel_id=1, source_target_pairs={{0,1},{1,0},{2,3},{3,2},{4,5},{5,4},{6,7},{7,6},{8,9},{9,8},{10,11... | collective-permute-start | bytes 3538952 | tf_op jit(solution)/shard_map/ppermute | solution.py:365
  307.3 1.3 collective-permute-start.7
  308.6 22.0 %copy-start.20 = (bf16[8,3072]{1,0:T(8,128)(2,1)S(1)}, bf16[8,3072]{1,0:T(8,128)(2,1)}, u32[]{:S(2)}) copy-start(bf16[8,3072]{1,0:T(8,128)(2,1)} %copy-done.19) | copy-start | bytes 147460
  348.9 0.8 copy-start.5
  356.3 16.8 %collective-permute-start.8 = (bf16[192,3072]{1,0:T(8,128)(2,1)S(1)}, bf16[192,3072]{1,0:T(8,128)(2,1)S(1)}, u32[]{:S(2)}, u32[]{:S(2)}) collective-permute-start(bf16[192,3072]{1,0:T(8,128)(2,1)S(1)} %get-tuple-element.57.own_hbm), channel_id=1, source_target_pairs={{0,1},{1,0},{2,3},{3,2},{4,5},{5,4},{6,7},{7,6},{8,9},{9,8},{10,11... | collective-permute-start | bytes 3538952 | tf_op jit(solution)/shard_map/ppermute | solution.py:365
  376.0 1.3 collective-permute-start.9
  377.3 19.3 %copy-start.23 = (bf16[8,3072]{1,0:T(8,128)(2,1)S(1)}, bf16[8,3072]{1,0:T(8,128)(2,1)}, u32[]{:S(2)}) copy-start(bf16[8,3072]{1,0:T(8,128)(2,1)} %copy-done.22) | copy-start | bytes 147460
  377.3 19.9 %copy-start.18 = (bf16[8,3072]{1,0:T(8,128)(2,1)S(1)}, bf16[8,3072]{1,0:T(8,128)(2,1)}, u32[]{:S(2)}) copy-start(bf16[8,3072]{1,0:T(8,128)(2,1)} %copy-done.16) | copy-start | bytes 147460
  377.3 19.9 %copy-start.21 = (bf16[8,3072]{1,0:T(8,128)(2,1)S(1)}, bf16[8,3072]{1,0:T(8,128)(2,1)}, u32[]{:S(2)}) copy-start(bf16[8,3072]{1,0:T(8,128)(2,1)} %copy-done.19) | copy-start | bytes 147460
  377.8 31.2 %copy-start.1 = (f32[1000,512]{1,0:T(8,128)S(1)}, f32[1000,512]{1,0:T(8,128)}, u32[]{:S(2)}) copy-start(f32[1000,512]{1,0:T(8,128)} %param.15) | copy-start | bytes 6144004
  (22 other events, 15.9 us)
Sparse Core Ops, SparseCore 0:
  30.2 66.1 all-gather.4
  98.9 71.3 all-gather.6
  172.8 62.3 all-gather.8
  237.5 65.9 all-gather.10

commit v2 on v1

--- a/solution.py
+++ b/solution.py
@@ -66,7 +66,7 @@
     return (2 * ((index >> 2) & 1) + half) * 64 + 4 * (index >> 3) + (index & 3)
 
 
-def prepare_kernel(scalars, row_ref, ada_ref, rate_ref, rec_ref, mod_out, cos_out, sin_out, text_out):
+def prepare_kernel(scalars, row_ref, ada_ref, rate_ref, rec_ref, mod_out, tables_out):
     half = scalars[0]
     time_row = row_ref[pl.ds(scalars[5], 1), :]
     embedding = (time_row / (1.0 + jnp.exp(-time_row))).astype(BF)
@@ -90,9 +90,9 @@
         lane = iota((rows, 128), 1) & (HD - 1)
         coordinate = jnp.where(lane < HD // 4, frame, jnp.where(lane < HD // 4 + HD * 3 // 8, height, width))
         phase = coordinate * rate
-        cos_out[at : at + rows, :] = jnp.where(text, 1.0, jnp.cos(phase))
-        sin_out[at : at + rows, :] = jnp.where(text, 0.0, jnp.sin(phase))
-        text_out[at : at + rows, :] = jnp.where(text, 1.0, 0.0)
+        tables_out[0, at : at + rows, :] = jnp.where(text, 1.0, jnp.cos(phase))
+        tables_out[1, at : at + rows, :] = jnp.where(text, 0.0, jnp.sin(phase))
+        tables_out[2, at : at + rows, :] = jnp.where(text, 1.0, 0.0)
 
     tables(offset_in_patch(iota((GROUP, 128), 0), half) + scalars[6], GROUP, 0)
     slot = rec_ref[...]
@@ -104,10 +104,9 @@
     tables(start + (slot & (PLEN - 1)), REC_GROUP, GROUP)
 
 
-def normalize(x_ref, mod_ref, layer, text_ref, norm_ref):
+def normalize(x_ref, mod_ref, tables_ref, norm_ref, small):
     chunks = D // 128
     rows = x_ref.shape[0]
-    text = text_ref[...] > 0.5
 
     def over_chunks(step, start):
         return lax.fori_loop(0, chunks, lambda k, carry: step(pl.ds(pl.multiple_of(k * 128, 128), 128), carry), start, unroll=6)
@@ -123,10 +122,13 @@
 
     total = jnp.sum(over_chunks(add_square, jnp.zeros((rows, 128), F32)), axis=1, keepdims=True)
     factor = lax.rsqrt(total * (1.0 / D) + 1e-5)
+    for copy in small:
+        copy.wait()
+    text = tables_ref[2] > 0.5
 
     def write(lanes, carry):
-        shift = jnp.where(text, mod_ref[layer, 3:4, lanes], mod_ref[layer, 0:1, lanes])
-        scale = jnp.where(text, mod_ref[layer, 4:5, lanes], mod_ref[layer, 1:2, lanes])
+        shift = jnp.where(text, mod_ref[3:4, lanes], mod_ref[0:1, lanes])
+        scale = jnp.where(text, mod_ref[4:5, lanes], mod_ref[1:2, lanes])
         centered = x_ref[:, lanes].astype(F32) - mean
         norm_ref[:, lanes] = (centered * factor * (1.0 + scale) + shift).astype(BF)
         return carry
@@ -134,7 +136,7 @@
     over_chunks(write, 0)
 
 
-def heads_from(mixed, gain_ref, cos_ref, sin_ref, q_out, kv_out):
+def heads_from(mixed, gain_ref, tables_ref, q_out, kv_out):
     rows = mixed.shape[0]
     lane = iota((128, 128), 1)
     block = jnp.where((iota((128, 128), 0) >> 6) == (lane >> 6), 1.0 / HD, 0.0).astype(BF)
@@ -148,15 +150,10 @@
 
     low_half = iota((rows, 128), 1) < HD
     even = (iota((rows, 128), 1) & 1) == 0
-    cosine, sine = cos_ref[...], sin_ref[...]
-    gain_q = gain_ref[0:1, :]
-    gain_k = gain_ref[1:2, :]
-    gains = (
-        jnp.where(low_half, gain_q, gain_k),
-        jnp.broadcast_to(gain_q, (rows, 128)),
-        jnp.broadcast_to(gain_k, (rows, 128)),
-        jnp.where(low_half, gain_q, gain_k),
-    )
+    cosine, sine = tables_ref[0], tables_ref[1]
+    gain = gain_ref[...]
+    other_gain = pltpu.roll(jnp.broadcast_to(gain, (8, 128)), 64, 1)[0:1]
+    gains = (gain, other_gain, other_gain, gain)
     plain, turned = [], []
     for k in range(4):
         values = mixed[:, 128 * k : 128 * k + 128]
@@ -186,16 +183,52 @@
     return lax.dot_general(norm, weights, (((1,), (1,)), ((), ())), preferred_element_type=F32)
 
 
-def rec_kernel(scalars, x_ref, mod_ref, gain_ref, cos_ref, sin_ref, text_ref, w_ref, kv_out, norm_ref, w_vmem, sem):
+def small_copies(mod_hbm, rows_hbm, tables_hbm, layer, rows, mod_ref, gain_ref, tables_ref, sems):
+    copies = [
+        pltpu.make_async_copy(mod_hbm.at[layer], mod_ref, sems.at[0]),
+        pltpu.make_async_copy(rows_hbm.at[4 * layer, pl.ds(16, 1), pl.ds(0, 128)], gain_ref, sems.at[1]),
+        pltpu.make_async_copy(tables_hbm.at[:, rows, :], tables_ref, sems.at[2]),
+    ]
+    for copy in copies:
+        copy.start()
+    return copies
+
+
+def small_scratch(rows):
+    return [
+        pltpu.VMEM((6, D), F32),
+        pltpu.VMEM((1, 128), F32),
+        pltpu.VMEM((3, rows, 128), F32),
+        pltpu.SemaphoreType.DMA((3,)),
+    ]
+
+
+def rec_kernel(
+    scalars, gathered_ref, mod_hbm, rows_hbm, tables_hbm, w_ref,
+    kv_out, x_ref, norm_ref, w_vmem, sem, mod_ref, gain_ref, tables_ref, sems,
+):
     fetch = pltpu.make_async_copy(w_ref, w_vmem, sem)
     fetch.start()
-    normalize(x_ref, mod_ref, scalars[7], text_ref, norm_ref)
+    rows = pl.ds(GROUP, REC_GROUP)
+    small = small_copies(mod_hbm, rows_hbm, tables_hbm, scalars[7], rows, mod_ref, gain_ref, tables_ref, sems)
+    share = gathered_ref[:, D : D + 768]
+    for k in range(4):
+        pick = iota((REC_GROUP, GROUP), 1) == 4 * iota((REC_GROUP, GROUP), 0) + k
+        pick = jnp.where(pick, 1.0, 0.0).astype(BF)
+        x_ref[:, 768 * k : 768 * k + 768] = jnp.dot(pick, share, preferred_element_type=F32).astype(BF)
+    normalize(x_ref, mod_ref, tables_ref, norm_ref, small)
     fetch.wait()
-    heads_from(times_weights(norm_ref[...], w_vmem[...]), gain_ref, cos_ref, sin_ref, None, kv_out)
+    heads_from(times_weights(norm_ref[...], w_vmem[...]), gain_ref, tables_ref, None, kv_out)
 
 
 def qkv_kernel_of(layer):
-    def qkv_kernel(x_ref, mod_ref, gain_ref, cos_ref, sin_ref, text_ref, rec_ref, packed_ref, q_out, kv_out, weights_out, norm_ref, w_vmem, sems):
+    def qkv_kernel(
+        x_ref, rec_ref, mod_hbm, rows_hbm, tables_hbm, packed_ref,
+        q_out, kv_out, weights_out, norm_ref, w_vmem, sems, mod_ref, gain_ref, tables_ref, small_sems,
+    ):
+        rows = pl.ds(0, GROUP)
+        small = small_copies(mod_hbm, rows_hbm, tables_hbm, layer, rows, mod_ref, gain_ref, tables_ref, small_sems)
+
         def fetch(k):
             to = w_vmem.at[pl.ds(288 * (k % 2), 288), pl.ds(384 * (k // 2), 384)]
             return pltpu.make_async_copy(packed_ref.at[k, pl.ds(0, 288), :], to, sems.at[k])
@@ -208,14 +241,14 @@
             fetch(k).start()
         for k in range(16):
             pass_on(k).start()
-        normalize(x_ref, mod_ref, layer, text_ref, norm_ref)
+        normalize(x_ref, mod_ref, tables_ref, norm_ref, small)
         mixed = jnp.zeros((GROUP, 576), F32)
         for piece in range(4):
             for k in range(4 * piece, 4 * piece + 4):
                 fetch(k).wait()
             lanes = slice(768 * piece, 768 * piece + 768)
             mixed = mixed + times_weights(norm_ref[:, lanes], w_vmem[:, lanes])
-        heads_from(mixed, gain_ref, cos_ref, sin_ref, q_out, kv_out)
+        heads_from(mixed, gain_ref, tables_ref, q_out, kv_out)
         if layer == 0:
             for copy in range(kv_out.shape[0]):
                 kv_out[copy, GROUP:, :] = rec_ref[0]
@@ -277,8 +310,8 @@
 
 def attend_kernel_of(layer):
     def attend_kernel(
-        scalars, q_ref, fresh_ref, target_ref, rec_ref, stale_ref, own_hbm, other_hbm,
-        keep_out, send_out, weights_out, base_ref, cache_ref, rec_vmem, sems,
+        scalars, q_ref, fresh_ref, targets_hbm, rec_ref, stale_ref, own_hbm, other_hbm,
+        keep_out, send_out, weights_out, base_ref, cache_ref, rec_vmem, target_ref, sems,
     ):
         section = scalars[7]
         rec_copies = [
@@ -289,6 +322,7 @@
             )
             for h in range(2)
         ]
+        rec_copies.append(pltpu.make_async_copy(targets_hbm, target_ref, sems.at[6]))
         for copy in rec_copies:
             copy.start()
         from_base = [
@@ -304,11 +338,11 @@
         for copy in from_base + weights:
             copy.start()
         rec_vmem[64:, :] = jnp.zeros((64, 384), BF)
+        for copy in rec_copies:
+            copy.wait()
         match = iota((1024, 128), 0) == target_ref[0:1, :]
         chosen = jnp.where(match, 1.0, 0.0)
         hit = jnp.sum(chosen, axis=1, keepdims=True) > 0.5
-        for copy in rec_copies:
-            copy.wait()
         placed = jnp.dot(chosen.astype(BF), rec_vmem[...], preferred_element_type=F32)
         for copy in from_base:
             copy.wait()
@@ -342,16 +376,22 @@
 
 
 def residual_kernel_of(layer):
-    def residual_kernel(scalars, parts_ref, x_ref, mod_ref, out_ref):
+    def residual_kernel(scalars, parts_ref, x_ref, mod_hbm, out_ref, mod_ref, sem):
+        fetch = pltpu.make_async_copy(mod_hbm.at[layer], mod_ref, sem)
+        fetch.start()
         row = iota((8, 128), 0)
         offset = (2 * (row >> 2) + scalars[0]) * 64 + 4 * scalars[10] + (row & 3)
         text = (offset + scalars[6]) < TXT
-        for k in range(D // 128):
-            lanes = slice(128 * k, 128 * k + 128)
+        chunks = [slice(128 * k, 128 * k + 128) for k in range(D // 128)]
+        totals = []
+        for lanes in chunks:
             total = parts_ref[0, :, lanes].astype(F32)
             for source in range(1, 8):
                 total = total + parts_ref[source, :, lanes].astype(F32)
-            gate = jnp.where(text, mod_ref[layer, 5:6, lanes], mod_ref[layer, 2:3, lanes])
+            totals.append(total)
+        fetch.wait()
+        for lanes, total in zip(chunks, totals):
+            gate = jnp.where(text, mod_ref[5:6, lanes], mod_ref[2:3, lanes])
             out_ref[:, lanes] = (x_ref[:, lanes].astype(F32) + gate * total).astype(BF)
 
     return residual_kernel
@@ -439,10 +479,9 @@
     scalars = jnp.concatenate(
         [half[None], starts, timestep % 8, own_start, jnp.stack([section, row_index, core, col]), counts, req[None]]
     ).astype(jnp.int32)
-    table_rows = shape_of((GROUP + REC_GROUP, 128), F32)
-    mod_part, cosine, sine, text = call(
+    mod_part, tables = call(
         prepare_kernel,
-        (shape_of((2, 288), BF), table_rows, table_rows, table_rows),
+        (shape_of((2, 288), BF), shape_of((3, GROUP + REC_GROUP, 128), F32)),
         [SMEM, VMEM, VMEM, VMEM, VMEM],
         "prepare",
     )(
@@ -462,7 +501,6 @@
         axis=1,
     )
     gathered = lax.all_gather(payload, COL, axis=0, tiled=True)
-    rec_rows = gathered[:, D : D + 768].reshape(REC_GROUP, D)
     pieces = gathered[:, D + 768 : D + 840].reshape(16, 2, 288).astype(F32)
     summed = pieces[:, 0] + pieces[:, 1]
     gain_row = jnp.pad(qk_gain[0].reshape(1, 128), ((0, 0), (0, 160)))
@@ -470,21 +508,24 @@
     everyone = ("section",) + ROW
     rows = lax.all_to_all(jnp.broadcast_to(rows, (lax.axis_size(everyone), 17, 288)), everyone, 0, 0)
     modulation = rows[:, :16].reshape(sections, 6, D)
-    all_gains = rows.reshape(sections, 4, 17, 288)[:, 0, 16, :128].reshape(sections, 2, HD)
-    all_gains = jnp.concatenate([all_gains, all_gains], axis=2)
-    own_gains = jnp.concatenate([qk_gain[0], qk_gain[0]], axis=1)
-
+    in_hbm = [pltpu.with_memory_space_constraint(value, pltpu.HBM) for value in (modulation, rows, tables)]
     rec_fresh = call(
         rec_kernel,
         shape_of((1, REC_GROUP, 384), BF),
-        [SMEM] + [VMEM] * 6 + [HBM],
+        [SMEM, VMEM] + [HBM] * 4,
         "rec",
-        scratch=[pltpu.VMEM((REC_GROUP, D), BF), pltpu.VMEM((576, D), BF), pltpu.SemaphoreType.DMA],
-    )(scalars, rec_rows, modulation, own_gains, cosine[GROUP:], sine[GROUP:], text[GROUP:], weights_qkv)
-    cosine, sine, text = cosine[:GROUP], sine[:GROUP], text[:GROUP]
+        scratch=[
+            pltpu.VMEM((REC_GROUP, D), BF),
+            pltpu.VMEM((REC_GROUP, D), BF),
+            pltpu.VMEM((576, D), BF),
+            pltpu.SemaphoreType.DMA,
+        ]
+        + small_scratch(REC_GROUP),
+    )(scalars, gathered, *in_hbm, weights_qkv)
+    targets = pltpu.with_memory_space_constraint(targets, pltpu.HBM)
 
     half_rows = shape_of((64, 256), BF)
-    current, group, outs, first_fresh = tokens, gathered[:, :D], [], None
+    current, group, outs, first_fresh = tokens, gathered, [], None
     for layer in range(sections):
         packed = pltpu.with_memory_space_constraint(layers[layer], pltpu.HBM)
         if layer > 0:
@@ -496,32 +537,38 @@
                 shape_of((copies, GROUP + (REC_GROUP if layer == 0 else 0), 384), BF),
                 shape_of((192, D), BF),
             ),
-            [VMEM] * 7 + [HBM],
+            [VMEM] * 2 + [HBM] * 4,
             "qkv",
-            scratch=[pltpu.VMEM((GROUP, D), BF), pltpu.VMEM((576, D), BF), pltpu.SemaphoreType.DMA((32,))],
-        )(group, modulation, all_gains[layer], cosine, sine, text, rec_fresh, packed)
+            scratch=[pltpu.VMEM((GROUP, D), BF), pltpu.VMEM((576, D), BF), pltpu.SemaphoreType.DMA((32,))]
+            + small_scratch(GROUP),
+        )(group, rec_fresh, *in_hbm, packed)
         out_other = swapped(out_own, "core")
         fresh = lax.all_to_all(fresh, peers, 0, 0)
         first_fresh = fresh if layer == 0 else first_fresh
         keep, send, weights_out = call(
             attend_kernel_of(layer),
             (half_rows, half_rows, shape_of((2, 192, D), BF)),
-            [SMEM] + [VMEM] * 3 + [HBM] * 4,
+            [SMEM] + [VMEM] * 2 + [HBM] * 5,
             "attend",
             scratch=[
                 pltpu.VMEM((1024, 384), BF),
                 pltpu.VMEM((1024, 384), BF),
                 pltpu.VMEM((128, 384), BF),
-                pltpu.SemaphoreType.DMA((6,)),
+                pltpu.VMEM((8, 128), jnp.int32),
+                pltpu.SemaphoreType.DMA((7,)),
             ],
         )(scalars, queries, fresh, targets, first_fresh, stale_all, out_own, out_other)
         projected = call(project_kernel, shape_of((64, D), BF), [VMEM] * 3, "project")(
             keep, swapped(send, "core"), weights_out
         )
         parts = lax.all_to_all(projected.reshape(8, 8, D), "z", 0, 0)
-        current = call(residual_kernel_of(layer), shape_of((8, D), BF), [SMEM, VMEM, VMEM, VMEM], "residual")(
-            scalars, parts, current, modulation
-        )
+        current = call(
+            residual_kernel_of(layer),
+            shape_of((8, D), BF),
+            [SMEM, VMEM, VMEM, HBM],
+            "residual",
+            scratch=[pltpu.VMEM((6, D), F32), pltpu.SemaphoreType.DMA],
+        )(scalars, parts, current, in_hbm[0])
         outs.append(current)
 
     leaving = jnp.stack(outs).reshape(sections * 2, 4, D)

time: 418 us -> 419 us (level)
  local copies, waits for them, and re-layouts: 45.7 us -> 22.9 us
  waiting for transfers between devices: 43.8 us -> 57.5 us
  Pallas kernels: 41.6 us -> 51.6 us
    unnamed x108 -> x34, local copies, waits for them, and re-layouts: 22.9 us -> 7.52 us
    all_to_all x1, waiting for transfers between devices: 1.21 us -> 16 us  [local(): lax.all_to_all(jnp.broadcast_to(stale_share, (copies, STALE, 384)), peers...]
    pallas_call x4, Pallas kernels: 18 us -> 25.2 us  [local(): call(qkv_kernel_of(layer), (shape_of((GROUP, 384), BF), shape_of((copies,...]
    slice x9 -> x0, local copies, waits for them, and re-layouts: 6.49 us -> none  [the longest x3 1.87 us: local(): cosine, sine, text = (cosine[:GROUP], sine[:GROUP], text[:GROUP])]
    all_gather x3, blocking collectives: 50.7 us -> 55.1 us  [local(): group = lax.all_gather(current, COL, axis=0, tiled=True)]
  transfers between devices with their start and end apart: 17 -> 17, of which waited for: 7 -> 7; matrix products, arithmetic and copies ran while one was open for 6% -> 4% of each run, Pallas kernels for 8% -> 9%
where the time goes in v2:
time: 419 us; the launch traced here: 417 us
  blocking collectives  248 us (59%)
  waiting for transfers between devices  57.5 us (14%)
  Pallas kernels  51.6 us (12%)
  local copies, waits for them, and re-layouts  22.9 us (5%)
  starting transfers between devices  20.5 us (5%)
  between operations  16.2 us (4%)
    all_to_all x4, blocking collectives, local(): parts = lax.all_to_all(projected.reshape(8, 8, D), 'z', 0, 0)  78.8 us
    all_to_all x3, blocking collectives, local(): fresh = lax.all_to_all(fresh, peers, 0, 0)  58 us
    all_gather x3, blocking collectives, local(): group = lax.all_gather(current, COL, axis=0, tiled=True)  55.1 us
    pallas_call x4, Pallas kernels, local(): call(qkv_kernel_of(layer), (shape_of((GROUP, 384), BF), shape_of((copies,...  25.2 us
    all_gather x1, blocking collectives, local(): gathered = lax.all_gather(payload, COL, axis=0, tiled=True)  22.8 us
    all_to_all x1, blocking collectives, local(): chunks = lax.all_to_all(packed, 'section', 0, 0)  20.8 us
    all_to_all x1, waiting for transfers between devices, local(): fresh = lax.all_to_all(fresh, peers, 0, 0)  19.9 us
    all_to_all x1, waiting for transfers between devices, local(): lax.all_to_all(jnp.broadcast_to(stale_share, (copies, STALE, 384)), peers...  16 us
  transfers between devices with their start and end apart: 17, of which 7 were waited for; matrix products, arithmetic and copies ran while one was open for 4% of the time, Pallas kernels for 9%

profile of v2, /device:TPU:2, one launch (start us, length us, event | category | flops | bytes accessed | tf_op | source)
XLA Modules:
  0.0 417.4 jit_solution(1511767233087749099)
XLA Ops:
  6.5 1.6 pack.1
  8.1 20.8 %all_to_all.60 = bf16[4,384,384]{2,1,0:T(8,128)(2,1)S(1)} all-to-all(bf16[4,384,384]{2,1,0:T(8,128)(2,1)S(1)} %pack.1), channel_id=1, replica_groups=mesh['section'=4,'req'=2,'half'=2,'z'=8,'core'=2] {'section'}, dimensions={0} | all-to-all | bytes 2359296 | tf_op jit(solution)/shard_map/all_to_all | solution.py:444
  28.9 1.1 fusion.3
  32.4 2.2 collective-permute-start
  34.6 1.4 collective-permute-start.1
  41.3 1.4 concatenate.25.scalars
  45.0 22.8 %all_gather.24.gathered_ref.x_ref = bf16[128,3968]{1,0:T(8,128)(2,1)S(1)} all-gather(bf16[8,3968]{1,0:T(8,128)(2,1)S(1)} %fusion.1), channel_id=1, replica_groups=mesh['section'=4,'req'=2,'half'=2,'z'=8,'core'=2] {'z','core'}, dimensions={0}, use_global_device_ids=true | all-gather | bytes 1079296 | tf_op jit(solution)/shard_map/all_gather | solution.py:503
  68.9 5.4 %all-to-all-start = ((f32[16,17,288]{2,1,0:T(8,128)}), f32[16,17,288]{2,1,0:T(8,128)S(1)}, u32[]{:S(2)}, u32[]{:S(2)}) async-start(f32[16,17,288]{2,1,0:T(8,128)} %broadcast_in_dim.41), calls=%async_computation | async-start | bytes 1179648 | tf_op jit(solution)/shard_map/all_to_all | solution.py:509
  74.8 1.7 constant_dynamic-slice_fusion
  77.6 14.9 %all-to-all-done.rows_hbm = f32[16,17,288]{2,1,0:T(8,128)S(1)} async-done(((f32[16,17,288]{2,1,0:T(8,128)}), f32[16,17,288]{2,1,0:T(8,128)S(1)}, u32[]{:S(2)}, u32[]{:S(2)}) %all-to-all-start) | async-done | bytes 313376 | tf_op jit(solution)/shard_map/all_to_all | solution.py:509
  92.5 1.6 broadcast_in_dim.45
  94.1 5.0 %all-to-all-start.3 = ((bf16[8,384,384]{2,1,0:T(8,128)(2,1)}), bf16[8,384,384]{2,1,0:T(8,128)(2,1)S(1)}, u32[]{:S(2)}, u32[]{:S(2)}) async-start(bf16[8,384,384]{2,1,0:T(8,128)(2,1)} %broadcast_in_dim.45), calls=%async_computation.3 | async-start | bytes 4718592 | tf_op jit(solution)/shard_map/all_to_all | solution.py:452
  99.1 1.8 slice.125
  100.9 2.1 reshape.70.mod_hbm
  102.9 4.5 %rec.1.rec_ref = bf16[1,32,384]{2,1,0:T(8,128)(2,1)S(1)} custom-call(s32[16]{0:T(128)S(1)} %concatenate.25.scalars, bf16[128,3968]{1,0:T(8,128)(2,1)S(1)} %all_gather.24.gathered_ref.x_ref, f32[4,6,3072]{2,1,0:T(8,128)} %reshape.70.mod_hbm, f32[16,17,288]{2,1,0:T(8,128)} %copy-done.11, f32[3,160,128]{2,1,0:T(8,128)} %copy-done.2, bf16[576,3072]{1,0:T(8,128)(2,1)} %bitcast.78), custom_call_target="tpu_custom_call" | custom-call | tf_op jit(solution)/shard_map/rec/pallas_call | solution.py:512
  107.5 7.0 %qkv.4 = (bf16[128,384]{1,0:T(8,128)(2,1)S(1)}, bf16[8,160,384]{2,1,0:T(8,128)(2,1)S(1)}, bf16[192,3072]{1,0:T(8,128)(2,1)}) custom-call(bf16[128,3968]{1,0:T(8,128)(2,1)S(1)} %all_gather.24.gathered_ref.x_ref, bf16[1,32,384]{2,1,0:T(8,128)(2,1)S(1)} %rec.1.rec_ref, f32[4,6,3072]{2,1,0:T(8,128)} %reshape.70.mod_hbm, f32[16,17,288]{2,1,0:T(8,128)} %copy-done.11, ...), custom_call_target="tpu_custom_call" | custom-call | tf_op jit(solution)/shard_map/qkv/pallas_call | solution.py:533
  116.1 16.0 %all-to-all-done.3.stale_ref = bf16[8,384,384]{2,1,0:T(8,128)(2,1)S(1)} async-done(((bf16[8,384,384]{2,1,0:T(8,128)(2,1)}), bf16[8,384,384]{2,1,0:T(8,128)(2,1)S(1)}, u32[]{:S(2)}, u32[]{:S(2)}) %all-to-all-start.3) | async-done | bytes 2359328 | tf_op jit(solution)/shard_map/all_to_all | solution.py:452
  132.1 4.7 %all-to-all-start.2 = ((bf16[8,160,384]{2,1,0:T(8,128)(2,1)}), bf16[8,160,384]{2,1,0:T(8,128)(2,1)S(1)}, u32[]{:S(2)}, u32[]{:S(2)}) async-start(bf16[8,160,384]{2,1,0:T(8,128)(2,1)} %copy-done.6), calls=%async_computation.2 | async-start | bytes 1966080 | tf_op jit(solution)/shard_map/all_to_all | solution.py:546
  136.9 19.9 %all-to-all-done.2.fresh_ref.rec_ref = bf16[8,160,384]{2,1,0:T(8,128)(2,1)S(1)} async-done(((bf16[8,160,384]{2,1,0:T(8,128)(2,1)}), bf16[8,160,384]{2,1,0:T(8,128)(2,1)S(1)}, u32[]{:S(2)}, u32[]{:S(2)}) %all-to-all-start.2) | async-done | bytes 983072 | tf_op jit(solution)/shard_map/all_to_all | solution.py:546
  158.3 2.8 attend.4
  161.2 1.2 collective-permute-done.3.got_ref
  162.9 17.7 %all_to_all.61.parts_ref = bf16[8,8,3072]{2,1,0:T(8,128)(2,1)S(1)} all-to-all(bf16[8,8,3072]{2,1,0:T(8,128)(2,1)S(1)} %bitcast.68), channel_id=1, replica_groups=mesh['section'=4,'req'=2,'half'=2,'z'=8,'core'=2] {'z'}, dimensions={0} | all-to-all | bytes 786432 | tf_op jit(solution)/shard_map/all_to_all | solution.py:564
  180.6 1.5 residual.4.x_ref
  182.1 18.4 %all_gather.26.x_ref = bf16[128,3072]{1,0:T(8,128)(2,1)} all-gather(bf16[8,3072]{1,0:T(8,128)(2,1)S(1)} %residual.4.x_ref), channel_id=1, replica_groups=mesh['section'=4,'req'=2,'half'=2,'z'=8,'core'=2] {'z','core'}, dimensions={0}, use_global_device_ids=true | all-gather | bytes 835584 | tf_op jit(solution)/shard_map/all_gather | solution.py:532
  200.5 1.1 copy-done.4
  201.7 6.3 %qkv.5 = (bf16[128,384]{1,0:T(8,128)(2,1)S(1)}, bf16[8,128,384]{2,1,0:T(8,128)(2,1)S(1)}, bf16[192,3072]{1,0:T(8,128)(2,1)S(1)}) custom-call(bf16[128,3072]{1,0:T(8,128)(2,1)S(1)} %copy-done.4, bf16[1,32,384]{2,1,0:T(8,128)(2,1)S(1)} %rec.1.rec_ref, f32[4,6,3072]{2,1,0:T(8,128)} %reshape.70.mod_hbm, f32[16,17,288]{2,1,0:T(8,128)} %copy-done.11, ...), custom_call_target="tpu_custom_call" | custom-call | tf_op jit(solution)/shard_map/qkv/pallas_call | solution.py:533
  208.4 24.7 %all_to_all.62.fresh_ref = bf16[8,128,384]{2,1,0:T(8,128)(2,1)S(1)} all-to-all(bf16[8,128,384]{2,1,0:T(8,128)(2,1)S(1)} %get-tuple-element.40), channel_id=1, replica_groups=mesh['section'=4,'req'=2,'half'=2,'z'=8,'core'=2] {'section','half'}, dimensions={0} | all-to-all | bytes 1572864 | tf_op jit(solution)/shard_map/all_to_all | solution.py:546
  233.1 2.8 attend.5
  236.0 1.2 collective-permute-done.5.got_ref
  237.8 20.6 %all_to_all.63.parts_ref = bf16[8,8,3072]{2,1,0:T(8,128)(2,1)S(1)} all-to-all(bf16[8,8,3072]{2,1,0:T(8,128)(2,1)S(1)} %bitcast.69), channel_id=1, replica_groups=mesh['section'=4,'req'=2,'half'=2,'z'=8,'core'=2] {'z'}, dimensions={0} | all-to-all | bytes 786432 | tf_op jit(solution)/shard_map/all_to_all | solution.py:564
  258.4 1.5 residual.5.x_ref
  259.8 18.2 %all_gather.28.x_ref = bf16[128,3072]{1,0:T(8,128)(2,1)} all-gather(bf16[8,3072]{1,0:T(8,128)(2,1)S(1)} %residual.5.x_ref), channel_id=1, replica_groups=mesh['section'=4,'req'=2,'half'=2,'z'=8,'core'=2] {'z','core'}, dimensions={0}, use_global_device_ids=true | all-gather | bytes 835584 | tf_op jit(solution)/shard_map/all_gather | solution.py:532
  278.1 1.2 copy-done.5
  279.3 6.0 %qkv.6 = (bf16[128,384]{1,0:T(8,128)(2,1)S(1)}, bf16[8,128,384]{2,1,0:T(8,128)(2,1)S(1)}, bf16[192,3072]{1,0:T(8,128)(2,1)S(1)}) custom-call(bf16[128,3072]{1,0:T(8,128)(2,1)S(1)} %copy-done.5, bf16[1,32,384]{2,1,0:T(8,128)(2,1)S(1)} %rec.1.rec_ref, f32[4,6,3072]{2,1,0:T(8,128)} %reshape.70.mod_hbm, f32[16,17,288]{2,1,0:T(8,128)} %copy-done.11, ...), custom_call_target="tpu_custom_call" | custom-call | tf_op jit(solution)/shard_map/qkv/pallas_call | solution.py:533
  285.7 17.4 %all_to_all.64.fresh_ref = bf16[8,128,384]{2,1,0:T(8,128)(2,1)S(1)} all-to-all(bf16[8,128,384]{2,1,0:T(8,128)(2,1)S(1)} %get-tuple-element.46), channel_id=1, replica_groups=mesh['section'=4,'req'=2,'half'=2,'z'=8,'core'=2] {'section','half'}, dimensions={0} | all-to-all | bytes 1572864 | tf_op jit(solution)/shard_map/all_to_all | solution.py:546
  303.1 2.8 attend.6
  306.0 1.2 collective-permute-done.7.got_ref
  307.8 21.8 %all_to_all.65.parts_ref = bf16[8,8,3072]{2,1,0:T(8,128)(2,1)S(1)} all-to-all(bf16[8,8,3072]{2,1,0:T(8,128)(2,1)S(1)} %bitcast.70), channel_id=1, replica_groups=mesh['section'=4,'req'=2,'half'=2,'z'=8,'core'=2] {'z'}, dimensions={0} | all-to-all | bytes 786432 | tf_op jit(solution)/shard_map/all_to_all | solution.py:564
  329.6 1.5 residual.6.x_ref
  331.1 18.5 %all_gather.30.x_ref = bf16[128,3072]{1,0:T(8,128)(2,1)} all-gather(bf16[8,3072]{1,0:T(8,128)(2,1)S(1)} %residual.6.x_ref), channel_id=1, replica_groups=mesh['section'=4,'req'=2,'half'=2,'z'=8,'core'=2] {'z','core'}, dimensions={0}, use_global_device_ids=true | all-gather | bytes 835584 | tf_op jit(solution)/shard_map/all_gather | solution.py:532
  349.5 1.1 copy-done.3
  350.7 5.9 %qkv.7 = (bf16[128,384]{1,0:T(8,128)(2,1)S(1)}, bf16[8,128,384]{2,1,0:T(8,128)(2,1)S(1)}, bf16[192,3072]{1,0:T(8,128)(2,1)S(1)}) custom-call(bf16[128,3072]{1,0:T(8,128)(2,1)S(1)} %copy-done.3, bf16[1,32,384]{2,1,0:T(8,128)(2,1)S(1)} %rec.1.rec_ref, f32[4,6,3072]{2,1,0:T(8,128)} %reshape.70.mod_hbm, f32[16,17,288]{2,1,0:T(8,128)} %copy-done.11, ...), custom_call_target="tpu_custom_call" | custom-call | tf_op jit(solution)/shard_map/qkv/pallas_call | solution.py:533
  357.0 15.9 %all_to_all.66.fresh_ref = bf16[8,128,384]{2,1,0:T(8,128)(2,1)S(1)} all-to-all(bf16[8,128,384]{2,1,0:T(8,128)(2,1)S(1)} %get-tuple-element.52), channel_id=1, replica_groups=mesh['section'=4,'req'=2,'half'=2,'z'=8,'core'=2] {'section','half'}, dimensions={0} | all-to-all | bytes 1572864 | tf_op jit(solution)/shard_map/all_to_all | solution.py:546
  373.0 2.8 attend.7
  375.9 1.2 collective-permute-done.9.got_ref
  377.7 18.7 %all_to_all.67.parts_ref = bf16[8,8,3072]{2,1,0:T(8,128)(2,1)S(1)} all-to-all(bf16[8,8,3072]{2,1,0:T(8,128)(2,1)S(1)} %bitcast.71), channel_id=1, replica_groups=mesh['section'=4,'req'=2,'half'=2,'z'=8,'core'=2] {'z'}, dimensions={0} | all-to-all | bytes 786432 | tf_op jit(solution)/shard_map/all_to_all | solution.py:564
  396.4 1.5 residual.7
  398.0 12.0 %all_to_all.68 = bf16[8,4,3072]{2,1,0:T(4,128)(2,1)S(1)} all-to-all(bf16[8,4,3072]{2,1,0:T(4,128)(2,1)S(1)} %reshape.75), channel_id=1, replica_groups=mesh['section'=4,'req'=2,'half'=2,'z'=8,'core'=2] {'section','req'}, dimensions={0} | all-to-all | bytes 393216 | tf_op jit(solution)/shard_map/all_to_all | solution.py:575
  (101 shorter events, 17.8 us)
Async XLA Ops:
  6.5 33.2 %copy-start = (f32[1000,512]{1,0:T(8,128)S(1)}, f32[1000,512]{1,0:T(8,128)}, u32[]{:S(2)}) copy-start(f32[1000,512]{1,0:T(8,128)} %param.15) | copy-start | bytes 6144004
  6.5 100.9 %all-gather.5.cloned.1.call-start = ((), (), s32[]{:S(2)}) async-start(), calls=%async_computation.12 | async-start | bytes 5013504 | tf_op jit(solution)/shard_map/all_gather | solution.py:446
  28.9 5.7 %copy-start.12 = (bf16[1,1,2,3072]{3,2,1,0:T(2,128)(2,1)S(1)}, bf16[1,1,2,3072]{3,2,1,0:T(2,128)(2,1)}, u32[]{:S(2)}) copy-start(bf16[1,1,2,3072]{3,2,1,0:T(2,128)(2,1)} %param.21) | copy-start | bytes 36868
  28.9 7.8 %copy-start.14 = (s32[2,64]{1,0:T(2,128)S(1)}, s32[2,64]{1,0:T(2,128)}, u32[]{:S(2)}) copy-start(s32[2,64]{1,0:T(2,128)} %param.22) | copy-start | bytes 1540
  28.9 8.3 %copy-start.13 = (s32[2,4]{1,0:T(2,128)S(1)}, s32[2,4]{1,0:T(2,128)}, u32[]{:S(2)}) copy-start(s32[2,4]{1,0:T(2,128)} %param.13) | copy-start | bytes 100
  28.9 14.0 %copy-start.7 = (bf16[1,512,288]{1,2,0:T(8,128)(2,1)S(1)}, bf16[1,512,288]{1,2,0:T(8,128)(2,1)}, u32[]{:S(2)}) copy-start(bf16[1,512,288]{1,2,0:T(8,128)(2,1)} %param.16) | copy-start | bytes 884740
  28.9 14.0 %copy-start.10 = (f32[1,128]{1,0:T(1,128)S(1)}, f32[1,128]{1,0:T(1,128)}, u32[]{:S(2)}) copy-start(f32[1,128]{1,0:T(1,128)} %constant.86.clone.rate_ref) | copy-start | bytes 1540
  28.9 15.8 %copy-start.15 = (f32[1,2,64]{2,1,0:T(2,128)S(1)}, f32[1,2,64]{2,1,0:T(2,128)}, u32[]{:S(2)}) copy-start(f32[1,2,64]{2,1,0:T(2,128)} %param.19) | copy-start | bytes 1540
  30.0 170.5 %all-gather.7.cloned.1.call-start = ((), (), s32[]{:S(2)}) async-start(), calls=%async_computation.13 | async-start | bytes 5013504 | tf_op jit(solution)/shard_map/all_gather | solution.py:446
  30.8 247.3 %all-gather.9.cloned.1.call-start = ((), (), s32[]{:S(2)}) async-start(), calls=%async_computation.14 | async-start | bytes 5013504 | tf_op jit(solution)/shard_map/all_gather | solution.py:446
  32.4 12.5 %collective-permute-start = (bf16[4,2,3072]{2,0,1:T(4,128)(2,1)S(1)}, bf16[4,2,3072]{2,0,1:T(4,128)(2,1)S(1)}, u32[]{:S(2)}, u32[]{:S(2)}) collective-permute-start(bf16[4,2,3072]{2,0,1:T(4,128)(2,1)S(1)} %bitcast.82), channel_id=1, source_target_pairs={{0,32},{32,0},{1,33},{33,1},{2,34},{34,2},{3,35},{35,3},{4,36},{36... | collective-permute-start | bytes 147464 | tf_op jit(solution)/shard_map/ppermute | solution.py:405
  34.6 10.2 %collective-permute-start.1 = (bf16[1,2,3072]{2,1,0:T(2,128)(2,1)S(1)}, bf16[1,2,3072]{2,1,0:T(2,128)(2,1)S(1)}, u32[]{:S(2)}, u32[]{:S(2)}) collective-permute-start(bf16[1,2,3072]{2,1,0:T(2,128)(2,1)S(1)} %bitcast.85), channel_id=1, source_target_pairs={{0,32},{32,0},{1,33},{33,1},{2,34},{34,2},{3,35},{35,3},{4,36},{36... | collective-permute-start | bytes 36872 | tf_op jit(solution)/shard_map/ppermute | solution.py:405
  43.9 0.7 copy-start.2
  68.9 23.6 %all-to-all-start = ((f32[16,17,288]{2,1,0:T(8,128)}), f32[16,17,288]{2,1,0:T(8,128)S(1)}, u32[]{:S(2)}, u32[]{:S(2)}) async-start(f32[16,17,288]{2,1,0:T(8,128)} %broadcast_in_dim.41), calls=%async_computation | async-start | bytes 1179648 | tf_op jit(solution)/shard_map/all_to_all | solution.py:509
  74.2 275.3 %all-gather.11.cloned.1.call-start = ((), (), s32[]{:S(2)}) async-start(), calls=%async_computation.15 | async-start | bytes 5013504 | tf_op jit(solution)/shard_map/all_gather | solution.py:446
  92.5 1.6 copy-start.11
  94.1 38.0 %all-to-all-start.3 = ((bf16[8,384,384]{2,1,0:T(8,128)(2,1)}), bf16[8,384,384]{2,1,0:T(8,128)(2,1)S(1)}, u32[]{:S(2)}, u32[]{:S(2)}) async-start(bf16[8,384,384]{2,1,0:T(8,128)(2,1)} %broadcast_in_dim.45), calls=%async_computation.3 | async-start | bytes 4718592 | tf_op jit(solution)/shard_map/all_to_all | solution.py:452
  114.4 0.6 copy-start.8
  115.1 1.0 copy-start.6
  116.0 40.7 %collective-permute-start.2 = (bf16[192,3072]{1,0:T(8,128)(2,1)}, bf16[192,3072]{1,0:T(8,128)(2,1)}, u32[]{:S(2)}, u32[]{:S(2)}) collective-permute-start(bf16[192,3072]{1,0:T(8,128)(2,1)} %get-tuple-element.35.own_hbm), channel_id=1, source_target_pairs={{0,1},{1,0},{2,3},{3,2},{4,5},{5,4},{6,7},{7,6},{8,9},{9,8},{10,11... | collective-permute-start | bytes 3538952 | tf_op jit(solution)/shard_map/ppermute | solution.py:405
  132.1 24.7 %all-to-all-start.2 = ((bf16[8,160,384]{2,1,0:T(8,128)(2,1)}), bf16[8,160,384]{2,1,0:T(8,128)(2,1)S(1)}, u32[]{:S(2)}, u32[]{:S(2)}) async-start(bf16[8,160,384]{2,1,0:T(8,128)(2,1)} %copy-done.6), calls=%async_computation.2 | async-start | bytes 1966080 | tf_op jit(solution)/shard_map/all_to_all | solution.py:546
  157.4 0.9 copy-start.9
  161.1 1.3 collective-permute-start.3
  200.5 1.1 copy-start.4
  208.0 25.1 %collective-permute-start.4 = (bf16[192,3072]{1,0:T(8,128)(2,1)S(1)}, bf16[192,3072]{1,0:T(8,128)(2,1)S(1)}, u32[]{:S(2)}, u32[]{:S(2)}) collective-permute-start(bf16[192,3072]{1,0:T(8,128)(2,1)S(1)} %get-tuple-element.41.own_hbm), channel_id=1, source_target_pairs={{0,1},{1,0},{2,3},{3,2},{4,5},{5,4},{6,7},{7,6},{8,9},{9,8},{10,11... | collective-permute-start | bytes 3538952 | tf_op jit(solution)/shard_map/ppermute | solution.py:405
  235.9 1.3 collective-permute-start.5
  278.1 1.2 copy-start.5
  285.3 17.8 %collective-permute-start.6 = (bf16[192,3072]{1,0:T(8,128)(2,1)S(1)}, bf16[192,3072]{1,0:T(8,128)(2,1)S(1)}, u32[]{:S(2)}, u32[]{:S(2)}) collective-permute-start(bf16[192,3072]{1,0:T(8,128)(2,1)S(1)} %get-tuple-element.47.own_hbm), channel_id=1, source_target_pairs={{0,1},{1,0},{2,3},{3,2},{4,5},{5,4},{6,7},{7,6},{8,9},{9,8},{10,11... | collective-permute-start | bytes 3538952 | tf_op jit(solution)/shard_map/ppermute | solution.py:405
  305.9 1.3 collective-permute-start.7
  349.5 1.1 copy-start.3
  356.6 16.4 %collective-permute-start.8 = (bf16[192,3072]{1,0:T(8,128)(2,1)S(1)}, bf16[192,3072]{1,0:T(8,128)(2,1)S(1)}, u32[]{:S(2)}, u32[]{:S(2)}) collective-permute-start(bf16[192,3072]{1,0:T(8,128)(2,1)S(1)} %get-tuple-element.53.own_hbm), channel_id=1, source_target_pairs={{0,1},{1,0},{2,3},{3,2},{4,5},{5,4},{6,7},{7,6},{8,9},{9,8},{10,11... | collective-permute-start | bytes 3538952 | tf_op jit(solution)/shard_map/ppermute | solution.py:405
  375.8 1.3 collective-permute-start.9
  377.6 33.2 %copy-start.1 = (f32[1000,512]{1,0:T(8,128)S(1)}, f32[1000,512]{1,0:T(8,128)}, u32[]{:S(2)}) copy-start(f32[1000,512]{1,0:T(8,128)} %param.15) | copy-start | bytes 6144004
Sparse Core Ops, SparseCore 0:
  30.1 66.1 all-gather.4
  98.8 70.3 all-gather.6
  171.7 62.0 all-gather.8
  236.1 59.0 all-gather.10

commit v3 on v2

--- a/solution.py
+++ b/solution.py
@@ -224,7 +224,7 @@
 def qkv_kernel_of(layer):
     def qkv_kernel(
         x_ref, rec_ref, mod_hbm, rows_hbm, tables_hbm, packed_ref,
-        q_out, kv_out, weights_out, norm_ref, w_vmem, sems, mod_ref, gain_ref, tables_ref, small_sems,
+        q_out, kv_out, weights_out, gates_out, norm_ref, w_vmem, sems, mod_ref, gain_ref, tables_ref, small_sems,
     ):
         rows = pl.ds(0, GROUP)
         small = small_copies(mod_hbm, rows_hbm, tables_hbm, layer, rows, mod_ref, gain_ref, tables_ref, small_sems)
@@ -249,6 +249,8 @@
             lanes = slice(768 * piece, 768 * piece + 768)
             mixed = mixed + times_weights(norm_ref[:, lanes], w_vmem[:, lanes])
         heads_from(mixed, gain_ref, tables_ref, q_out, kv_out)
+        gates_out[0:1, :] = mod_ref[2:3, :]
+        gates_out[1:2, :] = mod_ref[5:6, :]
         if layer == 0:
             for copy in range(kv_out.shape[0]):
                 kv_out[copy, GROUP:, :] = rec_ref[0]
@@ -309,10 +311,11 @@
 
 
 def attend_kernel_of(layer):
-    def attend_kernel(
-        scalars, q_ref, fresh_ref, targets_hbm, rec_ref, stale_ref, own_hbm, other_hbm,
-        keep_out, send_out, weights_out, base_ref, cache_ref, rec_vmem, target_ref, sems,
-    ):
+    def attend_kernel(scalars, q_ref, *refs):
+        pieces, refs = refs[: 1 if layer == 0 else 8], refs[1 if layer == 0 else 8 :]
+        targets_hbm, rec_ref, stale_ref, own_hbm, other_hbm, keep_out, send_out, weights_out = refs[:8]
+        base_ref, cache_ref, rec_vmem, target_ref, sems = refs[8:]
+        half = scalars[0]
         section = scalars[7]
         rec_copies = [
             pltpu.make_async_copy(
@@ -348,12 +351,14 @@
             copy.wait()
         for patch in range(4):
             rows = slice(PLEN * patch, PLEN * patch + PLEN)
-
-            @pl.when(patch <= section)
-            def _(patch=patch, rows=rows):
-                cache_ref[rows, :] = jnp.concatenate(
-                    [fresh_ref[2 * patch, 0:GROUP, :], fresh_ref[2 * patch + 1, 0:GROUP, :]], axis=0
-                )
+            if layer == 0:
+
+                @pl.when(patch <= section)
+                def _(patch=patch, rows=rows):
+                    fresh_ref = pieces[0]
+                    cache_ref[rows, :] = jnp.concatenate(
+                        [fresh_ref[2 * patch, 0:GROUP, :], fresh_ref[2 * patch + 1, 0:GROUP, :]], axis=0
+                    )
 
             if patch == 0:
                 continue
@@ -361,6 +366,15 @@
             @pl.when(patch > section)
             def _(rows=rows):
                 cache_ref[rows, :] = jnp.where(hit[rows], placed[rows], base_ref[rows, :].astype(F32)).astype(BF)
+
+        if layer > 0:
+            for back in range(4):
+
+                @pl.when(section >= back)
+                def _(back=back):
+                    for piece, at in ((pieces[2 * back], half), (pieces[2 * back + 1], 1 - half)):
+                        start = pl.multiple_of((section - back) * PLEN + at * GROUP, GROUP)
+                        cache_ref[pl.ds(start, GROUP), :] = piece[...]
 
         attend(scalars, q_ref, cache_ref, keep_out, send_out)
         for copy in weights:
@@ -375,26 +389,17 @@
     out_ref[...] = out.astype(BF)
 
 
-def residual_kernel_of(layer):
-    def residual_kernel(scalars, parts_ref, x_ref, mod_hbm, out_ref, mod_ref, sem):
-        fetch = pltpu.make_async_copy(mod_hbm.at[layer], mod_ref, sem)
-        fetch.start()
-        row = iota((8, 128), 0)
-        offset = (2 * (row >> 2) + scalars[0]) * 64 + 4 * scalars[10] + (row & 3)
-        text = (offset + scalars[6]) < TXT
-        chunks = [slice(128 * k, 128 * k + 128) for k in range(D // 128)]
-        totals = []
-        for lanes in chunks:
-            total = parts_ref[0, :, lanes].astype(F32)
-            for source in range(1, 8):
-                total = total + parts_ref[source, :, lanes].astype(F32)
-            totals.append(total)
-        fetch.wait()
-        for lanes, total in zip(chunks, totals):
-            gate = jnp.where(text, mod_ref[5:6, lanes], mod_ref[2:3, lanes])
-            out_ref[:, lanes] = (x_ref[:, lanes].astype(F32) + gate * total).astype(BF)
-
-    return residual_kernel
+def residual_kernel(scalars, parts_ref, x_ref, gates_ref, out_ref):
+    row = iota((8, 128), 0)
+    offset = (2 * (row >> 2) + scalars[0]) * 64 + 4 * scalars[10] + (row & 3)
+    text = (offset + scalars[6]) < TXT
+    for k in range(D // 128):
+        lanes = slice(128 * k, 128 * k + 128)
+        total = parts_ref[0, :, lanes].astype(F32)
+        for source in range(1, 8):
+            total = total + parts_ref[source, :, lanes].astype(F32)
+        gate = jnp.where(text, gates_ref[1:2, lanes], gates_ref[0:1, lanes])
+        out_ref[:, lanes] = (x_ref[:, lanes].astype(F32) + gate * total).astype(BF)
 
 
 def time_block(timestep, time_table):
@@ -506,6 +511,7 @@
     gain_row = jnp.pad(qk_gain[0].reshape(1, 128), ((0, 0), (0, 160)))
     rows = jnp.concatenate([summed, gain_row], axis=0)[None]
     everyone = ("section",) + ROW
+    rows, stale_all = lax.optimization_barrier((rows, stale_all))
     rows = lax.all_to_all(jnp.broadcast_to(rows, (lax.axis_size(everyone), 17, 288)), everyone, 0, 0)
     modulation = rows[:, :16].reshape(sections, 6, D)
     in_hbm = [pltpu.with_memory_space_constraint(value, pltpu.HBM) for value in (modulation, rows, tables)]
@@ -524,18 +530,29 @@
     )(scalars, gathered, *in_hbm, weights_qkv)
     targets = pltpu.with_memory_space_constraint(targets, pltpu.HBM)
 
+    def upwards(fresh):
+        pieces = [fresh, swapped(fresh, "half")]
+        for back in range(1, sections):
+            pairs = [(i, i + back) for i in range(sections - back)]
+            pieces.append(lax.ppermute(fresh, "section", pairs))
+            crossed = [(2 * a + h, 2 * b + 1 - h) for a, b in pairs for h in range(2)]
+            pieces.append(lax.ppermute(fresh, peers, crossed))
+        return pieces
+
     half_rows = shape_of((64, 256), BF)
     current, group, outs, first_fresh = tokens, gathered, [], None
     for layer in range(sections):
         packed = pltpu.with_memory_space_constraint(layers[layer], pltpu.HBM)
         if layer > 0:
             group = lax.all_gather(current, COL, axis=0, tiled=True)
-        queries, fresh, out_own = call(
+            group = pltpu.with_memory_space_constraint(group, pltpu.VMEM)
+        queries, fresh, out_own, gates = call(
             qkv_kernel_of(layer),
             (
                 shape_of((GROUP, 384), BF),
-                shape_of((copies, GROUP + (REC_GROUP if layer == 0 else 0), 384), BF),
+                shape_of((copies, GROUP + REC_GROUP, 384) if layer == 0 else (1, GROUP, 384), BF),
                 shape_of((192, D), BF),
+                shape_of((2, D), F32),
             ),
             [VMEM] * 2 + [HBM] * 4,
             "qkv",
@@ -543,12 +560,15 @@
             + small_scratch(GROUP),
         )(group, rec_fresh, *in_hbm, packed)
         out_other = swapped(out_own, "core")
-        fresh = lax.all_to_all(fresh, peers, 0, 0)
-        first_fresh = fresh if layer == 0 else first_fresh
+        if layer == 0:
+            first_fresh = lax.all_to_all(fresh, peers, 0, 0)
+            pieces = [first_fresh]
+        else:
+            pieces = upwards(fresh[0])
         keep, send, weights_out = call(
             attend_kernel_of(layer),
             (half_rows, half_rows, shape_of((2, 192, D), BF)),
-            [SMEM] + [VMEM] * 2 + [HBM] * 5,
+            [SMEM] + [VMEM] * (1 + len(pieces)) + [HBM] * 5,
             "attend",
             scratch=[
                 pltpu.VMEM((1024, 384), BF),
@@ -557,18 +577,14 @@
                 pltpu.VMEM((8, 128), jnp.int32),
                 pltpu.SemaphoreType.DMA((7,)),
             ],
-        )(scalars, queries, fresh, targets, first_fresh, stale_all, out_own, out_other)
+        )(scalars, queries, *pieces, targets, first_fresh, stale_all, out_own, out_other)
         projected = call(project_kernel, shape_of((64, D), BF), [VMEM] * 3, "project")(
             keep, swapped(send, "core"), weights_out
         )
         parts = lax.all_to_all(projected.reshape(8, 8, D), "z", 0, 0)
-        current = call(
-            residual_kernel_of(layer),
-            shape_of((8, D), BF),
-            [SMEM, VMEM, VMEM, HBM],
-            "residual",
-            scratch=[pltpu.VMEM((6, D), F32), pltpu.SemaphoreType.DMA],
-        )(scalars, parts, current, in_hbm[0])
+        current = call(residual_kernel, shape_of((8, D), BF), [SMEM, VMEM, VMEM, VMEM], "residual")(
+            scalars, parts, current, gates
+        )
         outs.append(current)
 
     leaving = jnp.stack(outs).reshape(sections * 2, 4, D)

time: 419 us -> 396 us (0.945)
  starting transfers between devices: 20.5 us -> 64.1 us
  blocking collectives: 248 us -> 214 us
  waiting for transfers between devices: 57.5 us -> 37.5 us
  local copies, waits for them, and re-layouts: 22.9 us -> 15 us
  Pallas kernels: 51.6 us -> 46.8 us
    ppermute x0 -> x18, starting transfers between devices: none -> 45.8 us  [the longest x9 26.5 us: upwards(): pieces.append(lax.ppermute(fresh, 'section', pairs))]
    all_to_all x3 -> x1, blocking collectives: 58 us -> 25.3 us  [local(): lax.all_to_all(jnp.broadcast_to(rows, (lax.axis_size(everyone), 17, 288))...]
    all_to_all x2 -> x1, waiting for transfers between devices: 34.7 us -> 17.4 us  [local(): first_fresh = lax.all_to_all(fresh, peers, 0, 0)]
    all_to_all x1, waiting for transfers between devices: 16 us -> 0.09 us  [local(): lax.all_to_all(jnp.broadcast_to(stale_share, (copies, STALE, 384)), peers...]
    ppermute x0 -> x18, waiting for transfers between devices: none -> 10.2 us  [the longest x9 7.47 us: upwards(): pieces.append(lax.ppermute(fresh, 'section', pairs))]
    all_to_all x2 -> x1, starting transfers between devices: 10.1 us -> 4.79 us  [local(): first_fresh = lax.all_to_all(fresh, peers, 0, 0)]
    all_gather x3, blocking collectives: 55.1 us -> 50.7 us  [local(): group = lax.all_gather(current, COL, axis=0, tiled=True)]
    unnamed x34 -> x32, local copies, waits for them, and re-layouts: 7.52 us -> 3.18 us
  transfers between devices with their start and end apart: 17 -> 37, of which waited for: 7 -> 13; matrix products, arithmetic and copies ran while one was open for 4% -> 3% of each run, Pallas kernels for 9% -> 9%
where the time goes in v3:
time: 396 us; the launch traced here: 394 us
  blocking collectives  214 us (54%)
  starting transfers between devices  64.1 us (16%)
  Pallas kernels  46.8 us (12%)
  waiting for transfers between devices  37.5 us (9%)
  between operations  16.3 us (4%)
  local copies, waits for them, and re-layouts  15 us (4%)
    all_to_all x4, blocking collectives, local(): parts = lax.all_to_all(projected.reshape(8, 8, D), 'z', 0, 0)  79.4 us
    all_gather x3, blocking collectives, local(): group = lax.all_gather(current, COL, axis=0, tiled=True)  50.7 us
    ppermute x9, starting transfers between devices, upwards(): pieces.append(lax.ppermute(fresh, 'section', pairs))  26.5 us
    all_to_all x1, blocking collectives, local(): lax.all_to_all(jnp.broadcast_to(rows, (lax.axis_size(everyone), 17, 288))...  25.3 us
    pallas_call x4, Pallas kernels, local(): call(qkv_kernel_of(layer), (shape_of((GROUP, 384), BF), shape_of((copies,...  23.6 us
    all_gather x1, blocking collectives, local(): gathered = lax.all_gather(payload, COL, axis=0, tiled=True)  22.8 us
    all_to_all x1, blocking collectives, local(): chunks = lax.all_to_all(packed, 'section', 0, 0)  20.8 us
    ppermute x9, starting transfers between devices, upwards(): pieces.append(lax.ppermute(fresh, peers, crossed))  19.3 us
  transfers between devices with their start and end apart: 37, of which 13 were waited for; matrix products, arithmetic and copies ran while one was open for 3% of the time, Pallas kernels for 9%

profile of v3, /device:TPU:2, one launch (start us, length us, event | category | flops | bytes accessed | tf_op | source)
XLA Modules:
  0.0 394.4 jit_solution(17736992835455404721)
XLA Ops:
  6.5 1.6 pack.1
  8.1 20.8 %all_to_all.45 = bf16[4,384,384]{2,1,0:T(8,128)(2,1)S(1)} all-to-all(bf16[4,384,384]{2,1,0:T(8,128)(2,1)S(1)} %pack.1), channel_id=1, replica_groups=mesh['section'=4,'req'=2,'half'=2,'z'=8,'core'=2] {'section'}, dimensions={0} | all-to-all | bytes 2359296 | tf_op jit(solution)/shard_map/all_to_all | solution.py:449
  32.4 2.2 collective-permute-start
  34.6 1.4 collective-permute-start.1
  36.0 1.7 constant_dynamic-slice_fusion
  38.8 1.6 broadcast_in_dim.47
  40.4 4.9 %all-to-all-start = ((bf16[8,384,384]{2,1,0:T(8,128)(2,1)}), bf16[8,384,384]{2,1,0:T(8,128)(2,1)}, u32[]{:S(2)}, u32[]{:S(2)}) async-start(bf16[8,384,384]{2,1,0:T(8,128)(2,1)} %broadcast_in_dim.47), calls=%async_computation | async-start | bytes 4718592 | tf_op jit(solution)/shard_map/all_to_all | solution.py:457
  50.5 1.5 concatenate.25.scalars
  54.2 22.8 %all_gather.24.gathered_ref.x_ref = bf16[128,3968]{1,0:T(8,128)(2,1)S(1)} all-gather(bf16[8,3968]{1,0:T(8,128)(2,1)S(1)} %fusion.1), channel_id=1, replica_groups=mesh['section'=4,'req'=2,'half'=2,'z'=8,'core'=2] {'z','core'}, dimensions={0}, use_global_device_ids=true | all-gather | bytes 1079296 | tf_op jit(solution)/shard_map/all_gather | solution.py:508
  77.3 25.3 %all_to_all.46.rows_hbm = f32[16,17,288]{2,1,0:T(8,128)S(1)} all-to-all(f32[16,17,288]{2,1,0:T(8,128)S(1)} %broadcast_in_dim.49), channel_id=1, replica_groups=mesh['section'=4,'req'=2,'half'=2,'z'=8,'core'=2] {'section','req','half'}, dimensions={0} | all-to-all | bytes 626688 | tf_op jit(solution)/shard_map/all_to_all | solution.py:515
  103.7 4.6 %rec.1.rec_ref = bf16[1,32,384]{2,1,0:T(8,128)(2,1)S(1)} custom-call(s32[16]{0:T(128)S(1)} %concatenate.25.scalars, bf16[128,3968]{1,0:T(8,128)(2,1)S(1)} %all_gather.24.gathered_ref.x_ref, f32[4,6,3072]{2,1,0:T(8,128)} %reshape.69.mod_hbm, f32[16,17,288]{2,1,0:T(8,128)} %copy-done.8, f32[3,160,128]{2,1,0:T(8,128)} %copy-done.2, bf16[576,3072]{1,0:T(8,128)(2,1)} %bitcast.108), custom_call_target="tpu_custom_call" | custom-call | tf_op jit(solution)/shard_map/rec/pallas_call | solution.py:518
  108.3 2.3 all-gather.5.cloned.1.call-done.packed_ref
  110.6 5.9 %qkv.4 = (bf16[128,384]{1,0:T(8,128)(2,1)S(1)}, bf16[8,160,384]{2,1,0:T(8,128)(2,1)S(1)}, bf16[192,3072]{1,0:T(8,128)(2,1)S(1)}, f32[2,3072]{1,0:T(2,128)S(1)}) custom-call(bf16[128,3968]{1,0:T(8,128)(2,1)S(1)} %all_gather.24.gathered_ref.x_ref, bf16[1,32,384]{2,1,0:T(8,128)(2,1)S(1)} %rec.1.rec_ref, f32[4,6,3072]{2,1,0:T(8,128)} %reshape.69.mod_hbm, ...), custom_call_target="tpu_custom_call" | custom-call | tf_op jit(solution)/shard_map/qkv/pallas_call | solution.py:549
  118.1 4.8 %all-to-all-start.3 = ((bf16[8,160,384]{2,1,0:T(8,128)(2,1)}), bf16[8,160,384]{2,1,0:T(8,128)(2,1)S(1)}, u32[]{:S(2)}, u32[]{:S(2)}) async-start(bf16[8,160,384]{2,1,0:T(8,128)(2,1)} %copy-done.3), calls=%async_computation.3 | async-start | bytes 1966080 | tf_op jit(solution)/shard_map/all_to_all | solution.py:564
  123.0 17.4 %all-to-all-done.3.refs_0_.refs_2_.refs_9_ = bf16[8,160,384]{2,1,0:T(8,128)(2,1)S(1)} async-done(((bf16[8,160,384]{2,1,0:T(8,128)(2,1)}), bf16[8,160,384]{2,1,0:T(8,128)(2,1)S(1)}, u32[]{:S(2)}, u32[]{:S(2)}) %all-to-all-start.3) | async-done | bytes 983072 | tf_op jit(solution)/shard_map/all_to_all | solution.py:564
  140.9 2.8 attend.4
  145.6 21.9 %all_to_all.47.parts_ref = bf16[8,8,3072]{2,1,0:T(8,128)(2,1)S(1)} all-to-all(bf16[8,8,3072]{2,1,0:T(8,128)(2,1)S(1)} %bitcast.74), channel_id=1, replica_groups=mesh['section'=4,'req'=2,'half'=2,'z'=8,'core'=2] {'z'}, dimensions={0} | all-to-all | bytes 786432 | tf_op jit(solution)/shard_map/all_to_all | solution.py:584
  168.1 17.0 %all_gather.26.x_ref = bf16[128,3072]{1,0:T(8,128)(2,1)S(1)} all-gather(bf16[8,3072]{1,0:T(8,128)(2,1)S(1)} %residual.4.x_ref), channel_id=1, replica_groups=mesh['section'=4,'req'=2,'half'=2,'z'=8,'core'=2] {'z','core'}, dimensions={0}, use_global_device_ids=true | all-gather | bytes 835584 | tf_op jit(solution)/shard_map/all_gather | solution.py:547
  185.1 5.9 %qkv.5 = (bf16[128,384]{1,0:T(8,128)(2,1)S(1)}, bf16[1,128,384]{2,1,0:T(8,128)(2,1)S(1)}, bf16[192,3072]{1,0:T(8,128)(2,1)S(1)}, f32[2,3072]{1,0:T(2,128)S(1)}) custom-call(bf16[128,3072]{1,0:T(8,128)(2,1)S(1)} %all_gather.26.x_ref, bf16[1,32,384]{2,1,0:T(8,128)(2,1)S(1)} %rec.1.rec_ref, f32[4,6,3072]{2,1,0:T(8,128)} %reshape.69.mod_hbm, ...), custom_call_target="tpu_custom_call" | custom-call | tf_op jit(solution)/shard_map/qkv/pallas_call | solution.py:549
  191.5 3.9 collective-permute-start.10
  196.9 1.7 collective-permute-start.6
  198.6 1.4 collective-permute-done.10.refs_7_
  200.0 2.6 collective-permute-start.7
  202.6 1.3 collective-permute-done.4.refs_1_
  205.3 2.8 collective-permute-start.9
  208.1 3.4 collective-permute-done.9.refs_6_
  211.5 2.8 attend.5
  216.2 19.3 %all_to_all.48.parts_ref = bf16[8,8,3072]{2,1,0:T(8,128)(2,1)S(1)} all-to-all(bf16[8,8,3072]{2,1,0:T(8,128)(2,1)S(1)} %bitcast.75), channel_id=1, replica_groups=mesh['section'=4,'req'=2,'half'=2,'z'=8,'core'=2] {'z'}, dimensions={0} | all-to-all | bytes 786432 | tf_op jit(solution)/shard_map/all_to_all | solution.py:584
  236.2 16.8 %all_gather.28.x_ref = bf16[128,3072]{1,0:T(8,128)(2,1)S(1)} all-gather(bf16[8,3072]{1,0:T(8,128)(2,1)S(1)} %residual.5.x_ref), channel_id=1, replica_groups=mesh['section'=4,'req'=2,'half'=2,'z'=8,'core'=2] {'z','core'}, dimensions={0}, use_global_device_ids=true | all-gather | bytes 835584 | tf_op jit(solution)/shard_map/all_gather | solution.py:547
  253.0 5.9 %qkv.6 = (bf16[128,384]{1,0:T(8,128)(2,1)S(1)}, bf16[1,128,384]{2,1,0:T(8,128)(2,1)S(1)}, bf16[192,3072]{1,0:T(8,128)(2,1)S(1)}, f32[2,3072]{1,0:T(2,128)S(1)}) custom-call(bf16[128,3072]{1,0:T(8,128)(2,1)S(1)} %all_gather.28.x_ref, bf16[1,32,384]{2,1,0:T(8,128)(2,1)S(1)} %rec.1.rec_ref, f32[4,6,3072]{2,1,0:T(8,128)} %reshape.69.mod_hbm, ...), custom_call_target="tpu_custom_call" | custom-call | tf_op jit(solution)/shard_map/qkv/pallas_call | solution.py:549
  261.9 4.4 %collective-permute-start.15 = (bf16[128,384]{1,0:T(8,128)(2,1)S(1)}, bf16[128,384]{1,0:T(8,128)(2,1)S(1)}, u32[]{:S(2)}, u32[]{:S(2)}) collective-permute-start(bf16[128,384]{1,0:T(8,128)(2,1)S(1)} %bitcast.101), channel_id=1, source_target_pairs={{0,80},{16,64},{64,144},{80,128},{128,208},{144,192},{1,81},{17,65... | collective-permute-start | bytes 294920 | tf_op jit(solution)/shard_map/ppermute | solution.py:539
  266.4 5.2 %collective-permute-start.16 = (bf16[128,384]{1,0:T(8,128)(2,1)S(1)}, bf16[128,384]{1,0:T(8,128)(2,1)S(1)}, u32[]{:S(2)}, u32[]{:S(2)}) collective-permute-start(bf16[128,384]{1,0:T(8,128)(2,1)S(1)} %bitcast.102), channel_id=1, source_target_pairs={{0,128},{64,192},{1,129},{65,193},{2,130},{66,194},{3,131},{67,195... | collective-permute-start | bytes 294920 | tf_op jit(solution)/shard_map/ppermute | solution.py:537
  271.6 1.6 collective-permute-start.17
  273.1 3.0 collective-permute-start.18
  276.2 1.3 collective-permute-start.19
  278.4 1.3 collective-permute-done.19.refs_7_
  279.7 2.8 attend.6
  284.6 19.5 %all_to_all.49.parts_ref = bf16[8,8,3072]{2,1,0:T(8,128)(2,1)S(1)} all-to-all(bf16[8,8,3072]{2,1,0:T(8,128)(2,1)S(1)} %bitcast.76), channel_id=1, replica_groups=mesh['section'=4,'req'=2,'half'=2,'z'=8,'core'=2] {'z'}, dimensions={0} | all-to-all | bytes 786432 | tf_op jit(solution)/shard_map/all_to_all | solution.py:584
  304.7 16.8 %all_gather.30.x_ref = bf16[128,3072]{1,0:T(8,128)(2,1)S(1)} all-gather(bf16[8,3072]{1,0:T(8,128)(2,1)S(1)} %residual.6.x_ref), channel_id=1, replica_groups=mesh['section'=4,'req'=2,'half'=2,'z'=8,'core'=2] {'z','core'}, dimensions={0}, use_global_device_ids=true | all-gather | bytes 835584 | tf_op jit(solution)/shard_map/all_gather | solution.py:547
  321.5 5.9 %qkv.7 = (bf16[128,384]{1,0:T(8,128)(2,1)S(1)}, bf16[1,128,384]{2,1,0:T(8,128)(2,1)S(1)}, bf16[192,3072]{1,0:T(8,128)(2,1)S(1)}, f32[2,3072]{1,0:T(2,128)S(1)}) custom-call(bf16[128,3072]{1,0:T(8,128)(2,1)S(1)} %all_gather.30.x_ref, bf16[1,32,384]{2,1,0:T(8,128)(2,1)S(1)} %rec.1.rec_ref, f32[4,6,3072]{2,1,0:T(8,128)} %reshape.69.mod_hbm, ...), custom_call_target="tpu_custom_call" | custom-call | tf_op jit(solution)/shard_map/qkv/pallas_call | solution.py:549
  327.9 1.5 collective-permute-start.22
  330.7 2.0 collective-permute-start.24
  332.6 7.8 %collective-permute-start.25 = (bf16[128,384]{1,0:T(8,128)(2,1)S(1)}, bf16[128,384]{1,0:T(8,128)(2,1)S(1)}, u32[]{:S(2)}, u32[]{:S(2)}) collective-permute-start(bf16[128,384]{1,0:T(8,128)(2,1)S(1)} %bitcast.86), channel_id=1, source_target_pairs={{0,128},{64,192},{1,129},{65,193},{2,130},{66,194},{3,131},{67,195... | collective-permute-start | bytes 294920 | tf_op jit(solution)/shard_map/ppermute | solution.py:537
  340.4 1.9 collective-permute-start.26
  345.0 3.2 collective-permute-done.27.refs_6_
  348.2 2.8 attend.7
  352.9 18.7 %all_to_all.50.parts_ref = bf16[8,8,3072]{2,1,0:T(8,128)(2,1)S(1)} all-to-all(bf16[8,8,3072]{2,1,0:T(8,128)(2,1)S(1)} %bitcast.77), channel_id=1, replica_groups=mesh['section'=4,'req'=2,'half'=2,'z'=8,'core'=2] {'z'}, dimensions={0} | all-to-all | bytes 786432 | tf_op jit(solution)/shard_map/all_to_all | solution.py:584
  372.4 14.7 %all_to_all.51 = bf16[8,4,3072]{2,1,0:T(4,128)(2,1)S(1)} all-to-all(bf16[8,4,3072]{2,1,0:T(4,128)(2,1)S(1)} %reshape.74), channel_id=1, replica_groups=mesh['section'=4,'req'=2,'half'=2,'z'=8,'core'=2] {'section','req'}, dimensions={0} | all-to-all | bytes 393216 | tf_op jit(solution)/shard_map/all_to_all | solution.py:591
  (137 shorter events, 35.6 us)
Async XLA Ops:
  6.5 42.4 %copy-start = (f32[1000,512]{1,0:T(8,128)S(1)}, f32[1000,512]{1,0:T(8,128)}, u32[]{:S(2)}) copy-start(f32[1000,512]{1,0:T(8,128)} %param.15) | copy-start | bytes 6144004
  6.5 104.1 %all-gather.5.cloned.1.call-start = ((), (), s32[]{:S(2)}) async-start(), calls=%async_computation.9 | async-start | bytes 5013504 | tf_op jit(solution)/shard_map/all_gather | solution.py:451
  28.9 5.7 %copy-start.9 = (bf16[1,1,2,3072]{3,2,1,0:T(2,128)(2,1)S(1)}, bf16[1,1,2,3072]{3,2,1,0:T(2,128)(2,1)}, u32[]{:S(2)}) copy-start(bf16[1,1,2,3072]{3,2,1,0:T(2,128)(2,1)} %param.21) | copy-start | bytes 36868
  30.0 155.1 %all-gather.7.cloned.1.call-start = ((), (), s32[]{:S(2)}) async-start(), calls=%async_computation.10 | async-start | bytes 5013504 | tf_op jit(solution)/shard_map/all_gather | solution.py:451
  30.8 222.2 %all-gather.9.cloned.1.call-start = ((), (), s32[]{:S(2)}) async-start(), calls=%async_computation.11 | async-start | bytes 5013504 | tf_op jit(solution)/shard_map/all_gather | solution.py:451
  32.4 21.7 %collective-permute-start = (bf16[4,2,3072]{2,0,1:T(4,128)(2,1)S(1)}, bf16[4,2,3072]{2,0,1:T(4,128)(2,1)S(1)}, u32[]{:S(2)}, u32[]{:S(2)}) collective-permute-start(bf16[4,2,3072]{2,0,1:T(4,128)(2,1)S(1)} %bitcast.112), channel_id=1, source_target_pairs={{0,32},{32,0},{1,33},{33,1},{2,34},{34,2},{3,35},{35,3},{4,36},{36... | collective-permute-start | bytes 147464 | tf_op jit(solution)/shard_map/ppermute | solution.py:410
  34.6 19.4 %collective-permute-start.1 = (bf16[1,2,3072]{2,1,0:T(2,128)(2,1)S(1)}, bf16[1,2,3072]{2,1,0:T(2,128)(2,1)S(1)}, u32[]{:S(2)}, u32[]{:S(2)}) collective-permute-start(bf16[1,2,3072]{2,1,0:T(2,128)(2,1)S(1)} %bitcast.116), channel_id=1, source_target_pairs={{0,32},{32,0},{1,33},{33,1},{2,34},{34,2},{3,35},{35,3},{4,36},{36... | collective-permute-start | bytes 36872 | tf_op jit(solution)/shard_map/ppermute | solution.py:410
  40.4 5.6 %copy-start.13 = (s32[2,64]{1,0:T(2,128)S(1)}, s32[2,64]{1,0:T(2,128)}, u32[]{:S(2)}) copy-start(s32[2,64]{1,0:T(2,128)} %param.22) | copy-start | bytes 1540
  40.4 6.1 %copy-start.12 = (s32[2,4]{1,0:T(2,128)S(1)}, s32[2,4]{1,0:T(2,128)}, u32[]{:S(2)}) copy-start(s32[2,4]{1,0:T(2,128)} %param.13) | copy-start | bytes 100
  40.4 11.7 %copy-start.4 = (bf16[1,512,288]{1,2,0:T(8,128)(2,1)S(1)}, bf16[1,512,288]{1,2,0:T(8,128)(2,1)}, u32[]{:S(2)}) copy-start(bf16[1,512,288]{1,2,0:T(8,128)(2,1)} %param.16) | copy-start | bytes 884740
  40.4 11.7 %copy-start.7 = (f32[1,128]{1,0:T(1,128)S(1)}, f32[1,128]{1,0:T(1,128)}, u32[]{:S(2)}) copy-start(f32[1,128]{1,0:T(1,128)} %constant.86.clone.rate_ref) | copy-start | bytes 1540
  40.4 13.5 %copy-start.14 = (f32[1,2,64]{2,1,0:T(2,128)S(1)}, f32[1,2,64]{2,1,0:T(2,128)}, u32[]{:S(2)}) copy-start(f32[1,2,64]{2,1,0:T(2,128)} %param.19) | copy-start | bytes 1540
  40.4 36.9 %all-to-all-start = ((bf16[8,384,384]{2,1,0:T(8,128)(2,1)}), bf16[8,384,384]{2,1,0:T(8,128)(2,1)}, u32[]{:S(2)}, u32[]{:S(2)}) async-start(bf16[8,384,384]{2,1,0:T(8,128)(2,1)} %broadcast_in_dim.47), calls=%async_computation | async-start | bytes 4718592 | tf_op jit(solution)/shard_map/all_to_all | solution.py:457
  45.3 276.2 %all-gather.11.cloned.1.call-start = ((), (), s32[]{:S(2)}) async-start(), calls=%async_computation.12 | async-start | bytes 5013504 | tf_op jit(solution)/shard_map/all_gather | solution.py:451
  46.5 5.6 %copy-start.10 = (s32[32]{0:T(128)}, s32[32]{0:T(128)S(1)}, u32[]{:S(2)}) copy-start(s32[32]{0:T(128)S(1)} %reshape.67) | copy-start | bytes 388
  117.1 5.8 %copy-start.11 = (s32[32]{0:T(128)S(1)}, s32[32]{0:T(128)}, u32[]{:S(2)}) copy-start(s32[32]{0:T(128)} %copy-done.10) | copy-start | bytes 388
  117.1 23.2 %collective-permute-start.2 = (bf16[192,3072]{1,0:T(8,128)(2,1)S(1)}, bf16[192,3072]{1,0:T(8,128)(2,1)S(1)}, u32[]{:S(2)}, u32[]{:S(2)}) collective-permute-start(bf16[192,3072]{1,0:T(8,128)(2,1)S(1)} %get-tuple-element.43.refs_4_), channel_id=1, source_target_pairs={{0,1},{1,0},{2,3},{3,2},{4,5},{5,4},{6,7},{7,6},{8,9},{9,8},{10,11... | collective-permute-start | bytes 3538952 | tf_op jit(solution)/shard_map/ppermute | solution.py:410
  118.1 22.2 %all-to-all-start.3 = ((bf16[8,160,384]{2,1,0:T(8,128)(2,1)}), bf16[8,160,384]{2,1,0:T(8,128)(2,1)S(1)}, u32[]{:S(2)}, u32[]{:S(2)}) async-start(bf16[8,160,384]{2,1,0:T(8,128)(2,1)} %copy-done.3), calls=%async_computation.3 | async-start | bytes 1966080 | tf_op jit(solution)/shard_map/all_to_all | solution.py:564
  143.7 1.3 collective-permute-start.3
  145.0 22.5 %copy-start.6 = (f32[2,3072]{1,0:T(2,128)S(1)}, f32[2,3072]{1,0:T(2,128)}, u32[]{:S(2)}) copy-start(f32[2,3072]{1,0:T(2,128)} %copy-done.5) | copy-start | bytes 73732
  191.0 20.5 %collective-permute-start.11 = (bf16[192,3072]{1,0:T(8,128)(2,1)S(1)}, bf16[192,3072]{1,0:T(8,128)(2,1)S(1)}, u32[]{:S(2)}, u32[]{:S(2)}) collective-permute-start(bf16[192,3072]{1,0:T(8,128)(2,1)S(1)} %get-tuple-element.50.refs_11_), channel_id=1, source_target_pairs={{0,1},{1,0},{2,3},{3,2},{4,5},{5,4},{6,7},{7,6},{8,9},{9,8},{10,11... | collective-permute-start | bytes 3538952 | tf_op jit(solution)/shard_map/ppermute | solution.py:410
  191.5 8.6 %collective-permute-start.10 = (bf16[128,384]{1,0:T(8,128)(2,1)S(1)}, bf16[128,384]{1,0:T(8,128)(2,1)S(1)}, u32[]{:S(2)}, u32[]{:S(2)}) collective-permute-start(bf16[128,384]{1,0:T(8,128)(2,1)S(1)} %bitcast.91), channel_id=1, source_target_pairs={{0,208},{16,192},{1,209},{17,193},{2,210},{18,194},{3,211},{19,195... | collective-permute-start | bytes 294920 | tf_op jit(solution)/shard_map/ppermute | solution.py:539
  195.4 8.6 %collective-permute-start.4 = (bf16[128,384]{1,0:T(8,128)(2,1)S(1)}, bf16[128,384]{1,0:T(8,128)(2,1)S(1)}, u32[]{:S(2)}, u32[]{:S(2)}) collective-permute-start(bf16[128,384]{1,0:T(8,128)(2,1)S(1)} %bitcast.92), channel_id=1, source_target_pairs={{0,16},{16,0},{1,17},{17,1},{2,18},{18,2},{3,19},{19,3},{4,20},{20... | collective-permute-start | bytes 294920 | tf_op jit(solution)/shard_map/ppermute | solution.py:410
  195.7 9.6 %collective-permute-start.5 = (bf16[128,384]{1,0:T(8,128)(2,1)S(1)}, bf16[128,384]{1,0:T(8,128)(2,1)S(1)}, u32[]{:S(2)}, u32[]{:S(2)}) collective-permute-start(bf16[128,384]{1,0:T(8,128)(2,1)S(1)} %bitcast.93), channel_id=1, source_target_pairs={{0,64},{64,128},{128,192},{1,65},{65,129},{129,193},{2,66},{66,130... | collective-permute-start | bytes 294920 | tf_op jit(solution)/shard_map/ppermute | solution.py:537
  196.9 11.2 %collective-permute-start.6 = (bf16[128,384]{1,0:T(8,128)(2,1)S(1)}, bf16[128,384]{1,0:T(8,128)(2,1)S(1)}, u32[]{:S(2)}, u32[]{:S(2)}) collective-permute-start(bf16[128,384]{1,0:T(8,128)(2,1)S(1)} %bitcast.94), channel_id=1, source_target_pairs={{0,80},{16,64},{64,144},{80,128},{128,208},{144,192},{1,81},{17,65... | collective-permute-start | bytes 294920 | tf_op jit(solution)/shard_map/ppermute | solution.py:539
  200.0 8.1 %collective-permute-start.7 = (bf16[128,384]{1,0:T(8,128)(2,1)S(1)}, bf16[128,384]{1,0:T(8,128)(2,1)S(1)}, u32[]{:S(2)}, u32[]{:S(2)}) collective-permute-start(bf16[128,384]{1,0:T(8,128)(2,1)S(1)} %bitcast.95), channel_id=1, source_target_pairs={{0,128},{64,192},{1,129},{65,193},{2,130},{66,194},{3,131},{67,195... | collective-permute-start | bytes 294920 | tf_op jit(solution)/shard_map/ppermute | solution.py:537
  204.0 4.2 %collective-permute-start.8 = (bf16[128,384]{1,0:T(8,128)(2,1)S(1)}, bf16[128,384]{1,0:T(8,128)(2,1)S(1)}, u32[]{:S(2)}, u32[]{:S(2)}) collective-permute-start(bf16[128,384]{1,0:T(8,128)(2,1)S(1)} %bitcast.96), channel_id=1, source_target_pairs={{0,144},{16,128},{64,208},{80,192},{1,145},{17,129},{65,209},{81,1... | collective-permute-start | bytes 294920 | tf_op jit(solution)/shard_map/ppermute | solution.py:539
  205.3 6.2 %collective-permute-start.9 = (bf16[128,384]{1,0:T(8,128)(2,1)S(1)}, bf16[128,384]{1,0:T(8,128)(2,1)S(1)}, u32[]{:S(2)}, u32[]{:S(2)}) collective-permute-start(bf16[128,384]{1,0:T(8,128)(2,1)S(1)} %bitcast.97), channel_id=1, source_target_pairs={{0,192},{1,193},{2,194},{3,195},{4,196},{5,197},{6,198},{7,199},{8... | collective-permute-start | bytes 294920 | tf_op jit(solution)/shard_map/ppermute | solution.py:537
  214.3 1.3 collective-permute-start.12
  258.9 20.8 %collective-permute-start.20 = (bf16[192,3072]{1,0:T(8,128)(2,1)S(1)}, bf16[192,3072]{1,0:T(8,128)(2,1)S(1)}, u32[]{:S(2)}, u32[]{:S(2)}) collective-permute-start(bf16[192,3072]{1,0:T(8,128)(2,1)S(1)} %get-tuple-element.57.refs_11_), channel_id=1, source_target_pairs={{0,1},{1,0},{2,3},{3,2},{4,5},{5,4},{6,7},{7,6},{8,9},{9,8},{10,11... | collective-permute-start | bytes 3538952 | tf_op jit(solution)/shard_map/ppermute | solution.py:410
  259.4 12.2 %collective-permute-start.13 = (bf16[128,384]{1,0:T(8,128)(2,1)S(1)}, bf16[128,384]{1,0:T(8,128)(2,1)S(1)}, u32[]{:S(2)}, u32[]{:S(2)}) collective-permute-start(bf16[128,384]{1,0:T(8,128)(2,1)S(1)} %bitcast.99), channel_id=1, source_target_pairs={{0,16},{16,0},{1,17},{17,1},{2,18},{18,2},{3,19},{19,3},{4,20},{20... | collective-permute-start | bytes 294920 | tf_op jit(solution)/shard_map/ppermute | solution.py:410
  260.6 12.5 %collective-permute-start.14 = (bf16[128,384]{1,0:T(8,128)(2,1)S(1)}, bf16[128,384]{1,0:T(8,128)(2,1)S(1)}, u32[]{:S(2)}, u32[]{:S(2)}) collective-permute-start(bf16[128,384]{1,0:T(8,128)(2,1)S(1)} %bitcast.100), channel_id=1, source_target_pairs={{0,64},{64,128},{128,192},{1,65},{65,129},{129,193},{2,66},{66,130... | collective-permute-start | bytes 294920 | tf_op jit(solution)/shard_map/ppermute | solution.py:537
  261.9 14.2 %collective-permute-start.15 = (bf16[128,384]{1,0:T(8,128)(2,1)S(1)}, bf16[128,384]{1,0:T(8,128)(2,1)S(1)}, u32[]{:S(2)}, u32[]{:S(2)}) collective-permute-start(bf16[128,384]{1,0:T(8,128)(2,1)S(1)} %bitcast.101), channel_id=1, source_target_pairs={{0,80},{16,64},{64,144},{80,128},{128,208},{144,192},{1,81},{17,65... | collective-permute-start | bytes 294920 | tf_op jit(solution)/shard_map/ppermute | solution.py:539
  266.4 11.1 %collective-permute-start.16 = (bf16[128,384]{1,0:T(8,128)(2,1)S(1)}, bf16[128,384]{1,0:T(8,128)(2,1)S(1)}, u32[]{:S(2)}, u32[]{:S(2)}) collective-permute-start(bf16[128,384]{1,0:T(8,128)(2,1)S(1)} %bitcast.102), channel_id=1, source_target_pairs={{0,128},{64,192},{1,129},{65,193},{2,130},{66,194},{3,131},{67,195... | collective-permute-start | bytes 294920 | tf_op jit(solution)/shard_map/ppermute | solution.py:537
  271.6 5.9 %collective-permute-start.17 = (bf16[128,384]{1,0:T(8,128)(2,1)S(1)}, bf16[128,384]{1,0:T(8,128)(2,1)S(1)}, u32[]{:S(2)}, u32[]{:S(2)}) collective-permute-start(bf16[128,384]{1,0:T(8,128)(2,1)S(1)} %bitcast.103), channel_id=1, source_target_pairs={{0,144},{16,128},{64,208},{80,192},{1,145},{17,129},{65,209},{81,1... | collective-permute-start | bytes 294920 | tf_op jit(solution)/shard_map/ppermute | solution.py:539
  273.1 5.2 %collective-permute-start.18 = (bf16[128,384]{1,0:T(8,128)(2,1)S(1)}, bf16[128,384]{1,0:T(8,128)(2,1)S(1)}, u32[]{:S(2)}, u32[]{:S(2)}) collective-permute-start(bf16[128,384]{1,0:T(8,128)(2,1)S(1)} %bitcast.104), channel_id=1, source_target_pairs={{0,192},{1,193},{2,194},{3,195},{4,196},{5,197},{6,198},{7,199},{8... | collective-permute-start | bytes 294920 | tf_op jit(solution)/shard_map/ppermute | solution.py:537
  276.2 3.5 collective-permute-start.19
  282.5 1.5 collective-permute-start.21
  327.5 20.7 %collective-permute-start.29 = (bf16[192,3072]{1,0:T(8,128)(2,1)S(1)}, bf16[192,3072]{1,0:T(8,128)(2,1)S(1)}, u32[]{:S(2)}, u32[]{:S(2)}) collective-permute-start(bf16[192,3072]{1,0:T(8,128)(2,1)S(1)} %get-tuple-element.64.refs_11_), channel_id=1, source_target_pairs={{0,1},{1,0},{2,3},{3,2},{4,5},{5,4},{6,7},{7,6},{8,9},{9,8},{10,11... | collective-permute-start | bytes 3538952 | tf_op jit(solution)/shard_map/ppermute | solution.py:410
  327.9 12.5 %collective-permute-start.22 = (bf16[128,384]{1,0:T(8,128)(2,1)S(1)}, bf16[128,384]{1,0:T(8,128)(2,1)S(1)}, u32[]{:S(2)}, u32[]{:S(2)}) collective-permute-start(bf16[128,384]{1,0:T(8,128)(2,1)S(1)} %bitcast.83), channel_id=1, source_target_pairs={{0,16},{16,0},{1,17},{17,1},{2,18},{18,2},{3,19},{19,3},{4,20},{20... | collective-permute-start | bytes 294920 | tf_op jit(solution)/shard_map/ppermute | solution.py:410
  329.4 13.0 %collective-permute-start.23 = (bf16[128,384]{1,0:T(8,128)(2,1)S(1)}, bf16[128,384]{1,0:T(8,128)(2,1)S(1)}, u32[]{:S(2)}, u32[]{:S(2)}) collective-permute-start(bf16[128,384]{1,0:T(8,128)(2,1)S(1)} %bitcast.84), channel_id=1, source_target_pairs={{0,64},{64,128},{128,192},{1,65},{65,129},{129,193},{2,66},{66,130... | collective-permute-start | bytes 294920 | tf_op jit(solution)/shard_map/ppermute | solution.py:537
  330.7 13.0 %collective-permute-start.24 = (bf16[128,384]{1,0:T(8,128)(2,1)S(1)}, bf16[128,384]{1,0:T(8,128)(2,1)S(1)}, u32[]{:S(2)}, u32[]{:S(2)}) collective-permute-start(bf16[128,384]{1,0:T(8,128)(2,1)S(1)} %bitcast.85), channel_id=1, source_target_pairs={{0,80},{16,64},{64,144},{80,128},{128,208},{144,192},{1,81},{17,65... | collective-permute-start | bytes 294920 | tf_op jit(solution)/shard_map/ppermute | solution.py:539
  332.6 12.3 %collective-permute-start.25 = (bf16[128,384]{1,0:T(8,128)(2,1)S(1)}, bf16[128,384]{1,0:T(8,128)(2,1)S(1)}, u32[]{:S(2)}, u32[]{:S(2)}) collective-permute-start(bf16[128,384]{1,0:T(8,128)(2,1)S(1)} %bitcast.86), channel_id=1, source_target_pairs={{0,128},{64,192},{1,129},{65,193},{2,130},{66,194},{3,131},{67,195... | collective-permute-start | bytes 294920 | tf_op jit(solution)/shard_map/ppermute | solution.py:537
  340.4 4.6 %collective-permute-start.26 = (bf16[128,384]{1,0:T(8,128)(2,1)S(1)}, bf16[128,384]{1,0:T(8,128)(2,1)S(1)}, u32[]{:S(2)}, u32[]{:S(2)}) collective-permute-start(bf16[128,384]{1,0:T(8,128)(2,1)S(1)} %bitcast.87), channel_id=1, source_target_pairs={{0,144},{16,128},{64,208},{80,192},{1,145},{17,129},{65,209},{81,1... | collective-permute-start | bytes 294920 | tf_op jit(solution)/shard_map/ppermute | solution.py:539
  342.3 5.9 %collective-permute-start.27 = (bf16[128,384]{1,0:T(8,128)(2,1)S(1)}, bf16[128,384]{1,0:T(8,128)(2,1)S(1)}, u32[]{:S(2)}, u32[]{:S(2)}) collective-permute-start(bf16[128,384]{1,0:T(8,128)(2,1)S(1)} %bitcast.88), channel_id=1, source_target_pairs={{0,192},{1,193},{2,194},{3,195},{4,196},{5,197},{6,198},{7,199},{8... | collective-permute-start | bytes 294920 | tf_op jit(solution)/shard_map/ppermute | solution.py:537
  343.7 4.6 %collective-permute-start.28 = (bf16[128,384]{1,0:T(8,128)(2,1)S(1)}, bf16[128,384]{1,0:T(8,128)(2,1)S(1)}, u32[]{:S(2)}, u32[]{:S(2)}) collective-permute-start(bf16[128,384]{1,0:T(8,128)(2,1)S(1)} %bitcast.89), channel_id=1, source_target_pairs={{0,208},{16,192},{1,209},{17,193},{2,210},{18,194},{3,211},{19,195... | collective-permute-start | bytes 294920 | tf_op jit(solution)/shard_map/ppermute | solution.py:539
  351.0 1.3 collective-permute-start.30
  352.3 35.5 %copy-start.1 = (f32[1000,512]{1,0:T(8,128)S(1)}, f32[1000,512]{1,0:T(8,128)}, u32[]{:S(2)}) copy-start(f32[1000,512]{1,0:T(8,128)} %param.15) | copy-start | bytes 6144004
  (4 other events, 3.4 us)
Sparse Core Ops, SparseCore 0:
  30.1 80.4 all-gather.4
  113.1 63.5 all-gather.6
  179.2 63.5 all-gather.8
  245.2 63.6 all-gather.10

commit v4 on v3

--- a/solution.py
+++ b/solution.py
@@ -239,9 +239,9 @@
 
         for k in range(16):
             fetch(k).start()
+        normalize(x_ref, mod_ref, tables_ref, norm_ref, small)
         for k in range(16):
             pass_on(k).start()
-        normalize(x_ref, mod_ref, tables_ref, norm_ref, small)
         mixed = jnp.zeros((GROUP, 576), F32)
         for piece in range(4):
             for k in range(4 * piece, 4 * piece + 4):
@@ -310,77 +310,111 @@
             send_out[to, lanes] = jnp.where(core == 0, value[odd], value[even])
 
 
-def attend_kernel_of(layer):
-    def attend_kernel(scalars, q_ref, *refs):
-        pieces, refs = refs[: 1 if layer == 0 else 8], refs[1 if layer == 0 else 8 :]
-        targets_hbm, rec_ref, stale_ref, own_hbm, other_hbm, keep_out, send_out, weights_out = refs[:8]
-        base_ref, cache_ref, rec_vmem, target_ref, sems = refs[8:]
-        half = scalars[0]
-        section = scalars[7]
-        rec_copies = [
-            pltpu.make_async_copy(
-                rec_ref.at[2 * layer + h, pl.ds(GROUP, REC_GROUP), :],
-                rec_vmem.at[pl.ds(REC_GROUP * h, REC_GROUP), :],
-                sems.at[4 + h],
+def merge_copies(layer, targets_hbm, rec_ref, stale_ref, base_ref, rec_vmem, target_ref, sems):
+    copies = [
+        pltpu.make_async_copy(
+            rec_ref.at[2 * layer + h, pl.ds(GROUP, REC_GROUP), :],
+            rec_vmem.at[pl.ds(REC_GROUP * h, REC_GROUP), :],
+            sems.at[h],
+        )
+        for h in range(2)
+    ]
+    copies += [
+        pltpu.make_async_copy(
+            stale_ref.at[2 * layer + h], base_ref.at[pl.ds(PLEN + STALE * h, STALE), :], sems.at[2 + h]
+        )
+        for h in range(2)
+    ]
+    copies.append(pltpu.make_async_copy(targets_hbm, target_ref, sems.at[4]))
+    for copy in copies:
+        copy.start()
+    return copies
+
+
+def merge(copies, base_ref, rec_vmem, target_ref, table_ref):
+    rec_vmem[2 * REC_GROUP :, :] = jnp.zeros((128 - 2 * REC_GROUP, 384), BF)
+    for copy in copies:
+        copy.wait()
+    match = iota((3 * PLEN, 128), 0) + PLEN == target_ref[0:1, :]
+    chosen = jnp.where(match, 1.0, 0.0)
+    hit = jnp.sum(chosen, axis=1, keepdims=True) > 0.5
+    placed = jnp.dot(chosen.astype(BF), rec_vmem[...], preferred_element_type=F32)
+    table_ref[PLEN:, :] = jnp.where(hit, placed, base_ref[PLEN:, :].astype(F32)).astype(BF)
+
+
+def merge_scratch():
+    return [
+        pltpu.VMEM((1024, 384), BF),
+        pltpu.VMEM((128, 384), BF),
+        pltpu.VMEM((8, 128), jnp.int32),
+        pltpu.SemaphoreType.DMA((5,)),
+    ]
+
+
+def table_kernel_of(layer):
+    def table_kernel(fresh_ref, targets_hbm, rec_ref, stale_ref, table_out, base_ref, rec_vmem, target_ref, sems):
+        del fresh_ref
+        copies = merge_copies(layer, targets_hbm, rec_ref, stale_ref, base_ref, rec_vmem, target_ref, sems)
+        table_out[0:PLEN, :] = jnp.zeros((PLEN, 384), BF)
+        merge(copies, base_ref, rec_vmem, target_ref, table_out)
+
+    return table_kernel
+
+
+def weight_copies(own_hbm, other_hbm, weights_out, sems):
+    copies = [
+        pltpu.make_async_copy(own_hbm, weights_out.at[0], sems.at[0]),
+        pltpu.make_async_copy(other_hbm, weights_out.at[1], sems.at[1]),
+    ]
+    for copy in copies:
+        copy.start()
+    return copies
+
+
+def attend_first_kernel(
+    scalars, q_ref, fresh_ref, targets_hbm, rec_ref, stale_ref, own_hbm, other_hbm,
+    keep_out, send_out, weights_out, cache_ref, weight_sems, base_ref, rec_vmem, target_ref, sems,
+):
+    copies = merge_copies(0, targets_hbm, rec_ref, stale_ref, base_ref, rec_vmem, target_ref, sems)
+    weights = weight_copies(own_hbm, other_hbm, weights_out, weight_sems)
+    merge(copies, base_ref, rec_vmem, target_ref, cache_ref)
+    for patch in range(4):
+
+        @pl.when(patch <= scalars[7])
+        def _(patch=patch):
+            cache_ref[PLEN * patch : PLEN * patch + PLEN, :] = jnp.concatenate(
+                [fresh_ref[2 * patch, 0:GROUP, :], fresh_ref[2 * patch + 1, 0:GROUP, :]], axis=0
             )
-            for h in range(2)
-        ]
-        rec_copies.append(pltpu.make_async_copy(targets_hbm, target_ref, sems.at[6]))
-        for copy in rec_copies:
-            copy.start()
-        from_base = [
-            pltpu.make_async_copy(
-                stale_ref.at[2 * layer + h], base_ref.at[pl.ds(PLEN + STALE * h, STALE), :], sems.at[h]
-            )
-            for h in range(2)
-        ]
-        weights = [
-            pltpu.make_async_copy(own_hbm, weights_out.at[0], sems.at[2]),
-            pltpu.make_async_copy(other_hbm, weights_out.at[1], sems.at[3]),
-        ]
-        for copy in from_base + weights:
-            copy.start()
-        rec_vmem[64:, :] = jnp.zeros((64, 384), BF)
-        for copy in rec_copies:
-            copy.wait()
-        match = iota((1024, 128), 0) == target_ref[0:1, :]
-        chosen = jnp.where(match, 1.0, 0.0)
-        hit = jnp.sum(chosen, axis=1, keepdims=True) > 0.5
-        placed = jnp.dot(chosen.astype(BF), rec_vmem[...], preferred_element_type=F32)
-        for copy in from_base:
-            copy.wait()
-        for patch in range(4):
+
+    attend(scalars, q_ref, cache_ref, keep_out, send_out)
+    for copy in weights:
+        copy.wait()
+
+
+def attend_kernel(
+    scalars, q_ref, own_ref, back1_ref, back2_ref, back3_ref, table_ref, own_hbm, other_hbm,
+    keep_out, send_out, weights_out, cache_ref, weight_sems,
+):
+    section, half = scalars[7], scalars[0]
+    weights = weight_copies(own_hbm, other_hbm, weights_out, weight_sems)
+    for patch in range(1, 4):
+
+        @pl.when(patch > section)
+        def _(patch=patch):
             rows = slice(PLEN * patch, PLEN * patch + PLEN)
-            if layer == 0:
-
-                @pl.when(patch <= section)
-                def _(patch=patch, rows=rows):
-                    fresh_ref = pieces[0]
-                    cache_ref[rows, :] = jnp.concatenate(
-                        [fresh_ref[2 * patch, 0:GROUP, :], fresh_ref[2 * patch + 1, 0:GROUP, :]], axis=0
-                    )
-
-            if patch == 0:
-                continue
-
-            @pl.when(patch > section)
-            def _(rows=rows):
-                cache_ref[rows, :] = jnp.where(hit[rows], placed[rows], base_ref[rows, :].astype(F32)).astype(BF)
-
-        if layer > 0:
-            for back in range(4):
-
-                @pl.when(section >= back)
-                def _(back=back):
-                    for piece, at in ((pieces[2 * back], half), (pieces[2 * back + 1], 1 - half)):
-                        start = pl.multiple_of((section - back) * PLEN + at * GROUP, GROUP)
-                        cache_ref[pl.ds(start, GROUP), :] = piece[...]
-
-        attend(scalars, q_ref, cache_ref, keep_out, send_out)
-        for copy in weights:
-            copy.wait()
-
-    return attend_kernel
+            cache_ref[rows, :] = table_ref[rows, :]
+
+    for back, piece in enumerate((own_ref, back1_ref, back2_ref, back3_ref)):
+
+        @pl.when(section >= back)
+        def _(back=back, piece=piece):
+            for at, rows in ((half, slice(0, GROUP)), (1 - half, slice(GROUP, 2 * GROUP))):
+                start = pl.multiple_of((section - back) * PLEN + at * GROUP, GROUP)
+                cache_ref[pl.ds(start, GROUP), :] = piece[rows, :]
+
+    attend(scalars, q_ref, cache_ref, keep_out, send_out)
+    for copy in weights:
+        copy.wait()
 
 
 def project_kernel(keep_ref, got_ref, weights_ref, out_ref):
@@ -531,13 +565,9 @@
     targets = pltpu.with_memory_space_constraint(targets, pltpu.HBM)
 
     def upwards(fresh):
-        pieces = [fresh, swapped(fresh, "half")]
-        for back in range(1, sections):
-            pairs = [(i, i + back) for i in range(sections - back)]
-            pieces.append(lax.ppermute(fresh, "section", pairs))
-            crossed = [(2 * a + h, 2 * b + 1 - h) for a, b in pairs for h in range(2)]
-            pieces.append(lax.ppermute(fresh, peers, crossed))
-        return pieces
+        both = jnp.concatenate([fresh, swapped(fresh, "half")], axis=0)
+        pairs = [[(i, i + back) for i in range(sections - back)] for back in range(1, sections)]
+        return [both] + [lax.ppermute(both, "section", steps) for steps in pairs]
 
     half_rows = shape_of((64, 256), BF)
     current, group, outs, first_fresh = tokens, gathered, [], None
@@ -560,24 +590,33 @@
             + small_scratch(GROUP),
         )(group, rec_fresh, *in_hbm, packed)
         out_other = swapped(out_own, "core")
+        attend_out = (half_rows, half_rows, shape_of((2, 192, D), BF))
+        attend_scratch = [pltpu.VMEM((1024, 384), BF), pltpu.SemaphoreType.DMA((2,))]
         if layer == 0:
             first_fresh = lax.all_to_all(fresh, peers, 0, 0)
-            pieces = [first_fresh]
+            keep, send, weights_out = call(
+                attend_first_kernel,
+                attend_out,
+                [SMEM, VMEM, VMEM] + [HBM] * 5,
+                "attend_first",
+                scratch=attend_scratch + merge_scratch(),
+            )(scalars, queries, first_fresh, targets, first_fresh, stale_all, out_own, out_other)
         else:
             pieces = upwards(fresh[0])
-        keep, send, weights_out = call(
-            attend_kernel_of(layer),
-            (half_rows, half_rows, shape_of((2, 192, D), BF)),
-            [SMEM] + [VMEM] * (1 + len(pieces)) + [HBM] * 5,
-            "attend",
-            scratch=[
-                pltpu.VMEM((1024, 384), BF),
-                pltpu.VMEM((1024, 384), BF),
-                pltpu.VMEM((128, 384), BF),
-                pltpu.VMEM((8, 128), jnp.int32),
-                pltpu.SemaphoreType.DMA((7,)),
-            ],
-        )(scalars, queries, *pieces, targets, first_fresh, stale_all, out_own, out_other)
+            merged = call(
+                table_kernel_of(layer),
+                shape_of((1024, 384), BF),
+                [HBM] * 4,
+                "table",
+                scratch=merge_scratch(),
+            )(fresh, targets, first_fresh, stale_all)
+            keep, send, weights_out = call(
+                attend_kernel,
+                attend_out,
+                [SMEM] + [VMEM] * 6 + [HBM] * 2,
+                "attend",
+                scratch=attend_scratch,
+            )(scalars, queries, *pieces, merged, out_own, out_other)
         projected = call(project_kernel, shape_of((64, D), BF), [VMEM] * 3, "project")(
             keep, swapped(send, "core"), weights_out
         )

time: 396 us -> 391 us (0.987)
  starting transfers between devices: 64.1 us -> 47.3 us
  waiting for transfers between devices: 37.5 us -> 48.3 us
    ppermute x18 -> x9, starting transfers between devices: 45.8 us -> 28.7 us  [upwards(): return [both] + [lax.ppermute(both, 'section', steps) for steps in pairs]]
    ppermute x13, waiting for transfers between devices: 6.13 us -> 17.1 us  [swapped(): return lax.ppermute(value, axis, [(0, 1), (1, 0)])]
    pallas_call x4 -> x7, Pallas kernels: 11.2 us -> 13.6 us  [the longest x3 6.09 us: local(): call(attend_kernel, attend_out, [SMEM] + [VMEM] * 6 + [HBM] * 2, 'attend'...]
    ppermute x18 -> x9, waiting for transfers between devices: 10.2 us -> 9.43 us  [upwards(): return [both] + [lax.ppermute(both, 'section', steps) for steps in pairs]]
  transfers between devices with their start and end apart: 37 -> 28, of which waited for: 13 -> 16; matrix products, arithmetic and copies ran while one was open for 3% -> 3% of each run, Pallas kernels for 9% -> 10%
where the time goes in v4:
time: 391 us; the launch traced here: 390 us
  blocking collectives  215 us (55%)
  waiting for transfers between devices  48.3 us (12%)
  Pallas kernels  47.5 us (12%)
  starting transfers between devices  47.3 us (12%)
  between operations  16.2 us (4%)
  local copies, waits for them, and re-layouts  14.8 us (4%)
    all_to_all x4, blocking collectives, local(): parts = lax.all_to_all(projected.reshape(8, 8, D), 'z', 0, 0)  81.6 us
    all_gather x3, blocking collectives, local(): group = lax.all_gather(current, COL, axis=0, tiled=True)  50.9 us
    ppermute x9, starting transfers between devices, upwards(): return [both] + [lax.ppermute(both, 'section', steps) for steps in pairs]  28.7 us
    all_to_all x1, blocking collectives, local(): lax.all_to_all(jnp.broadcast_to(rows, (lax.axis_size(everyone), 17, 288))...  24.9 us
    all_gather x1, blocking collectives, local(): gathered = lax.all_gather(payload, COL, axis=0, tiled=True)  22.8 us
    pallas_call x4, Pallas kernels, local(): call(qkv_kernel_of(layer), (shape_of((GROUP, 384), BF), shape_of((copies,...  22.1 us
    all_to_all x1, blocking collectives, local(): chunks = lax.all_to_all(packed, 'section', 0, 0)  20.8 us
    all_to_all x1, waiting for transfers between devices, local(): first_fresh = lax.all_to_all(fresh, peers, 0, 0)  17.1 us
  transfers between devices with their start and end apart: 28, of which 16 were waited for; matrix products, arithmetic and copies ran while one was open for 3% of the time, Pallas kernels for 10%

profile of v4, /device:TPU:2, one launch (start us, length us, event | category | flops | bytes accessed | tf_op | source)
XLA Modules:
  0.0 390.3 jit_solution(1133507618284196506)
XLA Ops:
  6.5 1.6 pack.1
  8.1 20.8 %all_to_all.45 = bf16[4,384,384]{2,1,0:T(8,128)(2,1)S(1)} all-to-all(bf16[4,384,384]{2,1,0:T(8,128)(2,1)S(1)} %pack.1), channel_id=1, replica_groups=mesh['section'=4,'req'=2,'half'=2,'z'=8,'core'=2] {'section'}, dimensions={0} | all-to-all | bytes 2359296 | tf_op jit(solution)/shard_map/all_to_all | solution.py:483
  32.4 2.2 collective-permute-start
  34.6 1.4 collective-permute-start.1
  36.0 1.7 constant_dynamic-slice_fusion
  38.8 1.6 broadcast_in_dim.47
  40.5 4.9 %all-to-all-start = ((bf16[8,384,384]{2,1,0:T(8,128)(2,1)}), bf16[8,384,384]{2,1,0:T(8,128)(2,1)}, u32[]{:S(2)}, u32[]{:S(2)}) async-start(bf16[8,384,384]{2,1,0:T(8,128)(2,1)} %broadcast_in_dim.47), calls=%async_computation | async-start | bytes 4718592 | tf_op jit(solution)/shard_map/all_to_all | solution.py:491
  53.9 22.8 %all_gather.24.gathered_ref.x_ref = bf16[128,3968]{1,0:T(8,128)(2,1)S(1)} all-gather(bf16[8,3968]{1,0:T(8,128)(2,1)S(1)} %fusion.1), channel_id=1, replica_groups=mesh['section'=4,'req'=2,'half'=2,'z'=8,'core'=2] {'z','core'}, dimensions={0}, use_global_device_ids=true | all-gather | bytes 1079296 | tf_op jit(solution)/shard_map/all_gather | solution.py:542
  77.4 24.9 %all_to_all.46.rows_hbm = f32[16,17,288]{2,1,0:T(8,128)S(1)} all-to-all(f32[16,17,288]{2,1,0:T(8,128)S(1)} %broadcast_in_dim.49), channel_id=1, replica_groups=mesh['section'=4,'req'=2,'half'=2,'z'=8,'core'=2] {'section','req','half'}, dimensions={0} | all-to-all | bytes 626688 | tf_op jit(solution)/shard_map/all_to_all | solution.py:549
  103.4 4.6 %rec.1.rec_ref = bf16[1,32,384]{2,1,0:T(8,128)(2,1)S(1)} custom-call(s32[16]{0:T(128)S(1)} %concatenate.34.scalars, bf16[128,3968]{1,0:T(8,128)(2,1)S(1)} %all_gather.24.gathered_ref.x_ref, f32[4,6,3072]{2,1,0:T(8,128)} %reshape.69.mod_hbm, f32[16,17,288]{2,1,0:T(8,128)} %copy-done.8, f32[3,160,128]{2,1,0:T(8,128)} %copy-done.2, bf16[576,3072]{1,0:T(8,128)(2,1)} %bitcast.90), custom_call_target="tpu_custom_call" | custom-call | tf_op jit(solution)/shard_map/rec/pallas_call | solution.py:552
  108.0 2.7 all-gather.5.cloned.1.call-done.packed_ref
  110.6 5.5 %qkv.4 = (bf16[128,384]{1,0:T(8,128)(2,1)S(1)}, bf16[8,160,384]{2,1,0:T(8,128)(2,1)S(1)}, bf16[192,3072]{1,0:T(8,128)(2,1)S(1)}, f32[2,3072]{1,0:T(2,128)S(1)}) custom-call(bf16[128,3968]{1,0:T(8,128)(2,1)S(1)} %all_gather.24.gathered_ref.x_ref, bf16[1,32,384]{2,1,0:T(8,128)(2,1)S(1)} %rec.1.rec_ref, f32[4,6,3072]{2,1,0:T(8,128)} %reshape.69.mod_hbm, ...), custom_call_target="tpu_custom_call" | custom-call | tf_op jit(solution)/shard_map/qkv/pallas_call | solution.py:579
  117.7 4.8 %all-to-all-start.3 = ((bf16[8,160,384]{2,1,0:T(8,128)(2,1)}), bf16[8,160,384]{2,1,0:T(8,128)(2,1)S(1)}, u32[]{:S(2)}, u32[]{:S(2)}) async-start(bf16[8,160,384]{2,1,0:T(8,128)(2,1)} %copy-done.3), calls=%async_computation.3 | async-start | bytes 1966080 | tf_op jit(solution)/shard_map/all_to_all | solution.py:596
  122.6 17.1 %all-to-all-done.3.fresh_ref.rec_ref = bf16[8,160,384]{2,1,0:T(8,128)(2,1)S(1)} async-done(((bf16[8,160,384]{2,1,0:T(8,128)(2,1)}), bf16[8,160,384]{2,1,0:T(8,128)(2,1)S(1)}, u32[]{:S(2)}, u32[]{:S(2)}) %all-to-all-start.3) | async-done | bytes 983072 | tf_op jit(solution)/shard_map/all_to_all | solution.py:596
  140.3 3.0 attend_first.1
  145.2 21.8 %all_to_all.47.parts_ref = bf16[8,8,3072]{2,1,0:T(8,128)(2,1)S(1)} all-to-all(bf16[8,8,3072]{2,1,0:T(8,128)(2,1)S(1)} %bitcast.74), channel_id=1, replica_groups=mesh['section'=4,'req'=2,'half'=2,'z'=8,'core'=2] {'z'}, dimensions={0} | all-to-all | bytes 786432 | tf_op jit(solution)/shard_map/all_to_all | solution.py:623
  167.7 17.0 %all_gather.26.x_ref = bf16[128,3072]{1,0:T(8,128)(2,1)S(1)} all-gather(bf16[8,3072]{1,0:T(8,128)(2,1)S(1)} %residual.4.x_ref), channel_id=1, replica_groups=mesh['section'=4,'req'=2,'half'=2,'z'=8,'core'=2] {'z','core'}, dimensions={0}, use_global_device_ids=true | all-gather | bytes 835584 | tf_op jit(solution)/shard_map/all_gather | solution.py:577
  184.7 5.5 %qkv.5 = (bf16[128,384]{1,0:T(8,128)(2,1)S(1)}, bf16[1,128,384]{2,1,0:T(8,128)(2,1)S(1)}, bf16[192,3072]{1,0:T(8,128)(2,1)S(1)}, f32[2,3072]{1,0:T(2,128)S(1)}) custom-call(bf16[128,3072]{1,0:T(8,128)(2,1)S(1)} %all_gather.26.x_ref, bf16[1,32,384]{2,1,0:T(8,128)(2,1)S(1)} %rec.1.rec_ref, f32[4,6,3072]{2,1,0:T(8,128)} %reshape.69.mod_hbm, ...), custom_call_target="tpu_custom_call" | custom-call | tf_op jit(solution)/shard_map/qkv/pallas_call | solution.py:579
  190.7 1.7 collective-permute-start.4
  192.4 4.3 %collective-permute-done.4 = bf16[128,384]{1,0:T(8,128)(2,1)S(1)} collective-permute-done((bf16[128,384]{1,0:T(8,128)(2,1)S(1)}, bf16[128,384]{1,0:T(8,128)(2,1)S(1)}, u32[]{:S(2)}, u32[]{:S(2)}) %collective-permute-start.4) | collective-permute-done | bytes 98336 | tf_op jit(solution)/shard_map/ppermute | solution.py:444
  196.7 2.8 collective-permute-start.5
  199.5 3.7 collective-permute-start.6
  203.2 1.3 collective-permute-start.7
  204.5 1.5 table.3.table_ref
  206.0 2.7 collective-permute-done.6.back2_ref
  209.3 2.0 attend.3
  213.2 20.5 %all_to_all.48.parts_ref = bf16[8,8,3072]{2,1,0:T(8,128)(2,1)S(1)} all-to-all(bf16[8,8,3072]{2,1,0:T(8,128)(2,1)S(1)} %bitcast.75), channel_id=1, replica_groups=mesh['section'=4,'req'=2,'half'=2,'z'=8,'core'=2] {'z'}, dimensions={0} | all-to-all | bytes 786432 | tf_op jit(solution)/shard_map/all_to_all | solution.py:623
  234.4 16.8 %all_gather.28.x_ref = bf16[128,3072]{1,0:T(8,128)(2,1)S(1)} all-gather(bf16[8,3072]{1,0:T(8,128)(2,1)S(1)} %residual.5.x_ref), channel_id=1, replica_groups=mesh['section'=4,'req'=2,'half'=2,'z'=8,'core'=2] {'z','core'}, dimensions={0}, use_global_device_ids=true | all-gather | bytes 835584 | tf_op jit(solution)/shard_map/all_gather | solution.py:577
  251.2 5.5 %qkv.6 = (bf16[128,384]{1,0:T(8,128)(2,1)S(1)}, bf16[1,128,384]{2,1,0:T(8,128)(2,1)S(1)}, bf16[192,3072]{1,0:T(8,128)(2,1)S(1)}, f32[2,3072]{1,0:T(2,128)S(1)}) custom-call(bf16[128,3072]{1,0:T(8,128)(2,1)S(1)} %all_gather.28.x_ref, bf16[1,32,384]{2,1,0:T(8,128)(2,1)S(1)} %rec.1.rec_ref, f32[4,6,3072]{2,1,0:T(8,128)} %reshape.69.mod_hbm, ...), custom_call_target="tpu_custom_call" | custom-call | tf_op jit(solution)/shard_map/qkv/pallas_call | solution.py:579
  258.2 3.9 collective-permute-done.10
  262.1 1.3 collective-permute-start.11
  263.4 8.0 %collective-permute-start.12 = (bf16[256,384]{1,0:T(8,128)(2,1)S(1)}, bf16[256,384]{1,0:T(8,128)(2,1)S(1)}, u32[]{:S(2)}, u32[]{:S(2)}) collective-permute-start(bf16[256,384]{1,0:T(8,128)(2,1)S(1)} %pad_maximum_fusion.1.own_ref), channel_id=1, source_target_pairs={{0,128},{64,192},{1,129},{65,193},{2,130},{66,194},{3,131},{67,195... | collective-permute-start | bytes 589832 | tf_op jit(solution)/shard_map/ppermute | solution.py:570
  271.4 1.3 collective-permute-start.13
  272.7 1.5 table.4.table_ref
  274.6 2.6 collective-permute-done.13.back3_ref
  277.1 2.0 attend.4
  281.0 20.5 %all_to_all.49.parts_ref = bf16[8,8,3072]{2,1,0:T(8,128)(2,1)S(1)} all-to-all(bf16[8,8,3072]{2,1,0:T(8,128)(2,1)S(1)} %bitcast.76), channel_id=1, replica_groups=mesh['section'=4,'req'=2,'half'=2,'z'=8,'core'=2] {'z'}, dimensions={0} | all-to-all | bytes 786432 | tf_op jit(solution)/shard_map/all_to_all | solution.py:623
  302.2 17.1 %all_gather.30.x_ref = bf16[128,3072]{1,0:T(8,128)(2,1)S(1)} all-gather(bf16[8,3072]{1,0:T(8,128)(2,1)S(1)} %residual.6.x_ref), channel_id=1, replica_groups=mesh['section'=4,'req'=2,'half'=2,'z'=8,'core'=2] {'z','core'}, dimensions={0}, use_global_device_ids=true | all-gather | bytes 835584 | tf_op jit(solution)/shard_map/all_gather | solution.py:577
  319.3 5.5 %qkv.7 = (bf16[128,384]{1,0:T(8,128)(2,1)S(1)}, bf16[1,128,384]{2,1,0:T(8,128)(2,1)S(1)}, bf16[192,3072]{1,0:T(8,128)(2,1)S(1)}, f32[2,3072]{1,0:T(2,128)S(1)}) custom-call(bf16[128,3072]{1,0:T(8,128)(2,1)S(1)} %all_gather.30.x_ref, bf16[1,32,384]{2,1,0:T(8,128)(2,1)S(1)} %rec.1.rec_ref, f32[4,6,3072]{2,1,0:T(8,128)} %reshape.69.mod_hbm, ...), custom_call_target="tpu_custom_call" | custom-call | tf_op jit(solution)/shard_map/qkv/pallas_call | solution.py:579
  326.0 4.2 %collective-permute-done.16 = bf16[128,384]{1,0:T(8,128)(2,1)S(1)} collective-permute-done((bf16[128,384]{1,0:T(8,128)(2,1)S(1)}, bf16[128,384]{1,0:T(8,128)(2,1)S(1)}, u32[]{:S(2)}, u32[]{:S(2)}) %collective-permute-start.16) | collective-permute-done | bytes 98336 | tf_op jit(solution)/shard_map/ppermute | solution.py:444
  330.1 1.3 collective-permute-start.17
  331.4 7.7 %collective-permute-start.18 = (bf16[256,384]{1,0:T(8,128)(2,1)S(1)}, bf16[256,384]{1,0:T(8,128)(2,1)S(1)}, u32[]{:S(2)}, u32[]{:S(2)}) collective-permute-start(bf16[256,384]{1,0:T(8,128)(2,1)S(1)} %pad_maximum_fusion.2.own_ref), channel_id=1, source_target_pairs={{0,128},{64,192},{1,129},{65,193},{2,130},{66,194},{3,131},{67,195... | collective-permute-start | bytes 589832 | tf_op jit(solution)/shard_map/ppermute | solution.py:570
  339.1 1.3 collective-permute-start.19
  340.4 1.5 table.5.table_ref
  342.5 2.7 collective-permute-done.19.back3_ref
  345.2 2.0 attend.5
  349.1 18.7 %all_to_all.50.parts_ref = bf16[8,8,3072]{2,1,0:T(8,128)(2,1)S(1)} all-to-all(bf16[8,8,3072]{2,1,0:T(8,128)(2,1)S(1)} %bitcast.77), channel_id=1, replica_groups=mesh['section'=4,'req'=2,'half'=2,'z'=8,'core'=2] {'z'}, dimensions={0} | all-to-all | bytes 786432 | tf_op jit(solution)/shard_map/all_to_all | solution.py:623
  368.6 14.4 %all_to_all.51 = bf16[8,4,3072]{2,1,0:T(4,128)(2,1)S(1)} all-to-all(bf16[8,4,3072]{2,1,0:T(4,128)(2,1)S(1)} %reshape.74), channel_id=1, replica_groups=mesh['section'=4,'req'=2,'half'=2,'z'=8,'core'=2] {'section','req'}, dimensions={0} | all-to-all | bytes 393216 | tf_op jit(solution)/shard_map/all_to_all | solution.py:630
  (125 shorter events, 29.9 us)
Async XLA Ops:
  6.5 42.5 %copy-start = (f32[1000,512]{1,0:T(8,128)S(1)}, f32[1000,512]{1,0:T(8,128)}, u32[]{:S(2)}) copy-start(f32[1000,512]{1,0:T(8,128)} %param.15) | copy-start | bytes 6144004
  6.5 104.1 %all-gather.5.cloned.1.call-start = ((), (), s32[]{:S(2)}) async-start(), calls=%async_computation.9 | async-start | bytes 5013504 | tf_op jit(solution)/shard_map/all_gather | solution.py:485
  28.9 5.8 %copy-start.9 = (bf16[1,1,2,3072]{3,2,1,0:T(2,128)(2,1)S(1)}, bf16[1,1,2,3072]{3,2,1,0:T(2,128)(2,1)}, u32[]{:S(2)}) copy-start(bf16[1,1,2,3072]{3,2,1,0:T(2,128)(2,1)} %param.21) | copy-start | bytes 36868
  30.1 154.6 %all-gather.7.cloned.1.call-start = ((), (), s32[]{:S(2)}) async-start(), calls=%async_computation.10 | async-start | bytes 5013504 | tf_op jit(solution)/shard_map/all_gather | solution.py:485
  30.8 220.4 %all-gather.9.cloned.1.call-start = ((), (), s32[]{:S(2)}) async-start(), calls=%async_computation.11 | async-start | bytes 5013504 | tf_op jit(solution)/shard_map/all_gather | solution.py:485
  32.4 21.4 %collective-permute-start = (bf16[4,2,3072]{2,0,1:T(4,128)(2,1)S(1)}, bf16[4,2,3072]{2,0,1:T(4,128)(2,1)S(1)}, u32[]{:S(2)}, u32[]{:S(2)}) collective-permute-start(bf16[4,2,3072]{2,0,1:T(4,128)(2,1)S(1)} %bitcast.94), channel_id=1, source_target_pairs={{0,32},{32,0},{1,33},{33,1},{2,34},{34,2},{3,35},{35,3},{4,36},{36... | collective-permute-start | bytes 147464 | tf_op jit(solution)/shard_map/ppermute | solution.py:444
  34.6 19.0 %collective-permute-start.1 = (bf16[1,2,3072]{2,1,0:T(2,128)(2,1)S(1)}, bf16[1,2,3072]{2,1,0:T(2,128)(2,1)S(1)}, u32[]{:S(2)}, u32[]{:S(2)}) collective-permute-start(bf16[1,2,3072]{2,1,0:T(2,128)(2,1)S(1)} %bitcast.98), channel_id=1, source_target_pairs={{0,32},{32,0},{1,33},{33,1},{2,34},{34,2},{3,35},{35,3},{4,36},{36... | collective-permute-start | bytes 36872 | tf_op jit(solution)/shard_map/ppermute | solution.py:444
  40.4 5.6 %copy-start.13 = (s32[2,64]{1,0:T(2,128)S(1)}, s32[2,64]{1,0:T(2,128)}, u32[]{:S(2)}) copy-start(s32[2,64]{1,0:T(2,128)} %param.22) | copy-start | bytes 1540
  40.4 6.1 %copy-start.12 = (s32[2,4]{1,0:T(2,128)S(1)}, s32[2,4]{1,0:T(2,128)}, u32[]{:S(2)}) copy-start(s32[2,4]{1,0:T(2,128)} %param.13) | copy-start | bytes 100
  40.4 11.3 %copy-start.4 = (bf16[1,512,288]{1,2,0:T(8,128)(2,1)S(1)}, bf16[1,512,288]{1,2,0:T(8,128)(2,1)}, u32[]{:S(2)}) copy-start(bf16[1,512,288]{1,2,0:T(8,128)(2,1)} %param.16) | copy-start | bytes 884740
  40.4 11.3 %copy-start.7 = (f32[1,128]{1,0:T(1,128)S(1)}, f32[1,128]{1,0:T(1,128)}, u32[]{:S(2)}) copy-start(f32[1,128]{1,0:T(1,128)} %constant.86.clone.rate_ref) | copy-start | bytes 1540
  40.4 13.1 %copy-start.14 = (f32[1,2,64]{2,1,0:T(2,128)S(1)}, f32[1,2,64]{2,1,0:T(2,128)}, u32[]{:S(2)}) copy-start(f32[1,2,64]{2,1,0:T(2,128)} %param.19) | copy-start | bytes 1540
  40.5 36.9 %all-to-all-start = ((bf16[8,384,384]{2,1,0:T(8,128)(2,1)}), bf16[8,384,384]{2,1,0:T(8,128)(2,1)}, u32[]{:S(2)}, u32[]{:S(2)}) async-start(bf16[8,384,384]{2,1,0:T(8,128)(2,1)} %broadcast_in_dim.47), calls=%async_computation | async-start | bytes 4718592 | tf_op jit(solution)/shard_map/all_to_all | solution.py:491
  45.4 273.9 %all-gather.11.cloned.1.call-start = ((), (), s32[]{:S(2)}) async-start(), calls=%async_computation.12 | async-start | bytes 5013504 | tf_op jit(solution)/shard_map/all_gather | solution.py:485
  46.6 5.2 %copy-start.10 = (s32[32]{0:T(128)}, s32[32]{0:T(128)S(1)}, u32[]{:S(2)}) copy-start(s32[32]{0:T(128)S(1)} %reshape.67) | copy-start | bytes 388
  52.8 0.7 copy-start.2
  102.3 1.1 copy-start.8
  116.2 0.6 copy-start.5
  116.8 1.0 copy-start.3
  116.8 5.7 %copy-start.11 = (s32[32]{0:T(128)S(1)}, s32[32]{0:T(128)}, u32[]{:S(2)}) copy-start(s32[32]{0:T(128)} %copy-done.10) | copy-start | bytes 388
  116.8 23.0 %collective-permute-start.2 = (bf16[192,3072]{1,0:T(8,128)(2,1)S(1)}, bf16[192,3072]{1,0:T(8,128)(2,1)S(1)}, u32[]{:S(2)}, u32[]{:S(2)}) collective-permute-start(bf16[192,3072]{1,0:T(8,128)(2,1)S(1)} %get-tuple-element.43.own_hbm), channel_id=1, source_target_pairs={{0,1},{1,0},{2,3},{3,2},{4,5},{5,4},{6,7},{7,6},{8,9},{9,8},{10,11... | collective-permute-start | bytes 3538952 | tf_op jit(solution)/shard_map/ppermute | solution.py:444
  117.7 22.0 %all-to-all-start.3 = ((bf16[8,160,384]{2,1,0:T(8,128)(2,1)}), bf16[8,160,384]{2,1,0:T(8,128)(2,1)S(1)}, u32[]{:S(2)}, u32[]{:S(2)}) async-start(bf16[8,160,384]{2,1,0:T(8,128)(2,1)} %copy-done.3), calls=%async_computation.3 | async-start | bytes 1966080 | tf_op jit(solution)/shard_map/all_to_all | solution.py:596
  143.4 1.3 collective-permute-start.3
  144.7 22.4 %copy-start.6 = (f32[2,3072]{1,0:T(2,128)S(1)}, f32[2,3072]{1,0:T(2,128)}, u32[]{:S(2)}) copy-start(f32[2,3072]{1,0:T(2,128)} %copy-done.5) | copy-start | bytes 73732
  190.2 19.1 %collective-permute-start.8 = (bf16[192,3072]{1,0:T(8,128)(2,1)S(1)}, bf16[192,3072]{1,0:T(8,128)(2,1)S(1)}, u32[]{:S(2)}, u32[]{:S(2)}) collective-permute-start(bf16[192,3072]{1,0:T(8,128)(2,1)S(1)} %get-tuple-element.50.own_hbm), channel_id=1, source_target_pairs={{0,1},{1,0},{2,3},{3,2},{4,5},{5,4},{6,7},{7,6},{8,9},{9,8},{10,11... | collective-permute-start | bytes 3538952 | tf_op jit(solution)/shard_map/ppermute | solution.py:444
  190.7 6.0 %collective-permute-start.4 = (bf16[128,384]{1,0:T(8,128)(2,1)S(1)}, bf16[128,384]{1,0:T(8,128)(2,1)S(1)}, u32[]{:S(2)}, u32[]{:S(2)}) collective-permute-start(bf16[128,384]{1,0:T(8,128)(2,1)S(1)} %bitcast.83), channel_id=1, source_target_pairs={{0,16},{16,0},{1,17},{17,1},{2,18},{18,2},{3,19},{19,3},{4,20},{20... | collective-permute-start | bytes 294920 | tf_op jit(solution)/shard_map/ppermute | solution.py:444
  196.7 9.3 %collective-permute-start.5 = (bf16[256,384]{1,0:T(8,128)(2,1)S(1)}, bf16[256,384]{1,0:T(8,128)(2,1)S(1)}, u32[]{:S(2)}, u32[]{:S(2)}) collective-permute-start(bf16[256,384]{1,0:T(8,128)(2,1)S(1)} %pad_maximum_fusion.own_ref), channel_id=1, source_target_pairs={{0,64},{64,128},{128,192},{1,65},{65,129},{129,193},{2,66},{66,130... | collective-permute-start | bytes 589832 | tf_op jit(solution)/shard_map/ppermute | solution.py:570
  199.5 9.2 %collective-permute-start.6 = (bf16[256,384]{1,0:T(8,128)(2,1)S(1)}, bf16[256,384]{1,0:T(8,128)(2,1)S(1)}, u32[]{:S(2)}, u32[]{:S(2)}) collective-permute-start(bf16[256,384]{1,0:T(8,128)(2,1)S(1)} %pad_maximum_fusion.own_ref), channel_id=1, source_target_pairs={{0,128},{64,192},{1,129},{65,193},{2,130},{66,194},{3,131},{67,195... | collective-permute-start | bytes 589832 | tf_op jit(solution)/shard_map/ppermute | solution.py:570
  203.2 6.1 %collective-permute-start.7 = (bf16[256,384]{1,0:T(8,128)(2,1)S(1)}, bf16[256,384]{1,0:T(8,128)(2,1)S(1)}, u32[]{:S(2)}, u32[]{:S(2)}) collective-permute-start(bf16[256,384]{1,0:T(8,128)(2,1)S(1)} %pad_maximum_fusion.own_ref), channel_id=1, source_target_pairs={{0,192},{1,193},{2,194},{3,195},{4,196},{5,197},{6,198},{7,199},{8... | collective-permute-start | bytes 589832 | tf_op jit(solution)/shard_map/ppermute | solution.py:570
  211.4 1.3 collective-permute-start.9
  256.8 20.4 %collective-permute-start.14 = (bf16[192,3072]{1,0:T(8,128)(2,1)S(1)}, bf16[192,3072]{1,0:T(8,128)(2,1)S(1)}, u32[]{:S(2)}, u32[]{:S(2)}) collective-permute-start(bf16[192,3072]{1,0:T(8,128)(2,1)S(1)} %get-tuple-element.57.own_hbm), channel_id=1, source_target_pairs={{0,1},{1,0},{2,3},{3,2},{4,5},{5,4},{6,7},{7,6},{8,9},{9,8},{10,11... | collective-permute-start | bytes 3538952 | tf_op jit(solution)/shard_map/ppermute | solution.py:444
  257.2 4.9 %collective-permute-start.10 = (bf16[128,384]{1,0:T(8,128)(2,1)S(1)}, bf16[128,384]{1,0:T(8,128)(2,1)S(1)}, u32[]{:S(2)}, u32[]{:S(2)}) collective-permute-start(bf16[128,384]{1,0:T(8,128)(2,1)S(1)} %bitcast.85), channel_id=1, source_target_pairs={{0,16},{16,0},{1,17},{17,1},{2,18},{18,2},{3,19},{19,3},{4,20},{20... | collective-permute-start | bytes 294920 | tf_op jit(solution)/shard_map/ppermute | solution.py:444
  262.1 12.2 %collective-permute-start.11 = (bf16[256,384]{1,0:T(8,128)(2,1)S(1)}, bf16[256,384]{1,0:T(8,128)(2,1)S(1)}, u32[]{:S(2)}, u32[]{:S(2)}) collective-permute-start(bf16[256,384]{1,0:T(8,128)(2,1)S(1)} %pad_maximum_fusion.1.own_ref), channel_id=1, source_target_pairs={{0,64},{64,128},{128,192},{1,65},{65,129},{129,193},{2,66},{66,130... | collective-permute-start | bytes 589832 | tf_op jit(solution)/shard_map/ppermute | solution.py:570
  263.4 11.2 %collective-permute-start.12 = (bf16[256,384]{1,0:T(8,128)(2,1)S(1)}, bf16[256,384]{1,0:T(8,128)(2,1)S(1)}, u32[]{:S(2)}, u32[]{:S(2)}) collective-permute-start(bf16[256,384]{1,0:T(8,128)(2,1)S(1)} %pad_maximum_fusion.1.own_ref), channel_id=1, source_target_pairs={{0,128},{64,192},{1,129},{65,193},{2,130},{66,194},{3,131},{67,195... | collective-permute-start | bytes 589832 | tf_op jit(solution)/shard_map/ppermute | solution.py:570
  271.4 5.7 %collective-permute-start.13 = (bf16[256,384]{1,0:T(8,128)(2,1)S(1)}, bf16[256,384]{1,0:T(8,128)(2,1)S(1)}, u32[]{:S(2)}, u32[]{:S(2)}) collective-permute-start(bf16[256,384]{1,0:T(8,128)(2,1)S(1)} %pad_maximum_fusion.1.own_ref), channel_id=1, source_target_pairs={{0,192},{1,193},{2,194},{3,195},{4,196},{5,197},{6,198},{7,199},{8... | collective-permute-start | bytes 589832 | tf_op jit(solution)/shard_map/ppermute | solution.py:570
  279.2 1.3 collective-permute-start.15
  324.8 20.4 %collective-permute-start.20 = (bf16[192,3072]{1,0:T(8,128)(2,1)S(1)}, bf16[192,3072]{1,0:T(8,128)(2,1)S(1)}, u32[]{:S(2)}, u32[]{:S(2)}) collective-permute-start(bf16[192,3072]{1,0:T(8,128)(2,1)S(1)} %get-tuple-element.64.own_hbm), channel_id=1, source_target_pairs={{0,1},{1,0},{2,3},{3,2},{4,5},{5,4},{6,7},{7,6},{8,9},{9,8},{10,11... | collective-permute-start | bytes 3538952 | tf_op jit(solution)/shard_map/ppermute | solution.py:444
  325.2 4.9 %collective-permute-start.16 = (bf16[128,384]{1,0:T(8,128)(2,1)S(1)}, bf16[128,384]{1,0:T(8,128)(2,1)S(1)}, u32[]{:S(2)}, u32[]{:S(2)}) collective-permute-start(bf16[128,384]{1,0:T(8,128)(2,1)S(1)} %bitcast.81), channel_id=1, source_target_pairs={{0,16},{16,0},{1,17},{17,1},{2,18},{18,2},{3,19},{19,3},{4,20},{20... | collective-permute-start | bytes 294920 | tf_op jit(solution)/shard_map/ppermute | solution.py:444
  330.1 11.8 %collective-permute-start.17 = (bf16[256,384]{1,0:T(8,128)(2,1)S(1)}, bf16[256,384]{1,0:T(8,128)(2,1)S(1)}, u32[]{:S(2)}, u32[]{:S(2)}) collective-permute-start(bf16[256,384]{1,0:T(8,128)(2,1)S(1)} %pad_maximum_fusion.2.own_ref), channel_id=1, source_target_pairs={{0,64},{64,128},{128,192},{1,65},{65,129},{129,193},{2,66},{66,130... | collective-permute-start | bytes 589832 | tf_op jit(solution)/shard_map/ppermute | solution.py:570
  331.4 11.0 %collective-permute-start.18 = (bf16[256,384]{1,0:T(8,128)(2,1)S(1)}, bf16[256,384]{1,0:T(8,128)(2,1)S(1)}, u32[]{:S(2)}, u32[]{:S(2)}) collective-permute-start(bf16[256,384]{1,0:T(8,128)(2,1)S(1)} %pad_maximum_fusion.2.own_ref), channel_id=1, source_target_pairs={{0,128},{64,192},{1,129},{65,193},{2,130},{66,194},{3,131},{67,195... | collective-permute-start | bytes 589832 | tf_op jit(solution)/shard_map/ppermute | solution.py:570
  339.1 6.1 %collective-permute-start.19 = (bf16[256,384]{1,0:T(8,128)(2,1)S(1)}, bf16[256,384]{1,0:T(8,128)(2,1)S(1)}, u32[]{:S(2)}, u32[]{:S(2)}) collective-permute-start(bf16[256,384]{1,0:T(8,128)(2,1)S(1)} %pad_maximum_fusion.2.own_ref), channel_id=1, source_target_pairs={{0,192},{1,193},{2,194},{3,195},{4,196},{5,197},{6,198},{7,199},{8... | collective-permute-start | bytes 589832 | tf_op jit(solution)/shard_map/ppermute | solution.py:570
  347.2 1.3 collective-permute-start.21
  348.5 35.3 %copy-start.1 = (f32[1000,512]{1,0:T(8,128)S(1)}, f32[1000,512]{1,0:T(8,128)}, u32[]{:S(2)}) copy-start(f32[1000,512]{1,0:T(8,128)} %param.15) | copy-start | bytes 6144004
Sparse Core Ops, SparseCore 0:
  30.2 80.4 all-gather.4
  113.1 63.4 all-gather.6
  179.1 62.7 all-gather.8
  244.3 62.5 all-gather.10

commit v5 on v4

--- a/solution.py
+++ b/solution.py
@@ -109,7 +109,7 @@
     rows = x_ref.shape[0]
 
     def over_chunks(step, start):
-        return lax.fori_loop(0, chunks, lambda k, carry: step(pl.ds(pl.multiple_of(k * 128, 128), 128), carry), start, unroll=6)
+        return lax.fori_loop(0, chunks, lambda k, carry: step(pl.ds(pl.multiple_of(k * 128, 128), 128), carry), start, unroll=12)
 
     def add(lanes, total):
         return total + x_ref[:, lanes].astype(F32)
@@ -223,7 +223,7 @@
 
 def qkv_kernel_of(layer):
     def qkv_kernel(
-        x_ref, rec_ref, mod_hbm, rows_hbm, tables_hbm, packed_ref,
+        x_ref, mod_hbm, rows_hbm, tables_hbm, packed_ref,
         q_out, kv_out, weights_out, gates_out, norm_ref, w_vmem, sems, mod_ref, gain_ref, tables_ref, small_sems,
     ):
         rows = pl.ds(0, GROUP)
@@ -251,9 +251,6 @@
         heads_from(mixed, gain_ref, tables_ref, q_out, kv_out)
         gates_out[0:1, :] = mod_ref[2:3, :]
         gates_out[1:2, :] = mod_ref[5:6, :]
-        if layer == 0:
-            for copy in range(kv_out.shape[0]):
-                kv_out[copy, GROUP:, :] = rec_ref[0]
         for k in range(16):
             pass_on(k).wait()
 
@@ -313,7 +310,7 @@
 def merge_copies(layer, targets_hbm, rec_ref, stale_ref, base_ref, rec_vmem, target_ref, sems):
     copies = [
         pltpu.make_async_copy(
-            rec_ref.at[2 * layer + h, pl.ds(GROUP, REC_GROUP), :],
+            rec_ref.at[2 * layer + h],
             rec_vmem.at[pl.ds(REC_GROUP * h, REC_GROUP), :],
             sems.at[h],
         )
@@ -369,26 +366,6 @@
     for copy in copies:
         copy.start()
     return copies
-
-
-def attend_first_kernel(
-    scalars, q_ref, fresh_ref, targets_hbm, rec_ref, stale_ref, own_hbm, other_hbm,
-    keep_out, send_out, weights_out, cache_ref, weight_sems, base_ref, rec_vmem, target_ref, sems,
-):
-    copies = merge_copies(0, targets_hbm, rec_ref, stale_ref, base_ref, rec_vmem, target_ref, sems)
-    weights = weight_copies(own_hbm, other_hbm, weights_out, weight_sems)
-    merge(copies, base_ref, rec_vmem, target_ref, cache_ref)
-    for patch in range(4):
-
-        @pl.when(patch <= scalars[7])
-        def _(patch=patch):
-            cache_ref[PLEN * patch : PLEN * patch + PLEN, :] = jnp.concatenate(
-                [fresh_ref[2 * patch, 0:GROUP, :], fresh_ref[2 * patch + 1, 0:GROUP, :]], axis=0
-            )
-
-    attend(scalars, q_ref, cache_ref, keep_out, send_out)
-    for copy in weights:
-        copy.wait()
 
 
 def attend_kernel(
@@ -551,7 +528,7 @@
     in_hbm = [pltpu.with_memory_space_constraint(value, pltpu.HBM) for value in (modulation, rows, tables)]
     rec_fresh = call(
         rec_kernel,
-        shape_of((1, REC_GROUP, 384), BF),
+        shape_of((copies, REC_GROUP, 384), BF),
         [SMEM, VMEM] + [HBM] * 4,
         "rec",
         scratch=[
@@ -570,7 +547,9 @@
         return [both] + [lax.ppermute(both, "section", steps) for steps in pairs]
 
     half_rows = shape_of((64, 256), BF)
-    current, group, outs, first_fresh = tokens, gathered, [], None
+    group, rec_fresh = lax.optimization_barrier((gathered, rec_fresh))
+    rec_all = lax.all_to_all(rec_fresh, peers, 0, 0)
+    current, outs = tokens, []
     for layer in range(sections):
         packed = pltpu.with_memory_space_constraint(layers[layer], pltpu.HBM)
         if layer > 0:
@@ -580,43 +559,33 @@
             qkv_kernel_of(layer),
             (
                 shape_of((GROUP, 384), BF),
-                shape_of((copies, GROUP + REC_GROUP, 384) if layer == 0 else (1, GROUP, 384), BF),
+                shape_of((1, GROUP, 384), BF),
                 shape_of((192, D), BF),
                 shape_of((2, D), F32),
             ),
-            [VMEM] * 2 + [HBM] * 4,
+            [VMEM] + [HBM] * 4,
             "qkv",
             scratch=[pltpu.VMEM((GROUP, D), BF), pltpu.VMEM((576, D), BF), pltpu.SemaphoreType.DMA((32,))]
             + small_scratch(GROUP),
-        )(group, rec_fresh, *in_hbm, packed)
+        )(group, *in_hbm, packed)
         out_other = swapped(out_own, "core")
         attend_out = (half_rows, half_rows, shape_of((2, 192, D), BF))
         attend_scratch = [pltpu.VMEM((1024, 384), BF), pltpu.SemaphoreType.DMA((2,))]
-        if layer == 0:
-            first_fresh = lax.all_to_all(fresh, peers, 0, 0)
-            keep, send, weights_out = call(
-                attend_first_kernel,
-                attend_out,
-                [SMEM, VMEM, VMEM] + [HBM] * 5,
-                "attend_first",
-                scratch=attend_scratch + merge_scratch(),
-            )(scalars, queries, first_fresh, targets, first_fresh, stale_all, out_own, out_other)
-        else:
-            pieces = upwards(fresh[0])
-            merged = call(
-                table_kernel_of(layer),
-                shape_of((1024, 384), BF),
-                [HBM] * 4,
-                "table",
-                scratch=merge_scratch(),
-            )(fresh, targets, first_fresh, stale_all)
-            keep, send, weights_out = call(
-                attend_kernel,
-                attend_out,
-                [SMEM] + [VMEM] * 6 + [HBM] * 2,
-                "attend",
-                scratch=attend_scratch,
-            )(scalars, queries, *pieces, merged, out_own, out_other)
+        pieces = upwards(fresh[0])
+        merged = call(
+            table_kernel_of(layer),
+            shape_of((1024, 384), BF),
+            [HBM] * 4,
+            "table",
+            scratch=merge_scratch(),
+        )(fresh, targets, rec_all, stale_all)
+        keep, send, weights_out = call(
+            attend_kernel,
+            attend_out,
+            [SMEM] + [VMEM] * 6 + [HBM] * 2,
+            "attend",
+            scratch=attend_scratch,
+        )(scalars, queries, *pieces, merged, out_own, out_other)
         projected = call(project_kernel, shape_of((64, D), BF), [VMEM] * 3, "project")(
             keep, swapped(send, "core"), weights_out
         )

time: 391 us -> 395 us (1.010)
  starting transfers between devices: 47.3 us -> 61.8 us
  waiting for transfers between devices: 48.3 us -> 39.9 us
    ppermute x9 -> x12, starting transfers between devices: 28.7 us -> 40.3 us  [upwards(): return [both] + [lax.ppermute(both, 'section', steps) for steps in pairs]]
    all_to_all x1, waiting for transfers between devices: 17.1 us -> 6.13 us  [local(): rec_all = lax.all_to_all(rec_fresh, peers, 0, 0)]
    all_to_all x4, blocking collectives: 81.6 us -> 76.9 us  [local(): parts = lax.all_to_all(projected.reshape(8, 8, D), 'z', 0, 0)]
    ppermute x13 -> x14, waiting for transfers between devices: 17.1 us -> 21.3 us  [swapped(): return lax.ppermute(value, axis, [(0, 1), (1, 0)])]
    ppermute x13 -> x14, starting transfers between devices: 8.75 us -> 11.4 us  [swapped(): return lax.ppermute(value, axis, [(0, 1), (1, 0)])]
    pallas_call x3 -> x4, Pallas kernels: 6.09 us -> 8.53 us  [local(): call(attend_kernel, attend_out, [SMEM] + [VMEM] * 6 + [HBM] * 2, 'attend'...]
    pallas_call x6 -> x5, Pallas kernels: 29.7 us -> 27.3 us  [the longest x4 22.1 us: local(): call(qkv_kernel_of(layer), (shape_of((GROUP, 384), BF), shape_of((1, GROU...]
    ppermute x9 -> x12, waiting for transfers between devices: 9.43 us -> 9.17 us  [upwards(): return [both] + [lax.ppermute(both, 'section', steps) for steps in pairs]]
  transfers between devices with their start and end apart: 28 -> 32, of which waited for: 16 -> 16; matrix products, arithmetic and copies ran while one was open for 3% -> 3% of each run, Pallas kernels for 10% -> 10%
where the time goes in v5:
time: 395 us; the launch traced here: 394 us
  blocking collectives  212 us (54%)
  starting transfers between devices  61.8 us (16%)
  Pallas kernels  49 us (12%)
  waiting for transfers between devices  39.9 us (10%)
  between operations  16.4 us (4%)
  local copies, waits for them, and re-layouts  13.2 us (3%)
    all_to_all x4, blocking collectives, local(): parts = lax.all_to_all(projected.reshape(8, 8, D), 'z', 0, 0)  76.9 us
    all_gather x3, blocking collectives, local(): group = lax.all_gather(current, COL, axis=0, tiled=True)  50.5 us
    ppermute x12, starting transfers between devices, upwards(): return [both] + [lax.ppermute(both, 'section', steps) for steps in pairs]  40.3 us
    all_to_all x1, blocking collectives, local(): lax.all_to_all(jnp.broadcast_to(rows, (lax.axis_size(everyone), 17, 288))...  25.2 us
    all_gather x1, blocking collectives, local(): gathered = lax.all_gather(payload, COL, axis=0, tiled=True)  22.8 us
    pallas_call x4, Pallas kernels, local(): call(qkv_kernel_of(layer), (shape_of((GROUP, 384), BF), shape_of((1, GROU...  22.1 us
    ppermute x14, waiting for transfers between devices, swapped(): return lax.ppermute(value, axis, [(0, 1), (1, 0)])  21.3 us
    all_to_all x1, blocking collectives, local(): chunks = lax.all_to_all(packed, 'section', 0, 0)  20.8 us
  transfers between devices with their start and end apart: 32, of which 16 were waited for; matrix products, arithmetic and copies ran while one was open for 3% of the time, Pallas kernels for 10%

profile of v5, /device:TPU:2, one launch (start us, length us, event | category | flops | bytes accessed | tf_op | source)
XLA Modules:
  0.0 393.5 jit_solution(5990141248267031940)
XLA Ops:
  6.5 1.6 pack.1
  8.1 20.8 %all_to_all.45 = bf16[4,384,384]{2,1,0:T(8,128)(2,1)S(1)} all-to-all(bf16[4,384,384]{2,1,0:T(8,128)(2,1)S(1)} %pack.1), channel_id=1, replica_groups=mesh['section'=4,'req'=2,'half'=2,'z'=8,'core'=2] {'section'}, dimensions={0} | all-to-all | bytes 2359296 | tf_op jit(solution)/shard_map/all_to_all | solution.py:460
  32.4 2.2 collective-permute-start
  36.0 1.7 constant_dynamic-slice_fusion
  38.8 1.6 broadcast_in_dim.47
  40.5 4.9 %all-to-all-start = ((bf16[8,384,384]{2,1,0:T(8,128)(2,1)}), bf16[8,384,384]{2,1,0:T(8,128)(2,1)}, u32[]{:S(2)}, u32[]{:S(2)}) async-start(bf16[8,384,384]{2,1,0:T(8,128)(2,1)} %broadcast_in_dim.47), calls=%async_computation | async-start | bytes 4718592 | tf_op jit(solution)/shard_map/all_to_all | solution.py:468
  54.2 22.8 %all_gather.24.gathered_ref.x_ref = bf16[128,3968]{1,0:T(8,128)(2,1)S(1)} all-gather(bf16[8,3968]{1,0:T(8,128)(2,1)S(1)} %fusion.1), channel_id=1, replica_groups=mesh['section'=4,'req'=2,'half'=2,'z'=8,'core'=2] {'z','core'}, dimensions={0}, use_global_device_ids=true | all-gather | bytes 1079296 | tf_op jit(solution)/shard_map/all_gather | solution.py:519
  77.4 25.2 %all_to_all.46.rows_hbm = f32[16,17,288]{2,1,0:T(8,128)S(1)} all-to-all(f32[16,17,288]{2,1,0:T(8,128)S(1)} %broadcast_in_dim.49), channel_id=1, replica_groups=mesh['section'=4,'req'=2,'half'=2,'z'=8,'core'=2] {'section','req','half'}, dimensions={0} | all-to-all | bytes 626688 | tf_op jit(solution)/shard_map/all_to_all | solution.py:526
  103.7 5.3 %rec.1 = bf16[8,32,384]{2,1,0:T(8,128)(2,1)} custom-call(s32[16]{0:T(128)S(1)} %concatenate.37.scalars, bf16[128,3968]{1,0:T(8,128)(2,1)S(1)} %all_gather.24.gathered_ref.x_ref, f32[4,6,3072]{2,1,0:T(8,128)} %reshape.69.mod_hbm, f32[16,17,288]{2,1,0:T(8,128)} %copy-done.5, f32[3,160,128]{2,1,0:T(8,128)} %copy-done.2, bf16[576,3072]{1,0:T(8,128)(2,1)} %bitcast.93), custom_call_target="tpu_custom_call" | custom-call | tf_op jit(solution)/shard_map/rec/pallas_call | solution.py:529
  109.0 1.7 all-gather.5.cloned.1.call-done.packed_ref
  110.7 5.5 %qkv.4 = (bf16[128,384]{1,0:T(8,128)(2,1)S(1)}, bf16[1,128,384]{2,1,0:T(8,128)(2,1)S(1)}, bf16[192,3072]{1,0:T(8,128)(2,1)S(1)}, f32[2,3072]{1,0:T(2,128)S(1)}) custom-call(bf16[128,3968]{1,0:T(8,128)(2,1)S(1)} %all_gather.24.gathered_ref.x_ref, f32[4,6,3072]{2,1,0:T(8,128)} %reshape.69.mod_hbm, f32[16,17,288]{2,1,0:T(8,128)} %copy-done.5, ...), custom_call_target="tpu_custom_call" | custom-call | tf_op jit(solution)/shard_map/qkv/pallas_call | solution.py:558
  116.9 4.6 %collective-permute-done.2 = bf16[128,384]{1,0:T(8,128)(2,1)S(1)} collective-permute-done((bf16[128,384]{1,0:T(8,128)(2,1)S(1)}, bf16[128,384]{1,0:T(8,128)(2,1)S(1)}, u32[]{:S(2)}, u32[]{:S(2)}) %collective-permute-start.2) | collective-permute-done | bytes 98336 | tf_op jit(solution)/shard_map/ppermute | solution.py:421
  121.5 2.1 collective-permute-start.3
  123.6 4.6 %collective-permute-start.4 = (bf16[256,384]{1,0:T(8,128)(2,1)S(1)}, bf16[256,384]{1,0:T(8,128)(2,1)S(1)}, u32[]{:S(2)}, u32[]{:S(2)}) collective-permute-start(bf16[256,384]{1,0:T(8,128)(2,1)S(1)} %pad_maximum_fusion.own_ref), channel_id=1, source_target_pairs={{0,128},{64,192},{1,129},{65,193},{2,130},{66,194},{3,131},{67,195... | collective-permute-start | bytes 589832 | tf_op jit(solution)/shard_map/ppermute | solution.py:547
  128.3 2.0 collective-permute-start.5
  130.2 5.1 %all-to-all-start.3 = ((bf16[8,32,384]{2,1,0:T(8,128)(2,1)}), bf16[8,32,384]{2,1,0:T(8,128)(2,1)S(1)}, u32[]{:S(2)}, u32[]{:S(2)}) async-start(bf16[8,32,384]{2,1,0:T(8,128)(2,1)} %rec.1), calls=%async_computation.3 | async-start | bytes 393216 | tf_op jit(solution)/shard_map/all_to_all | solution.py:551
  135.4 6.1 %all-to-all-done.3.rec_ref = bf16[8,32,384]{2,1,0:T(8,128)(2,1)S(1)} async-done(((bf16[8,32,384]{2,1,0:T(8,128)(2,1)}), bf16[8,32,384]{2,1,0:T(8,128)(2,1)S(1)}, u32[]{:S(2)}, u32[]{:S(2)}) %all-to-all-start.3) | async-done | bytes 196640 | tf_op jit(solution)/shard_map/all_to_all | solution.py:551
  143.6 2.4 attend.4
  148.1 21.8 %all_to_all.47.parts_ref = bf16[8,8,3072]{2,1,0:T(8,128)(2,1)S(1)} all-to-all(bf16[8,8,3072]{2,1,0:T(8,128)(2,1)S(1)} %bitcast.75), channel_id=1, replica_groups=mesh['section'=4,'req'=2,'half'=2,'z'=8,'core'=2] {'z'}, dimensions={0} | all-to-all | bytes 786432 | tf_op jit(solution)/shard_map/all_to_all | solution.py:592
  170.5 16.8 %all_gather.26.x_ref = bf16[128,3072]{1,0:T(8,128)(2,1)S(1)} all-gather(bf16[8,3072]{1,0:T(8,128)(2,1)S(1)} %residual.4.x_ref), channel_id=1, replica_groups=mesh['section'=4,'req'=2,'half'=2,'z'=8,'core'=2] {'z','core'}, dimensions={0}, use_global_device_ids=true | all-gather | bytes 835584 | tf_op jit(solution)/shard_map/all_gather | solution.py:556
  187.4 5.5 %qkv.5 = (bf16[128,384]{1,0:T(8,128)(2,1)S(1)}, bf16[1,128,384]{2,1,0:T(8,128)(2,1)S(1)}, bf16[192,3072]{1,0:T(8,128)(2,1)S(1)}, f32[2,3072]{1,0:T(2,128)S(1)}) custom-call(bf16[128,3072]{1,0:T(8,128)(2,1)S(1)} %all_gather.26.x_ref, f32[4,6,3072]{2,1,0:T(8,128)} %reshape.69.mod_hbm, f32[16,17,288]{2,1,0:T(8,128)} %copy-done.5, f32[3,160,128]{2,1,0:T(8,128)} %copy-done.2, ...), custom_call_target="tpu_custom_call" | custom-call | tf_op jit(solution)/shard_map/qkv/pallas_call | solution.py:558
  193.3 1.8 collective-permute-start.8
  195.1 4.8 %collective-permute-done.8 = bf16[128,384]{1,0:T(8,128)(2,1)S(1)} collective-permute-done((bf16[128,384]{1,0:T(8,128)(2,1)S(1)}, bf16[128,384]{1,0:T(8,128)(2,1)S(1)}, u32[]{:S(2)}, u32[]{:S(2)}) %collective-permute-start.8) | collective-permute-done | bytes 98336 | tf_op jit(solution)/shard_map/ppermute | solution.py:421
  200.0 2.1 collective-permute-start.10
  202.2 5.2 %collective-permute-start.11 = (bf16[256,384]{1,0:T(8,128)(2,1)S(1)}, bf16[256,384]{1,0:T(8,128)(2,1)S(1)}, u32[]{:S(2)}, u32[]{:S(2)}) collective-permute-start(bf16[256,384]{1,0:T(8,128)(2,1)S(1)} %pad_maximum_fusion.1.own_ref), channel_id=1, source_target_pairs={{0,192},{1,193},{2,194},{3,195},{4,196},{5,197},{6,198},{7,199},{8... | collective-permute-start | bytes 589832 | tf_op jit(solution)/shard_map/ppermute | solution.py:547
  207.4 2.2 collective-permute-start.9
  209.6 1.5 table.5.table_ref
  211.1 3.2 collective-permute-done.11.back3_ref
  214.2 2.0 attend.5
  218.1 17.7 %all_to_all.48.parts_ref = bf16[8,8,3072]{2,1,0:T(8,128)(2,1)S(1)} all-to-all(bf16[8,8,3072]{2,1,0:T(8,128)(2,1)S(1)} %bitcast.76), channel_id=1, replica_groups=mesh['section'=4,'req'=2,'half'=2,'z'=8,'core'=2] {'z'}, dimensions={0} | all-to-all | bytes 786432 | tf_op jit(solution)/shard_map/all_to_all | solution.py:592
  236.4 16.8 %all_gather.28.x_ref = bf16[128,3072]{1,0:T(8,128)(2,1)S(1)} all-gather(bf16[8,3072]{1,0:T(8,128)(2,1)S(1)} %residual.5.x_ref), channel_id=1, replica_groups=mesh['section'=4,'req'=2,'half'=2,'z'=8,'core'=2] {'z','core'}, dimensions={0}, use_global_device_ids=true | all-gather | bytes 835584 | tf_op jit(solution)/shard_map/all_gather | solution.py:556
  253.3 5.5 %qkv.6 = (bf16[128,384]{1,0:T(8,128)(2,1)S(1)}, bf16[1,128,384]{2,1,0:T(8,128)(2,1)S(1)}, bf16[192,3072]{1,0:T(8,128)(2,1)S(1)}, f32[2,3072]{1,0:T(2,128)S(1)}) custom-call(bf16[128,3072]{1,0:T(8,128)(2,1)S(1)} %all_gather.28.x_ref, f32[4,6,3072]{2,1,0:T(8,128)} %reshape.69.mod_hbm, f32[16,17,288]{2,1,0:T(8,128)} %copy-done.5, f32[3,160,128]{2,1,0:T(8,128)} %copy-done.2, ...), custom_call_target="tpu_custom_call" | custom-call | tf_op jit(solution)/shard_map/qkv/pallas_call | solution.py:558
  260.6 4.0 %collective-permute-done.14 = bf16[128,384]{1,0:T(8,128)(2,1)S(1)} collective-permute-done((bf16[128,384]{1,0:T(8,128)(2,1)S(1)}, bf16[128,384]{1,0:T(8,128)(2,1)S(1)}, u32[]{:S(2)}, u32[]{:S(2)}) %collective-permute-start.14) | collective-permute-done | bytes 98336 | tf_op jit(solution)/shard_map/ppermute | solution.py:421
  264.6 3.2 collective-permute-start.15
  267.8 7.3 %collective-permute-start.16 = (bf16[256,384]{1,0:T(8,128)(2,1)S(1)}, bf16[256,384]{1,0:T(8,128)(2,1)S(1)}, u32[]{:S(2)}, u32[]{:S(2)}) collective-permute-start(bf16[256,384]{1,0:T(8,128)(2,1)S(1)} %pad_maximum_fusion.2.own_ref), channel_id=1, source_target_pairs={{0,128},{64,192},{1,129},{65,193},{2,130},{66,194},{3,131},{67,195... | collective-permute-start | bytes 589832 | tf_op jit(solution)/shard_map/ppermute | solution.py:547
  276.4 1.5 table.6.table_ref
  278.3 2.4 collective-permute-done.17.back3_ref
  280.7 2.0 attend.6
  284.8 18.7 %all_to_all.49.parts_ref = bf16[8,8,3072]{2,1,0:T(8,128)(2,1)S(1)} all-to-all(bf16[8,8,3072]{2,1,0:T(8,128)(2,1)S(1)} %bitcast.77), channel_id=1, replica_groups=mesh['section'=4,'req'=2,'half'=2,'z'=8,'core'=2] {'z'}, dimensions={0} | all-to-all | bytes 786432 | tf_op jit(solution)/shard_map/all_to_all | solution.py:592
  304.2 16.8 %all_gather.30.x_ref = bf16[128,3072]{1,0:T(8,128)(2,1)S(1)} all-gather(bf16[8,3072]{1,0:T(8,128)(2,1)S(1)} %residual.6.x_ref), channel_id=1, replica_groups=mesh['section'=4,'req'=2,'half'=2,'z'=8,'core'=2] {'z','core'}, dimensions={0}, use_global_device_ids=true | all-gather | bytes 835584 | tf_op jit(solution)/shard_map/all_gather | solution.py:556
  321.0 5.5 %qkv.7 = (bf16[128,384]{1,0:T(8,128)(2,1)S(1)}, bf16[1,128,384]{2,1,0:T(8,128)(2,1)S(1)}, bf16[192,3072]{1,0:T(8,128)(2,1)S(1)}, f32[2,3072]{1,0:T(2,128)S(1)}) custom-call(bf16[128,3072]{1,0:T(8,128)(2,1)S(1)} %all_gather.30.x_ref, f32[4,6,3072]{2,1,0:T(8,128)} %reshape.69.mod_hbm, f32[16,17,288]{2,1,0:T(8,128)} %copy-done.5, f32[3,160,128]{2,1,0:T(8,128)} %copy-done.2, ...), custom_call_target="tpu_custom_call" | custom-call | tf_op jit(solution)/shard_map/qkv/pallas_call | solution.py:558
  327.0 1.7 collective-permute-start.20
  328.7 3.1 collective-permute-done.20
  333.2 7.7 %collective-permute-start.22 = (bf16[256,384]{1,0:T(8,128)(2,1)S(1)}, bf16[256,384]{1,0:T(8,128)(2,1)S(1)}, u32[]{:S(2)}, u32[]{:S(2)}) collective-permute-start(bf16[256,384]{1,0:T(8,128)(2,1)S(1)} %pad_maximum_fusion.3.own_ref), channel_id=1, source_target_pairs={{0,128},{64,192},{1,129},{65,193},{2,130},{66,194},{3,131},{67,195... | collective-permute-start | bytes 589832 | tf_op jit(solution)/shard_map/ppermute | solution.py:547
  344.2 2.7 collective-permute-done.23.back3_ref
  346.9 2.0 attend.7
  350.8 18.7 %all_to_all.50.parts_ref = bf16[8,8,3072]{2,1,0:T(8,128)(2,1)S(1)} all-to-all(bf16[8,8,3072]{2,1,0:T(8,128)(2,1)S(1)} %bitcast.78), channel_id=1, replica_groups=mesh['section'=4,'req'=2,'half'=2,'z'=8,'core'=2] {'z'}, dimensions={0} | all-to-all | bytes 786432 | tf_op jit(solution)/shard_map/all_to_all | solution.py:592
  370.3 15.9 %all_to_all.51 = bf16[8,4,3072]{2,1,0:T(4,128)(2,1)S(1)} all-to-all(bf16[8,4,3072]{2,1,0:T(4,128)(2,1)S(1)} %reshape.74), channel_id=1, replica_groups=mesh['section'=4,'req'=2,'half'=2,'z'=8,'core'=2] {'section','req'}, dimensions={0} | all-to-all | bytes 393216 | tf_op jit(solution)/shard_map/all_to_all | solution.py:599
  (125 shorter events, 36.6 us)
Async XLA Ops:
  6.5 42.7 %copy-start = (f32[1000,512]{1,0:T(8,128)S(1)}, f32[1000,512]{1,0:T(8,128)}, u32[]{:S(2)}) copy-start(f32[1000,512]{1,0:T(8,128)} %param.15) | copy-start | bytes 6144004
  6.5 104.1 %all-gather.5.cloned.1.call-start = ((), (), s32[]{:S(2)}) async-start(), calls=%async_computation.9 | async-start | bytes 5013504 | tf_op jit(solution)/shard_map/all_gather | solution.py:462
  28.9 5.8 %copy-start.6 = (bf16[1,1,2,3072]{3,2,1,0:T(2,128)(2,1)S(1)}, bf16[1,1,2,3072]{3,2,1,0:T(2,128)(2,1)}, u32[]{:S(2)}) copy-start(bf16[1,1,2,3072]{3,2,1,0:T(2,128)(2,1)} %param.21) | copy-start | bytes 36868
  30.1 157.3 %all-gather.7.cloned.1.call-start = ((), (), s32[]{:S(2)}) async-start(), calls=%async_computation.10 | async-start | bytes 5013504 | tf_op jit(solution)/shard_map/all_gather | solution.py:462
  30.8 222.4 %all-gather.9.cloned.1.call-start = ((), (), s32[]{:S(2)}) async-start(), calls=%async_computation.11 | async-start | bytes 5013504 | tf_op jit(solution)/shard_map/all_gather | solution.py:462
  32.4 21.7 %collective-permute-start = (bf16[4,2,3072]{2,0,1:T(4,128)(2,1)S(1)}, bf16[4,2,3072]{2,0,1:T(4,128)(2,1)S(1)}, u32[]{:S(2)}, u32[]{:S(2)}) collective-permute-start(bf16[4,2,3072]{2,0,1:T(4,128)(2,1)S(1)} %bitcast.97), channel_id=1, source_target_pairs={{0,32},{32,0},{1,33},{33,1},{2,34},{34,2},{3,35},{35,3},{4,36},{36... | collective-permute-start | bytes 147464 | tf_op jit(solution)/shard_map/ppermute | solution.py:421
  34.6 19.3 %collective-permute-start.1 = (bf16[1,2,3072]{2,1,0:T(2,128)(2,1)S(1)}, bf16[1,2,3072]{2,1,0:T(2,128)(2,1)S(1)}, u32[]{:S(2)}, u32[]{:S(2)}) collective-permute-start(bf16[1,2,3072]{2,1,0:T(2,128)(2,1)S(1)} %bitcast.101), channel_id=1, source_target_pairs={{0,32},{32,0},{1,33},{33,1},{2,34},{34,2},{3,35},{35,3},{4,36},{36... | collective-permute-start | bytes 36872 | tf_op jit(solution)/shard_map/ppermute | solution.py:421
  40.4 5.6 %copy-start.8 = (s32[2,64]{1,0:T(2,128)S(1)}, s32[2,64]{1,0:T(2,128)}, u32[]{:S(2)}) copy-start(s32[2,64]{1,0:T(2,128)} %param.22) | copy-start | bytes 1540
  40.4 6.1 %copy-start.7 = (s32[2,4]{1,0:T(2,128)S(1)}, s32[2,4]{1,0:T(2,128)}, u32[]{:S(2)}) copy-start(s32[2,4]{1,0:T(2,128)} %param.13) | copy-start | bytes 100
  40.4 11.6 %copy-start.3 = (bf16[1,512,288]{1,2,0:T(8,128)(2,1)S(1)}, bf16[1,512,288]{1,2,0:T(8,128)(2,1)}, u32[]{:S(2)}) copy-start(bf16[1,512,288]{1,2,0:T(8,128)(2,1)} %param.16) | copy-start | bytes 884740
  40.4 11.6 %copy-start.4 = (f32[1,128]{1,0:T(1,128)S(1)}, f32[1,128]{1,0:T(1,128)}, u32[]{:S(2)}) copy-start(f32[1,128]{1,0:T(1,128)} %constant.86.clone.rate_ref) | copy-start | bytes 1540
  40.5 13.5 %copy-start.9 = (f32[1,2,64]{2,1,0:T(2,128)S(1)}, f32[1,2,64]{2,1,0:T(2,128)}, u32[]{:S(2)}) copy-start(f32[1,2,64]{2,1,0:T(2,128)} %param.19) | copy-start | bytes 1540
  40.5 36.9 %all-to-all-start = ((bf16[8,384,384]{2,1,0:T(8,128)(2,1)}), bf16[8,384,384]{2,1,0:T(8,128)(2,1)}, u32[]{:S(2)}, u32[]{:S(2)}) async-start(bf16[8,384,384]{2,1,0:T(8,128)(2,1)} %broadcast_in_dim.47), calls=%async_computation | async-start | bytes 4718592 | tf_op jit(solution)/shard_map/all_to_all | solution.py:468
  45.4 275.6 %all-gather.11.cloned.1.call-start = ((), (), s32[]{:S(2)}) async-start(), calls=%async_computation.12 | async-start | bytes 5013504 | tf_op jit(solution)/shard_map/all_gather | solution.py:462
  53.1 0.7 copy-start.2
  102.6 1.1 copy-start.5
  116.2 27.5 %collective-permute-start.6 = (bf16[192,3072]{1,0:T(8,128)(2,1)S(1)}, bf16[192,3072]{1,0:T(8,128)(2,1)S(1)}, u32[]{:S(2)}, u32[]{:S(2)}) collective-permute-start(bf16[192,3072]{1,0:T(8,128)(2,1)S(1)} %get-tuple-element.47.own_hbm), channel_id=1, source_target_pairs={{0,1},{1,0},{2,3},{3,2},{4,5},{5,4},{6,7},{7,6},{8,9},{9,8},{10,11... | collective-permute-start | bytes 3538952 | tf_op jit(solution)/shard_map/ppermute | solution.py:421
  116.3 5.2 %collective-permute-start.2 = (bf16[128,384]{1,0:T(8,128)(2,1)S(1)}, bf16[128,384]{1,0:T(8,128)(2,1)S(1)}, u32[]{:S(2)}, u32[]{:S(2)}) collective-permute-start(bf16[128,384]{1,0:T(8,128)(2,1)S(1)} %bitcast.82), channel_id=1, source_target_pairs={{0,16},{16,0},{1,17},{17,1},{2,18},{18,2},{3,19},{19,3},{4,20},{20... | collective-permute-start | bytes 294920 | tf_op jit(solution)/shard_map/ppermute | solution.py:421
  121.5 22.1 %collective-permute-start.3 = (bf16[256,384]{1,0:T(8,128)(2,1)S(1)}, bf16[256,384]{1,0:T(8,128)(2,1)S(1)}, u32[]{:S(2)}, u32[]{:S(2)}) collective-permute-start(bf16[256,384]{1,0:T(8,128)(2,1)S(1)} %pad_maximum_fusion.own_ref), channel_id=1, source_target_pairs={{0,64},{64,128},{128,192},{1,65},{65,129},{129,193},{2,66},{66,130... | collective-permute-start | bytes 589832 | tf_op jit(solution)/shard_map/ppermute | solution.py:547
  123.6 19.9 %collective-permute-start.4 = (bf16[256,384]{1,0:T(8,128)(2,1)S(1)}, bf16[256,384]{1,0:T(8,128)(2,1)S(1)}, u32[]{:S(2)}, u32[]{:S(2)}) collective-permute-start(bf16[256,384]{1,0:T(8,128)(2,1)S(1)} %pad_maximum_fusion.own_ref), channel_id=1, source_target_pairs={{0,128},{64,192},{1,129},{65,193},{2,130},{66,194},{3,131},{67,195... | collective-permute-start | bytes 589832 | tf_op jit(solution)/shard_map/ppermute | solution.py:547
  128.3 15.3 %collective-permute-start.5 = (bf16[256,384]{1,0:T(8,128)(2,1)S(1)}, bf16[256,384]{1,0:T(8,128)(2,1)}, u32[]{:S(2)}, u32[]{:S(2)}) collective-permute-start(bf16[256,384]{1,0:T(8,128)(2,1)S(1)} %pad_maximum_fusion.own_ref), channel_id=1, source_target_pairs={{0,192},{1,193},{2,194},{3,195},{4,196},{5,197},{6,198},{7,199},{8... | collective-permute-start | bytes 589832 | tf_op jit(solution)/shard_map/ppermute | solution.py:547
  130.2 11.3 %all-to-all-start.3 = ((bf16[8,32,384]{2,1,0:T(8,128)(2,1)}), bf16[8,32,384]{2,1,0:T(8,128)(2,1)S(1)}, u32[]{:S(2)}, u32[]{:S(2)}) async-start(bf16[8,32,384]{2,1,0:T(8,128)(2,1)} %rec.1), calls=%async_computation.3 | async-start | bytes 393216 | tf_op jit(solution)/shard_map/all_to_all | solution.py:551
  146.1 1.5 collective-permute-start.7
  192.9 21.3 %collective-permute-start.12 = (bf16[192,3072]{1,0:T(8,128)(2,1)S(1)}, bf16[192,3072]{1,0:T(8,128)(2,1)S(1)}, u32[]{:S(2)}, u32[]{:S(2)}) collective-permute-start(bf16[192,3072]{1,0:T(8,128)(2,1)S(1)} %get-tuple-element.54.own_hbm), channel_id=1, source_target_pairs={{0,1},{1,0},{2,3},{3,2},{4,5},{5,4},{6,7},{7,6},{8,9},{9,8},{10,11... | collective-permute-start | bytes 3538952 | tf_op jit(solution)/shard_map/ppermute | solution.py:421
  193.3 6.6 %collective-permute-start.8 = (bf16[128,384]{1,0:T(8,128)(2,1)S(1)}, bf16[128,384]{1,0:T(8,128)(2,1)S(1)}, u32[]{:S(2)}, u32[]{:S(2)}) collective-permute-start(bf16[128,384]{1,0:T(8,128)(2,1)S(1)} %bitcast.86), channel_id=1, source_target_pairs={{0,16},{16,0},{1,17},{17,1},{2,18},{18,2},{3,19},{19,3},{4,20},{20... | collective-permute-start | bytes 294920 | tf_op jit(solution)/shard_map/ppermute | solution.py:421
  200.0 11.0 %collective-permute-start.10 = (bf16[256,384]{1,0:T(8,128)(2,1)S(1)}, bf16[256,384]{1,0:T(8,128)(2,1)S(1)}, u32[]{:S(2)}, u32[]{:S(2)}) collective-permute-start(bf16[256,384]{1,0:T(8,128)(2,1)S(1)} %pad_maximum_fusion.1.own_ref), channel_id=1, source_target_pairs={{0,128},{64,192},{1,129},{65,193},{2,130},{66,194},{3,131},{67,195... | collective-permute-start | bytes 589832 | tf_op jit(solution)/shard_map/ppermute | solution.py:547
  202.2 12.1 %collective-permute-start.11 = (bf16[256,384]{1,0:T(8,128)(2,1)S(1)}, bf16[256,384]{1,0:T(8,128)(2,1)S(1)}, u32[]{:S(2)}, u32[]{:S(2)}) collective-permute-start(bf16[256,384]{1,0:T(8,128)(2,1)S(1)} %pad_maximum_fusion.1.own_ref), channel_id=1, source_target_pairs={{0,192},{1,193},{2,194},{3,195},{4,196},{5,197},{6,198},{7,199},{8... | collective-permute-start | bytes 589832 | tf_op jit(solution)/shard_map/ppermute | solution.py:547
  207.4 6.8 %collective-permute-start.9 = (bf16[256,384]{1,0:T(8,128)(2,1)S(1)}, bf16[256,384]{1,0:T(8,128)(2,1)S(1)}, u32[]{:S(2)}, u32[]{:S(2)}) collective-permute-start(bf16[256,384]{1,0:T(8,128)(2,1)S(1)} %pad_maximum_fusion.1.own_ref), channel_id=1, source_target_pairs={{0,64},{64,128},{128,192},{1,65},{65,129},{129,193},{2,66},{66,130... | collective-permute-start | bytes 589832 | tf_op jit(solution)/shard_map/ppermute | solution.py:547
  216.3 1.3 collective-permute-start.13
  258.8 21.9 %collective-permute-start.18 = (bf16[192,3072]{1,0:T(8,128)(2,1)S(1)}, bf16[192,3072]{1,0:T(8,128)(2,1)S(1)}, u32[]{:S(2)}, u32[]{:S(2)}) collective-permute-start(bf16[192,3072]{1,0:T(8,128)(2,1)S(1)} %get-tuple-element.61.own_hbm), channel_id=1, source_target_pairs={{0,1},{1,0},{2,3},{3,2},{4,5},{5,4},{6,7},{7,6},{8,9},{9,8},{10,11... | collective-permute-start | bytes 3538952 | tf_op jit(solution)/shard_map/ppermute | solution.py:421
  259.2 5.4 %collective-permute-start.14 = (bf16[128,384]{1,0:T(8,128)(2,1)S(1)}, bf16[128,384]{1,0:T(8,128)(2,1)S(1)}, u32[]{:S(2)}, u32[]{:S(2)}) collective-permute-start(bf16[128,384]{1,0:T(8,128)(2,1)S(1)} %bitcast.88), channel_id=1, source_target_pairs={{0,16},{16,0},{1,17},{17,1},{2,18},{18,2},{3,19},{19,3},{4,20},{20... | collective-permute-start | bytes 294920 | tf_op jit(solution)/shard_map/ppermute | solution.py:421
  264.6 13.3 %collective-permute-start.15 = (bf16[256,384]{1,0:T(8,128)(2,1)S(1)}, bf16[256,384]{1,0:T(8,128)(2,1)S(1)}, u32[]{:S(2)}, u32[]{:S(2)}) collective-permute-start(bf16[256,384]{1,0:T(8,128)(2,1)S(1)} %pad_maximum_fusion.2.own_ref), channel_id=1, source_target_pairs={{0,64},{64,128},{128,192},{1,65},{65,129},{129,193},{2,66},{66,130... | collective-permute-start | bytes 589832 | tf_op jit(solution)/shard_map/ppermute | solution.py:547
  267.8 10.5 %collective-permute-start.16 = (bf16[256,384]{1,0:T(8,128)(2,1)S(1)}, bf16[256,384]{1,0:T(8,128)(2,1)S(1)}, u32[]{:S(2)}, u32[]{:S(2)}) collective-permute-start(bf16[256,384]{1,0:T(8,128)(2,1)S(1)} %pad_maximum_fusion.2.own_ref), channel_id=1, source_target_pairs={{0,128},{64,192},{1,129},{65,193},{2,130},{66,194},{3,131},{67,195... | collective-permute-start | bytes 589832 | tf_op jit(solution)/shard_map/ppermute | solution.py:547
  275.1 5.6 %collective-permute-start.17 = (bf16[256,384]{1,0:T(8,128)(2,1)S(1)}, bf16[256,384]{1,0:T(8,128)(2,1)S(1)}, u32[]{:S(2)}, u32[]{:S(2)}) collective-permute-start(bf16[256,384]{1,0:T(8,128)(2,1)S(1)} %pad_maximum_fusion.2.own_ref), channel_id=1, source_target_pairs={{0,192},{1,193},{2,194},{3,195},{4,196},{5,197},{6,198},{7,199},{8... | collective-permute-start | bytes 589832 | tf_op jit(solution)/shard_map/ppermute | solution.py:547
  282.7 1.5 collective-permute-start.19
  326.5 20.4 %collective-permute-start.24 = (bf16[192,3072]{1,0:T(8,128)(2,1)S(1)}, bf16[192,3072]{1,0:T(8,128)(2,1)S(1)}, u32[]{:S(2)}, u32[]{:S(2)}) collective-permute-start(bf16[192,3072]{1,0:T(8,128)(2,1)S(1)} %get-tuple-element.68.own_hbm), channel_id=1, source_target_pairs={{0,1},{1,0},{2,3},{3,2},{4,5},{5,4},{6,7},{7,6},{8,9},{9,8},{10,11... | collective-permute-start | bytes 3538952 | tf_op jit(solution)/shard_map/ppermute | solution.py:421
  327.0 4.9 %collective-permute-start.20 = (bf16[128,384]{1,0:T(8,128)(2,1)S(1)}, bf16[128,384]{1,0:T(8,128)(2,1)S(1)}, u32[]{:S(2)}, u32[]{:S(2)}) collective-permute-start(bf16[128,384]{1,0:T(8,128)(2,1)S(1)} %bitcast.84), channel_id=1, source_target_pairs={{0,16},{16,0},{1,17},{17,1},{2,18},{18,2},{3,19},{19,3},{4,20},{20... | collective-permute-start | bytes 294920 | tf_op jit(solution)/shard_map/ppermute | solution.py:421
  331.8 11.8 %collective-permute-start.21 = (bf16[256,384]{1,0:T(8,128)(2,1)S(1)}, bf16[256,384]{1,0:T(8,128)(2,1)S(1)}, u32[]{:S(2)}, u32[]{:S(2)}) collective-permute-start(bf16[256,384]{1,0:T(8,128)(2,1)S(1)} %pad_maximum_fusion.3.own_ref), channel_id=1, source_target_pairs={{0,64},{64,128},{128,192},{1,65},{65,129},{129,193},{2,66},{66,130... | collective-permute-start | bytes 589832 | tf_op jit(solution)/shard_map/ppermute | solution.py:547
  333.2 11.0 %collective-permute-start.22 = (bf16[256,384]{1,0:T(8,128)(2,1)S(1)}, bf16[256,384]{1,0:T(8,128)(2,1)S(1)}, u32[]{:S(2)}, u32[]{:S(2)}) collective-permute-start(bf16[256,384]{1,0:T(8,128)(2,1)S(1)} %pad_maximum_fusion.3.own_ref), channel_id=1, source_target_pairs={{0,128},{64,192},{1,129},{65,193},{2,130},{66,194},{3,131},{67,195... | collective-permute-start | bytes 589832 | tf_op jit(solution)/shard_map/ppermute | solution.py:547
  340.9 6.1 %collective-permute-start.23 = (bf16[256,384]{1,0:T(8,128)(2,1)S(1)}, bf16[256,384]{1,0:T(8,128)(2,1)S(1)}, u32[]{:S(2)}, u32[]{:S(2)}) collective-permute-start(bf16[256,384]{1,0:T(8,128)(2,1)S(1)} %pad_maximum_fusion.3.own_ref), channel_id=1, source_target_pairs={{0,192},{1,193},{2,194},{3,195},{4,196},{5,197},{6,198},{7,199},{8... | collective-permute-start | bytes 589832 | tf_op jit(solution)/shard_map/ppermute | solution.py:547
  349.0 1.3 collective-permute-start.25
  350.2 36.7 %copy-start.1 = (f32[1000,512]{1,0:T(8,128)S(1)}, f32[1000,512]{1,0:T(8,128)}, u32[]{:S(2)}) copy-start(f32[1000,512]{1,0:T(8,128)} %param.15) | copy-start | bytes 6144004
Sparse Core Ops, SparseCore 0:
  30.2 80.4 all-gather.4
  113.1 62.6 all-gather.6
  178.3 64.4 all-gather.8
  245.2 59.4 all-gather.10

commit v6 on v4

--- a/solution.py
+++ b/solution.py
@@ -371,24 +371,27 @@
     return copies
 
 
-def attend_first_kernel(
-    scalars, q_ref, fresh_ref, targets_hbm, rec_ref, stale_ref, own_hbm, other_hbm,
-    keep_out, send_out, weights_out, cache_ref, weight_sems, base_ref, rec_vmem, target_ref, sems,
-):
-    copies = merge_copies(0, targets_hbm, rec_ref, stale_ref, base_ref, rec_vmem, target_ref, sems)
-    weights = weight_copies(own_hbm, other_hbm, weights_out, weight_sems)
-    merge(copies, base_ref, rec_vmem, target_ref, cache_ref)
-    for patch in range(4):
-
-        @pl.when(patch <= scalars[7])
-        def _(patch=patch):
-            cache_ref[PLEN * patch : PLEN * patch + PLEN, :] = jnp.concatenate(
-                [fresh_ref[2 * patch, 0:GROUP, :], fresh_ref[2 * patch + 1, 0:GROUP, :]], axis=0
-            )
-
-    attend(scalars, q_ref, cache_ref, keep_out, send_out)
-    for copy in weights:
-        copy.wait()
+def attend_all_kernel_of(layer):
+    def attend_all_kernel(
+        scalars, q_ref, fresh_ref, targets_hbm, rec_ref, stale_ref, own_hbm, other_hbm,
+        keep_out, send_out, weights_out, cache_ref, weight_sems, base_ref, rec_vmem, target_ref, sems,
+    ):
+        copies = merge_copies(layer, targets_hbm, rec_ref, stale_ref, base_ref, rec_vmem, target_ref, sems)
+        weights = weight_copies(own_hbm, other_hbm, weights_out, weight_sems)
+        merge(copies, base_ref, rec_vmem, target_ref, cache_ref)
+        for patch in range(4):
+
+            @pl.when(patch <= scalars[7])
+            def _(patch=patch):
+                cache_ref[PLEN * patch : PLEN * patch + PLEN, :] = jnp.concatenate(
+                    [fresh_ref[2 * patch, 0:GROUP, :], fresh_ref[2 * patch + 1, 0:GROUP, :]], axis=0
+                )
+
+        attend(scalars, q_ref, cache_ref, keep_out, send_out)
+        for copy in weights:
+            copy.wait()
+
+    return attend_all_kernel
 
 
 def attend_kernel(
@@ -576,11 +579,12 @@
         if layer > 0:
             group = lax.all_gather(current, COL, axis=0, tiled=True)
             group = pltpu.with_memory_space_constraint(group, pltpu.VMEM)
+        to_all = layer in (0, sections - 1)
         queries, fresh, out_own, gates = call(
             qkv_kernel_of(layer),
             (
                 shape_of((GROUP, 384), BF),
-                shape_of((copies, GROUP + REC_GROUP, 384) if layer == 0 else (1, GROUP, 384), BF),
+                shape_of((copies if to_all else 1, GROUP + (REC_GROUP if layer == 0 else 0), 384), BF),
                 shape_of((192, D), BF),
                 shape_of((2, D), F32),
             ),
@@ -592,15 +596,16 @@
         out_other = swapped(out_own, "core")
         attend_out = (half_rows, half_rows, shape_of((2, 192, D), BF))
         attend_scratch = [pltpu.VMEM((1024, 384), BF), pltpu.SemaphoreType.DMA((2,))]
-        if layer == 0:
-            first_fresh = lax.all_to_all(fresh, peers, 0, 0)
+        if to_all:
+            fresh_all = lax.all_to_all(fresh, peers, 0, 0)
+            first_fresh = fresh_all if layer == 0 else first_fresh
             keep, send, weights_out = call(
-                attend_first_kernel,
+                attend_all_kernel_of(layer),
                 attend_out,
                 [SMEM, VMEM, VMEM] + [HBM] * 5,
-                "attend_first",
+                "attend_all",
                 scratch=attend_scratch + merge_scratch(),
-            )(scalars, queries, first_fresh, targets, first_fresh, stale_all, out_own, out_other)
+            )(scalars, queries, fresh_all, targets, first_fresh, stale_all, out_own, out_other)
         else:
             pieces = upwards(fresh[0])
             merged = call(

time: 391 us -> 388 us (level)
  blocking collectives: 215 us -> 231 us
  starting transfers between devices: 47.3 us -> 36.3 us
  waiting for transfers between devices: 48.3 us -> 40.1 us
    all_to_all x0 -> x1, blocking collectives: none -> 18.3 us  [local(): fresh_all = lax.all_to_all(fresh, peers, 0, 0)]
    ppermute x9 -> x6, starting transfers between devices: 28.7 us -> 18.5 us  [upwards(): return [both] + [lax.ppermute(both, 'section', steps) for steps in pairs]]
    ppermute x13 -> x12, waiting for transfers between devices: 17.1 us -> 12.9 us  [swapped(): return lax.ppermute(value, axis, [(0, 1), (1, 0)])]
    ppermute x9 -> x6, waiting for transfers between devices: 9.43 us -> 6.16 us  [upwards(): return [both] + [lax.ppermute(both, 'section', steps) for steps in pairs]]
    pallas_call x5 -> x6, Pallas kernels: 25.1 us -> 28.1 us  [the longest x4 22.1 us: local(): call(qkv_kernel_of(layer), (shape_of((GROUP, 384), BF), shape_of((copies...]
    ppermute x13 -> x12, starting transfers between devices: 8.75 us -> 8.06 us  [swapped(): return lax.ppermute(value, axis, [(0, 1), (1, 0)])]
  transfers between devices with their start and end apart: 28 -> 24, of which waited for: 16 -> 13; matrix products, arithmetic and copies ran while one was open for 3% -> 3% of each run, Pallas kernels for 10% -> 9%
where the time goes in v6:
time: 388 us; the launch traced here: 387 us
  blocking collectives  231 us (60%)
  Pallas kernels  47 us (12%)
  waiting for transfers between devices  40.1 us (10%)
  starting transfers between devices  36.3 us (9%)
  between operations  16.2 us (4%)
  local copies, waits for them, and re-layouts  15 us (4%)
    all_to_all x4, blocking collectives, local(): parts = lax.all_to_all(projected.reshape(8, 8, D), 'z', 0, 0)  81.6 us
    all_gather x3, blocking collectives, local(): group = lax.all_gather(current, COL, axis=0, tiled=True)  50.9 us
    all_to_all x1, blocking collectives, local(): lax.all_to_all(jnp.broadcast_to(rows, (lax.axis_size(everyone), 17, 288))...  25.2 us
    all_gather x1, blocking collectives, local(): gathered = lax.all_gather(payload, COL, axis=0, tiled=True)  22.8 us
    pallas_call x4, Pallas kernels, local(): call(qkv_kernel_of(layer), (shape_of((GROUP, 384), BF), shape_of((copies...  22.1 us
    all_to_all x1, blocking collectives, local(): chunks = lax.all_to_all(packed, 'section', 0, 0)  20.8 us
    ppermute x6, starting transfers between devices, upwards(): return [both] + [lax.ppermute(both, 'section', steps) for steps in pairs]  18.5 us
    all_to_all x1, blocking collectives, local(): fresh_all = lax.all_to_all(fresh, peers, 0, 0)  18.3 us
  transfers between devices with their start and end apart: 24, of which 13 were waited for; matrix products, arithmetic and copies ran while one was open for 3% of the time, Pallas kernels for 9%

profile of v6, /device:TPU:2, one launch (start us, length us, event | category | flops | bytes accessed | tf_op | source)
XLA Modules:
  0.0 387.1 jit_solution(2253813594872056672)
XLA Ops:
  6.5 1.6 pack.1
  8.1 20.8 %all_to_all.50 = bf16[4,384,384]{2,1,0:T(8,128)(2,1)S(1)} all-to-all(bf16[4,384,384]{2,1,0:T(8,128)(2,1)S(1)} %pack.1), channel_id=1, replica_groups=mesh['section'=4,'req'=2,'half'=2,'z'=8,'core'=2] {'section'}, dimensions={0} | all-to-all | bytes 2359296 | tf_op jit(solution)/shard_map/all_to_all | solution.py:486
  32.4 2.2 collective-permute-start
  34.6 1.4 collective-permute-start.1
  36.0 1.7 constant_dynamic-slice_fusion
  38.8 1.6 broadcast_in_dim.47
  40.4 5.0 %all-to-all-start = ((bf16[8,384,384]{2,1,0:T(8,128)(2,1)}), bf16[8,384,384]{2,1,0:T(8,128)(2,1)}, u32[]{:S(2)}, u32[]{:S(2)}) async-start(bf16[8,384,384]{2,1,0:T(8,128)(2,1)} %broadcast_in_dim.47), calls=%async_computation | async-start | bytes 4718592 | tf_op jit(solution)/shard_map/all_to_all | solution.py:494
  50.6 1.4 concatenate.31.scalars
  54.3 22.8 %all_gather.24.gathered_ref.x_ref = bf16[128,3968]{1,0:T(8,128)(2,1)S(1)} all-gather(bf16[8,3968]{1,0:T(8,128)(2,1)S(1)} %fusion.1), channel_id=1, replica_groups=mesh['section'=4,'req'=2,'half'=2,'z'=8,'core'=2] {'z','core'}, dimensions={0}, use_global_device_ids=true | all-gather | bytes 1079296 | tf_op jit(solution)/shard_map/all_gather | solution.py:545
  77.4 25.2 %all_to_all.51.rows_hbm = f32[16,17,288]{2,1,0:T(8,128)S(1)} all-to-all(f32[16,17,288]{2,1,0:T(8,128)S(1)} %broadcast_in_dim.49), channel_id=1, replica_groups=mesh['section'=4,'req'=2,'half'=2,'z'=8,'core'=2] {'section','req','half'}, dimensions={0} | all-to-all | bytes 626688 | tf_op jit(solution)/shard_map/all_to_all | solution.py:552
  103.7 4.6 %rec.1.rec_ref = bf16[1,32,384]{2,1,0:T(8,128)(2,1)S(1)} custom-call(s32[16]{0:T(128)S(1)} %concatenate.31.scalars, bf16[128,3968]{1,0:T(8,128)(2,1)S(1)} %all_gather.24.gathered_ref.x_ref, f32[4,6,3072]{2,1,0:T(8,128)} %reshape.69.mod_hbm, f32[16,17,288]{2,1,0:T(8,128)} %copy-done.8, f32[3,160,128]{2,1,0:T(8,128)} %copy-done.2, bf16[576,3072]{1,0:T(8,128)(2,1)} %bitcast.87), custom_call_target="tpu_custom_call" | custom-call | tf_op jit(solution)/shard_map/rec/pallas_call | solution.py:555
  108.3 2.3 all-gather.5.cloned.1.call-done.packed_ref
  110.6 5.5 %qkv.4 = (bf16[128,384]{1,0:T(8,128)(2,1)S(1)}, bf16[8,160,384]{2,1,0:T(8,128)(2,1)S(1)}, bf16[192,3072]{1,0:T(8,128)(2,1)S(1)}, f32[2,3072]{1,0:T(2,128)S(1)}) custom-call(bf16[128,3968]{1,0:T(8,128)(2,1)S(1)} %all_gather.24.gathered_ref.x_ref, bf16[1,32,384]{2,1,0:T(8,128)(2,1)S(1)} %rec.1.rec_ref, f32[4,6,3072]{2,1,0:T(8,128)} %reshape.69.mod_hbm, ...), custom_call_target="tpu_custom_call" | custom-call | tf_op jit(solution)/shard_map/qkv/pallas_call | solution.py:583
  117.7 4.8 %all-to-all-start.3 = ((bf16[8,160,384]{2,1,0:T(8,128)(2,1)}), bf16[8,160,384]{2,1,0:T(8,128)(2,1)S(1)}, u32[]{:S(2)}, u32[]{:S(2)}) async-start(bf16[8,160,384]{2,1,0:T(8,128)(2,1)} %copy-done.3), calls=%async_computation.3 | async-start | bytes 1966080 | tf_op jit(solution)/shard_map/all_to_all | solution.py:600
  122.6 17.1 %all-to-all-done.3.fresh_ref.rec_ref = bf16[8,160,384]{2,1,0:T(8,128)(2,1)S(1)} async-done(((bf16[8,160,384]{2,1,0:T(8,128)(2,1)}), bf16[8,160,384]{2,1,0:T(8,128)(2,1)S(1)}, u32[]{:S(2)}, u32[]{:S(2)}) %all-to-all-start.3) | async-done | bytes 983072 | tf_op jit(solution)/shard_map/all_to_all | solution.py:600
  140.3 3.0 attend_all.2
  143.4 1.2 collective-permute-done.3.got_ref
  145.2 21.8 %all_to_all.52.parts_ref = bf16[8,8,3072]{2,1,0:T(8,128)(2,1)S(1)} all-to-all(bf16[8,8,3072]{2,1,0:T(8,128)(2,1)S(1)} %bitcast.73), channel_id=1, replica_groups=mesh['section'=4,'req'=2,'half'=2,'z'=8,'core'=2] {'z'}, dimensions={0} | all-to-all | bytes 786432 | tf_op jit(solution)/shard_map/all_to_all | solution.py:628
  167.6 17.0 %all_gather.26.x_ref = bf16[128,3072]{1,0:T(8,128)(2,1)S(1)} all-gather(bf16[8,3072]{1,0:T(8,128)(2,1)S(1)} %residual.4.x_ref), channel_id=1, replica_groups=mesh['section'=4,'req'=2,'half'=2,'z'=8,'core'=2] {'z','core'}, dimensions={0}, use_global_device_ids=true | all-gather | bytes 835584 | tf_op jit(solution)/shard_map/all_gather | solution.py:580
  184.7 5.5 %qkv.5 = (bf16[128,384]{1,0:T(8,128)(2,1)S(1)}, bf16[1,128,384]{2,1,0:T(8,128)(2,1)S(1)}, bf16[192,3072]{1,0:T(8,128)(2,1)S(1)}, f32[2,3072]{1,0:T(2,128)S(1)}) custom-call(bf16[128,3072]{1,0:T(8,128)(2,1)S(1)} %all_gather.26.x_ref, bf16[1,32,384]{2,1,0:T(8,128)(2,1)S(1)} %rec.1.rec_ref, f32[4,6,3072]{2,1,0:T(8,128)} %reshape.69.mod_hbm, ...), custom_call_target="tpu_custom_call" | custom-call | tf_op jit(solution)/shard_map/qkv/pallas_call | solution.py:583
  190.6 1.7 collective-permute-start.4
  192.4 4.3 %collective-permute-done.4 = bf16[128,384]{1,0:T(8,128)(2,1)S(1)} collective-permute-done((bf16[128,384]{1,0:T(8,128)(2,1)S(1)}, bf16[128,384]{1,0:T(8,128)(2,1)S(1)}, u32[]{:S(2)}, u32[]{:S(2)}) %collective-permute-start.4) | collective-permute-done | bytes 98336 | tf_op jit(solution)/shard_map/ppermute | solution.py:447
  196.7 2.7 collective-permute-start.5
  199.5 3.7 collective-permute-start.6
  203.2 1.3 collective-permute-start.7
  204.5 1.5 table.2.table_ref
  206.0 2.7 collective-permute-done.6.back2_ref
  209.3 2.0 attend.2
  211.5 1.2 collective-permute-done.9.got_ref
  213.2 20.5 %all_to_all.53.parts_ref = bf16[8,8,3072]{2,1,0:T(8,128)(2,1)S(1)} all-to-all(bf16[8,8,3072]{2,1,0:T(8,128)(2,1)S(1)} %bitcast.74), channel_id=1, replica_groups=mesh['section'=4,'req'=2,'half'=2,'z'=8,'core'=2] {'z'}, dimensions={0} | all-to-all | bytes 786432 | tf_op jit(solution)/shard_map/all_to_all | solution.py:628
  234.4 16.8 %all_gather.28.x_ref = bf16[128,3072]{1,0:T(8,128)(2,1)S(1)} all-gather(bf16[8,3072]{1,0:T(8,128)(2,1)S(1)} %residual.5.x_ref), channel_id=1, replica_groups=mesh['section'=4,'req'=2,'half'=2,'z'=8,'core'=2] {'z','core'}, dimensions={0}, use_global_device_ids=true | all-gather | bytes 835584 | tf_op jit(solution)/shard_map/all_gather | solution.py:580
  251.2 5.5 %qkv.6 = (bf16[128,384]{1,0:T(8,128)(2,1)S(1)}, bf16[1,128,384]{2,1,0:T(8,128)(2,1)S(1)}, bf16[192,3072]{1,0:T(8,128)(2,1)S(1)}, f32[2,3072]{1,0:T(2,128)S(1)}) custom-call(bf16[128,3072]{1,0:T(8,128)(2,1)S(1)} %all_gather.28.x_ref, bf16[1,32,384]{2,1,0:T(8,128)(2,1)S(1)} %rec.1.rec_ref, f32[4,6,3072]{2,1,0:T(8,128)} %reshape.69.mod_hbm, ...), custom_call_target="tpu_custom_call" | custom-call | tf_op jit(solution)/shard_map/qkv/pallas_call | solution.py:583
  258.2 3.8 collective-permute-done.10
  262.1 1.3 collective-permute-start.11
  263.4 8.1 %collective-permute-start.12 = (bf16[256,384]{1,0:T(8,128)(2,1)S(1)}, bf16[256,384]{1,0:T(8,128)(2,1)S(1)}, u32[]{:S(2)}, u32[]{:S(2)}) collective-permute-start(bf16[256,384]{1,0:T(8,128)(2,1)S(1)} %pad_maximum_fusion.1.own_ref), channel_id=1, source_target_pairs={{0,128},{64,192},{1,129},{65,193},{2,130},{66,194},{3,131},{67,195... | collective-permute-start | bytes 589832 | tf_op jit(solution)/shard_map/ppermute | solution.py:573
  271.5 1.3 collective-permute-start.13
  272.8 1.5 table.3.table_ref
  274.6 2.5 collective-permute-done.13.back3_ref
  277.1 2.0 attend.3
  279.3 1.2 collective-permute-done.15.got_ref
  281.0 20.5 %all_to_all.54.parts_ref = bf16[8,8,3072]{2,1,0:T(8,128)(2,1)S(1)} all-to-all(bf16[8,8,3072]{2,1,0:T(8,128)(2,1)S(1)} %bitcast.75), channel_id=1, replica_groups=mesh['section'=4,'req'=2,'half'=2,'z'=8,'core'=2] {'z'}, dimensions={0} | all-to-all | bytes 786432 | tf_op jit(solution)/shard_map/all_to_all | solution.py:628
  302.2 17.1 %all_gather.30.x_ref = bf16[128,3072]{1,0:T(8,128)(2,1)S(1)} all-gather(bf16[8,3072]{1,0:T(8,128)(2,1)S(1)} %residual.6.x_ref), channel_id=1, replica_groups=mesh['section'=4,'req'=2,'half'=2,'z'=8,'core'=2] {'z','core'}, dimensions={0}, use_global_device_ids=true | all-gather | bytes 835584 | tf_op jit(solution)/shard_map/all_gather | solution.py:580
  319.2 5.5 %qkv.7 = (bf16[128,384]{1,0:T(8,128)(2,1)S(1)}, bf16[8,128,384]{2,1,0:T(8,128)(2,1)S(1)}, bf16[192,3072]{1,0:T(8,128)(2,1)S(1)}, f32[2,3072]{1,0:T(2,128)S(1)}) custom-call(bf16[128,3072]{1,0:T(8,128)(2,1)S(1)} %all_gather.30.x_ref, bf16[1,32,384]{2,1,0:T(8,128)(2,1)S(1)} %rec.1.rec_ref, f32[4,6,3072]{2,1,0:T(8,128)} %reshape.69.mod_hbm, ...), custom_call_target="tpu_custom_call" | custom-call | tf_op jit(solution)/shard_map/qkv/pallas_call | solution.py:583
  325.2 18.3 %all_to_all.55.fresh_ref = bf16[8,128,384]{2,1,0:T(8,128)(2,1)S(1)} all-to-all(bf16[8,128,384]{2,1,0:T(8,128)(2,1)S(1)} %get-tuple-element.63), channel_id=1, replica_groups=mesh['section'=4,'req'=2,'half'=2,'z'=8,'core'=2] {'section','half'}, dimensions={0} | all-to-all | bytes 1572864 | tf_op jit(solution)/shard_map/all_to_all | solution.py:600
  343.5 3.0 attend_all.3
  346.6 1.2 collective-permute-done.17.got_ref
  348.4 18.7 %all_to_all.56.parts_ref = bf16[8,8,3072]{2,1,0:T(8,128)(2,1)S(1)} all-to-all(bf16[8,8,3072]{2,1,0:T(8,128)(2,1)S(1)} %bitcast.76), channel_id=1, replica_groups=mesh['section'=4,'req'=2,'half'=2,'z'=8,'core'=2] {'z'}, dimensions={0} | all-to-all | bytes 786432 | tf_op jit(solution)/shard_map/all_to_all | solution.py:628
  367.9 11.9 %all_to_all.57 = bf16[8,4,3072]{2,1,0:T(4,128)(2,1)S(1)} all-to-all(bf16[8,4,3072]{2,1,0:T(4,128)(2,1)S(1)} %reshape.74), channel_id=1, replica_groups=mesh['section'=4,'req'=2,'half'=2,'z'=8,'core'=2] {'section','req'}, dimensions={0} | all-to-all | bytes 393216 | tf_op jit(solution)/shard_map/all_to_all | solution.py:635
  (116 shorter events, 22.3 us)
Async XLA Ops:
  6.5 42.6 %copy-start = (f32[1000,512]{1,0:T(8,128)S(1)}, f32[1000,512]{1,0:T(8,128)}, u32[]{:S(2)}) copy-start(f32[1000,512]{1,0:T(8,128)} %param.15) | copy-start | bytes 6144004
  6.5 104.1 %all-gather.5.cloned.1.call-start = ((), (), s32[]{:S(2)}) async-start(), calls=%async_computation.10 | async-start | bytes 5013504 | tf_op jit(solution)/shard_map/all_gather | solution.py:488
  28.9 5.7 %copy-start.9 = (bf16[1,1,2,3072]{3,2,1,0:T(2,128)(2,1)S(1)}, bf16[1,1,2,3072]{3,2,1,0:T(2,128)(2,1)}, u32[]{:S(2)}) copy-start(bf16[1,1,2,3072]{3,2,1,0:T(2,128)(2,1)} %param.21) | copy-start | bytes 36868
  30.0 154.6 %all-gather.7.cloned.1.call-start = ((), (), s32[]{:S(2)}) async-start(), calls=%async_computation.11 | async-start | bytes 5013504 | tf_op jit(solution)/shard_map/all_gather | solution.py:488
  30.8 220.4 %all-gather.9.cloned.1.call-start = ((), (), s32[]{:S(2)}) async-start(), calls=%async_computation.12 | async-start | bytes 5013504 | tf_op jit(solution)/shard_map/all_gather | solution.py:488
  32.4 21.7 %collective-permute-start = (bf16[4,2,3072]{2,0,1:T(4,128)(2,1)S(1)}, bf16[4,2,3072]{2,0,1:T(4,128)(2,1)S(1)}, u32[]{:S(2)}, u32[]{:S(2)}) collective-permute-start(bf16[4,2,3072]{2,0,1:T(4,128)(2,1)S(1)} %bitcast.91), channel_id=1, source_target_pairs={{0,32},{32,0},{1,33},{33,1},{2,34},{34,2},{3,35},{35,3},{4,36},{36... | collective-permute-start | bytes 147464 | tf_op jit(solution)/shard_map/ppermute | solution.py:447
  34.6 19.4 %collective-permute-start.1 = (bf16[1,2,3072]{2,1,0:T(2,128)(2,1)S(1)}, bf16[1,2,3072]{2,1,0:T(2,128)(2,1)S(1)}, u32[]{:S(2)}, u32[]{:S(2)}) collective-permute-start(bf16[1,2,3072]{2,1,0:T(2,128)(2,1)S(1)} %bitcast.95), channel_id=1, source_target_pairs={{0,32},{32,0},{1,33},{33,1},{2,34},{34,2},{3,35},{35,3},{4,36},{36... | collective-permute-start | bytes 36872 | tf_op jit(solution)/shard_map/ppermute | solution.py:447
  40.4 5.7 %copy-start.13 = (s32[2,64]{1,0:T(2,128)S(1)}, s32[2,64]{1,0:T(2,128)}, u32[]{:S(2)}) copy-start(s32[2,64]{1,0:T(2,128)} %param.22) | copy-start | bytes 1540
  40.4 6.2 %copy-start.12 = (s32[2,4]{1,0:T(2,128)S(1)}, s32[2,4]{1,0:T(2,128)}, u32[]{:S(2)}) copy-start(s32[2,4]{1,0:T(2,128)} %param.13) | copy-start | bytes 100
  40.4 11.7 %copy-start.4 = (bf16[1,512,288]{1,2,0:T(8,128)(2,1)S(1)}, bf16[1,512,288]{1,2,0:T(8,128)(2,1)}, u32[]{:S(2)}) copy-start(bf16[1,512,288]{1,2,0:T(8,128)(2,1)} %param.16) | copy-start | bytes 884740
  40.4 11.7 %copy-start.7 = (f32[1,128]{1,0:T(1,128)S(1)}, f32[1,128]{1,0:T(1,128)}, u32[]{:S(2)}) copy-start(f32[1,128]{1,0:T(1,128)} %constant.86.clone.rate_ref) | copy-start | bytes 1540
  40.4 13.5 %copy-start.14 = (f32[1,2,64]{2,1,0:T(2,128)S(1)}, f32[1,2,64]{2,1,0:T(2,128)}, u32[]{:S(2)}) copy-start(f32[1,2,64]{2,1,0:T(2,128)} %param.19) | copy-start | bytes 1540
  40.4 36.9 %all-to-all-start = ((bf16[8,384,384]{2,1,0:T(8,128)(2,1)}), bf16[8,384,384]{2,1,0:T(8,128)(2,1)}, u32[]{:S(2)}, u32[]{:S(2)}) async-start(bf16[8,384,384]{2,1,0:T(8,128)(2,1)} %broadcast_in_dim.47), calls=%async_computation | async-start | bytes 4718592 | tf_op jit(solution)/shard_map/all_to_all | solution.py:494
  45.4 273.9 %all-gather.11.cloned.1.call-start = ((), (), s32[]{:S(2)}) async-start(), calls=%async_computation.13 | async-start | bytes 5013504 | tf_op jit(solution)/shard_map/all_gather | solution.py:488
  46.5 5.5 %copy-start.10 = (s32[32]{0:T(128)}, s32[32]{0:T(128)S(1)}, u32[]{:S(2)}) copy-start(s32[32]{0:T(128)S(1)} %reshape.67) | copy-start | bytes 388
  53.1 0.7 copy-start.2
  102.6 1.1 copy-start.8
  116.1 0.6 copy-start.5
  116.7 1.0 copy-start.3
  116.7 5.7 %copy-start.11 = (s32[32]{0:T(128)S(1)}, s32[32]{0:T(128)}, u32[]{:S(2)}) copy-start(s32[32]{0:T(128)} %copy-done.10) | copy-start | bytes 388
  116.8 23.0 %collective-permute-start.2 = (bf16[192,3072]{1,0:T(8,128)(2,1)S(1)}, bf16[192,3072]{1,0:T(8,128)(2,1)S(1)}, u32[]{:S(2)}, u32[]{:S(2)}) collective-permute-start(bf16[192,3072]{1,0:T(8,128)(2,1)S(1)} %get-tuple-element.43.own_hbm), channel_id=1, source_target_pairs={{0,1},{1,0},{2,3},{3,2},{4,5},{5,4},{6,7},{7,6},{8,9},{9,8},{10,11... | collective-permute-start | bytes 3538952 | tf_op jit(solution)/shard_map/ppermute | solution.py:447
  117.7 22.0 %all-to-all-start.3 = ((bf16[8,160,384]{2,1,0:T(8,128)(2,1)}), bf16[8,160,384]{2,1,0:T(8,128)(2,1)S(1)}, u32[]{:S(2)}, u32[]{:S(2)}) async-start(bf16[8,160,384]{2,1,0:T(8,128)(2,1)} %copy-done.3), calls=%async_computation.3 | async-start | bytes 1966080 | tf_op jit(solution)/shard_map/all_to_all | solution.py:600
  143.3 1.3 collective-permute-start.3
  144.6 22.4 %copy-start.6 = (f32[2,3072]{1,0:T(2,128)S(1)}, f32[2,3072]{1,0:T(2,128)}, u32[]{:S(2)}) copy-start(f32[2,3072]{1,0:T(2,128)} %copy-done.5) | copy-start | bytes 73732
  190.2 19.1 %collective-permute-start.8 = (bf16[192,3072]{1,0:T(8,128)(2,1)S(1)}, bf16[192,3072]{1,0:T(8,128)(2,1)S(1)}, u32[]{:S(2)}, u32[]{:S(2)}) collective-permute-start(bf16[192,3072]{1,0:T(8,128)(2,1)S(1)} %get-tuple-element.50.own_hbm), channel_id=1, source_target_pairs={{0,1},{1,0},{2,3},{3,2},{4,5},{5,4},{6,7},{7,6},{8,9},{9,8},{10,11... | collective-permute-start | bytes 3538952 | tf_op jit(solution)/shard_map/ppermute | solution.py:447
  190.6 6.1 %collective-permute-start.4 = (bf16[128,384]{1,0:T(8,128)(2,1)S(1)}, bf16[128,384]{1,0:T(8,128)(2,1)S(1)}, u32[]{:S(2)}, u32[]{:S(2)}) collective-permute-start(bf16[128,384]{1,0:T(8,128)(2,1)S(1)} %bitcast.80), channel_id=1, source_target_pairs={{0,16},{16,0},{1,17},{17,1},{2,18},{18,2},{3,19},{19,3},{4,20},{20... | collective-permute-start | bytes 294920 | tf_op jit(solution)/shard_map/ppermute | solution.py:447
  196.7 9.3 %collective-permute-start.5 = (bf16[256,384]{1,0:T(8,128)(2,1)S(1)}, bf16[256,384]{1,0:T(8,128)(2,1)S(1)}, u32[]{:S(2)}, u32[]{:S(2)}) collective-permute-start(bf16[256,384]{1,0:T(8,128)(2,1)S(1)} %pad_maximum_fusion.own_ref), channel_id=1, source_target_pairs={{0,64},{64,128},{128,192},{1,65},{65,129},{129,193},{2,66},{66,130... | collective-permute-start | bytes 589832 | tf_op jit(solution)/shard_map/ppermute | solution.py:573
  199.5 9.3 %collective-permute-start.6 = (bf16[256,384]{1,0:T(8,128)(2,1)S(1)}, bf16[256,384]{1,0:T(8,128)(2,1)S(1)}, u32[]{:S(2)}, u32[]{:S(2)}) collective-permute-start(bf16[256,384]{1,0:T(8,128)(2,1)S(1)} %pad_maximum_fusion.own_ref), channel_id=1, source_target_pairs={{0,128},{64,192},{1,129},{65,193},{2,130},{66,194},{3,131},{67,195... | collective-permute-start | bytes 589832 | tf_op jit(solution)/shard_map/ppermute | solution.py:573
  203.2 6.1 %collective-permute-start.7 = (bf16[256,384]{1,0:T(8,128)(2,1)S(1)}, bf16[256,384]{1,0:T(8,128)(2,1)S(1)}, u32[]{:S(2)}, u32[]{:S(2)}) collective-permute-start(bf16[256,384]{1,0:T(8,128)(2,1)S(1)} %pad_maximum_fusion.own_ref), channel_id=1, source_target_pairs={{0,192},{1,193},{2,194},{3,195},{4,196},{5,197},{6,198},{7,199},{8... | collective-permute-start | bytes 589832 | tf_op jit(solution)/shard_map/ppermute | solution.py:573
  211.4 1.3 collective-permute-start.9
  256.7 20.4 %collective-permute-start.14 = (bf16[192,3072]{1,0:T(8,128)(2,1)S(1)}, bf16[192,3072]{1,0:T(8,128)(2,1)S(1)}, u32[]{:S(2)}, u32[]{:S(2)}) collective-permute-start(bf16[192,3072]{1,0:T(8,128)(2,1)S(1)} %get-tuple-element.57.own_hbm), channel_id=1, source_target_pairs={{0,1},{1,0},{2,3},{3,2},{4,5},{5,4},{6,7},{7,6},{8,9},{9,8},{10,11... | collective-permute-start | bytes 3538952 | tf_op jit(solution)/shard_map/ppermute | solution.py:447
  257.2 4.9 %collective-permute-start.10 = (bf16[128,384]{1,0:T(8,128)(2,1)S(1)}, bf16[128,384]{1,0:T(8,128)(2,1)S(1)}, u32[]{:S(2)}, u32[]{:S(2)}) collective-permute-start(bf16[128,384]{1,0:T(8,128)(2,1)S(1)} %bitcast.82), channel_id=1, source_target_pairs={{0,16},{16,0},{1,17},{17,1},{2,18},{18,2},{3,19},{19,3},{4,20},{20... | collective-permute-start | bytes 294920 | tf_op jit(solution)/shard_map/ppermute | solution.py:447
  262.1 12.2 %collective-permute-start.11 = (bf16[256,384]{1,0:T(8,128)(2,1)S(1)}, bf16[256,384]{1,0:T(8,128)(2,1)S(1)}, u32[]{:S(2)}, u32[]{:S(2)}) collective-permute-start(bf16[256,384]{1,0:T(8,128)(2,1)S(1)} %pad_maximum_fusion.1.own_ref), channel_id=1, source_target_pairs={{0,64},{64,128},{128,192},{1,65},{65,129},{129,193},{2,66},{66,130... | collective-permute-start | bytes 589832 | tf_op jit(solution)/shard_map/ppermute | solution.py:573
  263.4 11.2 %collective-permute-start.12 = (bf16[256,384]{1,0:T(8,128)(2,1)S(1)}, bf16[256,384]{1,0:T(8,128)(2,1)S(1)}, u32[]{:S(2)}, u32[]{:S(2)}) collective-permute-start(bf16[256,384]{1,0:T(8,128)(2,1)S(1)} %pad_maximum_fusion.1.own_ref), channel_id=1, source_target_pairs={{0,128},{64,192},{1,129},{65,193},{2,130},{66,194},{3,131},{67,195... | collective-permute-start | bytes 589832 | tf_op jit(solution)/shard_map/ppermute | solution.py:573
  271.5 5.7 %collective-permute-start.13 = (bf16[256,384]{1,0:T(8,128)(2,1)S(1)}, bf16[256,384]{1,0:T(8,128)(2,1)S(1)}, u32[]{:S(2)}, u32[]{:S(2)}) collective-permute-start(bf16[256,384]{1,0:T(8,128)(2,1)S(1)} %pad_maximum_fusion.1.own_ref), channel_id=1, source_target_pairs={{0,192},{1,193},{2,194},{3,195},{4,196},{5,197},{6,198},{7,199},{8... | collective-permute-start | bytes 589832 | tf_op jit(solution)/shard_map/ppermute | solution.py:573
  279.2 1.3 collective-permute-start.15
  324.8 18.7 %collective-permute-start.16 = (bf16[192,3072]{1,0:T(8,128)(2,1)S(1)}, bf16[192,3072]{1,0:T(8,128)(2,1)S(1)}, u32[]{:S(2)}, u32[]{:S(2)}) collective-permute-start(bf16[192,3072]{1,0:T(8,128)(2,1)S(1)} %get-tuple-element.64.own_hbm), channel_id=1, source_target_pairs={{0,1},{1,0},{2,3},{3,2},{4,5},{5,4},{6,7},{7,6},{8,9},{9,8},{10,11... | collective-permute-start | bytes 3538952 | tf_op jit(solution)/shard_map/ppermute | solution.py:447
  346.5 1.3 collective-permute-start.17
  347.8 32.8 %copy-start.1 = (f32[1000,512]{1,0:T(8,128)S(1)}, f32[1000,512]{1,0:T(8,128)}, u32[]{:S(2)}) copy-start(f32[1000,512]{1,0:T(8,128)} %param.15) | copy-start | bytes 6144004
Sparse Core Ops, SparseCore 0:
  30.2 80.4 all-gather.4
  113.1 63.4 all-gather.6
  179.1 62.7 all-gather.8
  244.3 62.5 all-gather.10

commit v7 on v6

--- a/solution.py
+++ b/solution.py
@@ -567,10 +567,11 @@
     )(scalars, gathered, *in_hbm, weights_qkv)
     targets = pltpu.with_memory_space_constraint(targets, pltpu.HBM)
 
-    def upwards(fresh):
+    def upwards(fresh, out_own):
         both = jnp.concatenate([fresh, swapped(fresh, "half")], axis=0)
         pairs = [[(i, i + back) for i in range(sections - back)] for back in range(1, sections)]
-        return [both] + [lax.ppermute(both, "section", steps) for steps in pairs]
+        both, out_own = lax.optimization_barrier((both, out_own))
+        return out_own, [both] + [lax.ppermute(both, "section", steps) for steps in pairs]
 
     half_rows = shape_of((64, 256), BF)
     current, group, outs, first_fresh = tokens, gathered, [], None
@@ -593,10 +594,10 @@
             scratch=[pltpu.VMEM((GROUP, D), BF), pltpu.VMEM((576, D), BF), pltpu.SemaphoreType.DMA((32,))]
             + small_scratch(GROUP),
         )(group, rec_fresh, *in_hbm, packed)
-        out_other = swapped(out_own, "core")
         attend_out = (half_rows, half_rows, shape_of((2, 192, D), BF))
         attend_scratch = [pltpu.VMEM((1024, 384), BF), pltpu.SemaphoreType.DMA((2,))]
         if to_all:
+            out_other = swapped(out_own, "core")
             fresh_all = lax.all_to_all(fresh, peers, 0, 0)
             first_fresh = fresh_all if layer == 0 else first_fresh
             keep, send, weights_out = call(
@@ -607,7 +608,8 @@
                 scratch=attend_scratch + merge_scratch(),
             )(scalars, queries, fresh_all, targets, first_fresh, stale_all, out_own, out_other)
         else:
-            pieces = upwards(fresh[0])
+            out_own, pieces = upwards(fresh[0], out_own)
+            out_other = swapped(out_own, "core")
             merged = call(
                 table_kernel_of(layer),
                 shape_of((1024, 384), BF),

time: 388 us -> 390 us (level)
  transfers between devices with their start and end apart: 24 -> 24, of which waited for: 13 -> 14; matrix products, arithmetic and copies ran while one was open for 3% -> 3% of each run, Pallas kernels for 9% -> 9%
where the time goes in v7:
time: 390 us; the launch traced here: 389 us
  blocking collectives  231 us (59%)
  Pallas kernels  47 us (12%)
  waiting for transfers between devices  43.6 us (11%)
  starting transfers between devices  35.5 us (9%)
  between operations  16.2 us (4%)
  local copies, waits for them, and re-layouts  15 us (4%)
    all_to_all x4, blocking collectives, local(): parts = lax.all_to_all(projected.reshape(8, 8, D), 'z', 0, 0)  80.6 us
    all_gather x3, blocking collectives, local(): group = lax.all_gather(current, COL, axis=0, tiled=True)  50.9 us
    all_to_all x1, blocking collectives, local(): lax.all_to_all(jnp.broadcast_to(rows, (lax.axis_size(everyone), 17, 288))...  25.2 us
    all_gather x1, blocking collectives, local(): gathered = lax.all_gather(payload, COL, axis=0, tiled=True)  22.8 us
    pallas_call x4, Pallas kernels, local(): call(qkv_kernel_of(layer), (shape_of((GROUP, 384), BF), shape_of((copies...  22.1 us
    all_to_all x1, blocking collectives, local(): chunks = lax.all_to_all(packed, 'section', 0, 0)  20.8 us
    all_to_all x1, blocking collectives, local(): fresh_all = lax.all_to_all(fresh, peers, 0, 0)  18.3 us
    ppermute x6, starting transfers between devices, upwards(): lax.ppermute(both, 'section', steps)  17.6 us
  transfers between devices with their start and end apart: 24, of which 14 were waited for; matrix products, arithmetic and copies ran while one was open for 3% of the time, Pallas kernels for 9%

profile of v7, /device:TPU:2, one launch (start us, length us, event | category | flops | bytes accessed | tf_op | source)
XLA Modules:
  0.0 388.9 jit_solution(13445444349683378875)
XLA Ops:
  6.5 1.6 pack.1
  8.1 20.8 %all_to_all.50 = bf16[4,384,384]{2,1,0:T(8,128)(2,1)S(1)} all-to-all(bf16[4,384,384]{2,1,0:T(8,128)(2,1)S(1)} %pack.1), channel_id=1, replica_groups=mesh['section'=4,'req'=2,'half'=2,'z'=8,'core'=2] {'section'}, dimensions={0} | all-to-all | bytes 2359296 | tf_op jit(solution)/shard_map/all_to_all | solution.py:486
  32.4 2.2 collective-permute-start
  34.6 1.4 collective-permute-start.1
  36.0 1.7 constant_dynamic-slice_fusion
  38.8 1.6 broadcast_in_dim.47
  40.4 5.0 %all-to-all-start = ((bf16[8,384,384]{2,1,0:T(8,128)(2,1)}), bf16[8,384,384]{2,1,0:T(8,128)(2,1)}, u32[]{:S(2)}, u32[]{:S(2)}) async-start(bf16[8,384,384]{2,1,0:T(8,128)(2,1)} %broadcast_in_dim.47), calls=%async_computation | async-start | bytes 4718592 | tf_op jit(solution)/shard_map/all_to_all | solution.py:494
  50.6 1.4 concatenate.31.scalars
  54.3 22.8 %all_gather.24.gathered_ref.x_ref = bf16[128,3968]{1,0:T(8,128)(2,1)S(1)} all-gather(bf16[8,3968]{1,0:T(8,128)(2,1)S(1)} %fusion.1), channel_id=1, replica_groups=mesh['section'=4,'req'=2,'half'=2,'z'=8,'core'=2] {'z','core'}, dimensions={0}, use_global_device_ids=true | all-gather | bytes 1079296 | tf_op jit(solution)/shard_map/all_gather | solution.py:545
  77.4 25.2 %all_to_all.51.rows_hbm = f32[16,17,288]{2,1,0:T(8,128)S(1)} all-to-all(f32[16,17,288]{2,1,0:T(8,128)S(1)} %broadcast_in_dim.49), channel_id=1, replica_groups=mesh['section'=4,'req'=2,'half'=2,'z'=8,'core'=2] {'section','req','half'}, dimensions={0} | all-to-all | bytes 626688 | tf_op jit(solution)/shard_map/all_to_all | solution.py:552
  103.7 4.6 %rec.1.rec_ref = bf16[1,32,384]{2,1,0:T(8,128)(2,1)S(1)} custom-call(s32[16]{0:T(128)S(1)} %concatenate.31.scalars, bf16[128,3968]{1,0:T(8,128)(2,1)S(1)} %all_gather.24.gathered_ref.x_ref, f32[4,6,3072]{2,1,0:T(8,128)} %reshape.69.mod_hbm, f32[16,17,288]{2,1,0:T(8,128)} %copy-done.8, f32[3,160,128]{2,1,0:T(8,128)} %copy-done.2, bf16[576,3072]{1,0:T(8,128)(2,1)} %bitcast.87), custom_call_target="tpu_custom_call" | custom-call | tf_op jit(solution)/shard_map/rec/pallas_call | solution.py:555
  108.3 2.3 all-gather.5.cloned.1.call-done.packed_ref
  110.6 5.5 %qkv.4 = (bf16[128,384]{1,0:T(8,128)(2,1)S(1)}, bf16[8,160,384]{2,1,0:T(8,128)(2,1)S(1)}, bf16[192,3072]{1,0:T(8,128)(2,1)S(1)}, f32[2,3072]{1,0:T(2,128)S(1)}) custom-call(bf16[128,3968]{1,0:T(8,128)(2,1)S(1)} %all_gather.24.gathered_ref.x_ref, bf16[1,32,384]{2,1,0:T(8,128)(2,1)S(1)} %rec.1.rec_ref, f32[4,6,3072]{2,1,0:T(8,128)} %reshape.69.mod_hbm, ...), custom_call_target="tpu_custom_call" | custom-call | tf_op jit(solution)/shard_map/qkv/pallas_call | solution.py:584
  117.7 4.8 %all-to-all-start.3 = ((bf16[8,160,384]{2,1,0:T(8,128)(2,1)}), bf16[8,160,384]{2,1,0:T(8,128)(2,1)S(1)}, u32[]{:S(2)}, u32[]{:S(2)}) async-start(bf16[8,160,384]{2,1,0:T(8,128)(2,1)} %copy-done.3), calls=%async_computation.3 | async-start | bytes 1966080 | tf_op jit(solution)/shard_map/all_to_all | solution.py:601
  122.6 17.1 %all-to-all-done.3.fresh_ref.rec_ref = bf16[8,160,384]{2,1,0:T(8,128)(2,1)S(1)} async-done(((bf16[8,160,384]{2,1,0:T(8,128)(2,1)}), bf16[8,160,384]{2,1,0:T(8,128)(2,1)S(1)}, u32[]{:S(2)}, u32[]{:S(2)}) %all-to-all-start.3) | async-done | bytes 983072 | tf_op jit(solution)/shard_map/all_to_all | solution.py:601
  140.3 3.0 attend_all.2
  143.4 1.2 collective-permute-done.3.got_ref
  145.2 21.8 %all_to_all.52.parts_ref = bf16[8,8,3072]{2,1,0:T(8,128)(2,1)S(1)} all-to-all(bf16[8,8,3072]{2,1,0:T(8,128)(2,1)S(1)} %bitcast.73), channel_id=1, replica_groups=mesh['section'=4,'req'=2,'half'=2,'z'=8,'core'=2] {'z'}, dimensions={0} | all-to-all | bytes 786432 | tf_op jit(solution)/shard_map/all_to_all | solution.py:630
  167.6 17.0 %all_gather.26.x_ref = bf16[128,3072]{1,0:T(8,128)(2,1)S(1)} all-gather(bf16[8,3072]{1,0:T(8,128)(2,1)S(1)} %residual.4.x_ref), channel_id=1, replica_groups=mesh['section'=4,'req'=2,'half'=2,'z'=8,'core'=2] {'z','core'}, dimensions={0}, use_global_device_ids=true | all-gather | bytes 835584 | tf_op jit(solution)/shard_map/all_gather | solution.py:581
  184.7 5.5 %qkv.5 = (bf16[128,384]{1,0:T(8,128)(2,1)S(1)}, bf16[1,128,384]{2,1,0:T(8,128)(2,1)S(1)}, bf16[192,3072]{1,0:T(8,128)(2,1)S(1)}, f32[2,3072]{1,0:T(2,128)S(1)}) custom-call(bf16[128,3072]{1,0:T(8,128)(2,1)S(1)} %all_gather.26.x_ref, bf16[1,32,384]{2,1,0:T(8,128)(2,1)S(1)} %rec.1.rec_ref, f32[4,6,3072]{2,1,0:T(8,128)} %reshape.69.mod_hbm, ...), custom_call_target="tpu_custom_call" | custom-call | tf_op jit(solution)/shard_map/qkv/pallas_call | solution.py:584
  190.2 1.8 collective-permute-start.4
  192.0 4.7 %collective-permute-done.4 = bf16[128,384]{1,0:T(8,128)(2,1)S(1)} collective-permute-done((bf16[128,384]{1,0:T(8,128)(2,1)S(1)}, bf16[128,384]{1,0:T(8,128)(2,1)S(1)}, u32[]{:S(2)}, u32[]{:S(2)}) %collective-permute-start.4) | collective-permute-done | bytes 98336 | tf_op jit(solution)/shard_map/ppermute | solution.py:447
  196.8 2.6 collective-permute-start.5
  199.4 3.2 collective-permute-start.6
  202.6 1.3 collective-permute-start.7
  203.9 1.5 table.2.table_ref
  205.8 3.8 collective-permute-done.6.back2_ref
  210.5 2.0 attend.2
  214.4 19.9 %all_to_all.53.parts_ref = bf16[8,8,3072]{2,1,0:T(8,128)(2,1)S(1)} all-to-all(bf16[8,8,3072]{2,1,0:T(8,128)(2,1)S(1)} %bitcast.74), channel_id=1, replica_groups=mesh['section'=4,'req'=2,'half'=2,'z'=8,'core'=2] {'z'}, dimensions={0} | all-to-all | bytes 786432 | tf_op jit(solution)/shard_map/all_to_all | solution.py:630
  234.9 16.8 %all_gather.28.x_ref = bf16[128,3072]{1,0:T(8,128)(2,1)S(1)} all-gather(bf16[8,3072]{1,0:T(8,128)(2,1)S(1)} %residual.5.x_ref), channel_id=1, replica_groups=mesh['section'=4,'req'=2,'half'=2,'z'=8,'core'=2] {'z','core'}, dimensions={0}, use_global_device_ids=true | all-gather | bytes 835584 | tf_op jit(solution)/shard_map/all_gather | solution.py:581
  251.8 5.5 %qkv.6 = (bf16[128,384]{1,0:T(8,128)(2,1)S(1)}, bf16[1,128,384]{2,1,0:T(8,128)(2,1)S(1)}, bf16[192,3072]{1,0:T(8,128)(2,1)S(1)}, f32[2,3072]{1,0:T(2,128)S(1)}) custom-call(bf16[128,3072]{1,0:T(8,128)(2,1)S(1)} %all_gather.28.x_ref, bf16[1,32,384]{2,1,0:T(8,128)(2,1)S(1)} %rec.1.rec_ref, f32[4,6,3072]{2,1,0:T(8,128)} %reshape.69.mod_hbm, ...), custom_call_target="tpu_custom_call" | custom-call | tf_op jit(solution)/shard_map/qkv/pallas_call | solution.py:584
  257.3 1.4 collective-permute-start.10
  258.7 3.8 collective-permute-done.10
  262.7 1.3 collective-permute-start.11
  264.0 8.0 %collective-permute-start.12 = (bf16[256,384]{1,0:T(8,128)(2,1)S(1)}, bf16[256,384]{1,0:T(8,128)(2,1)S(1)}, u32[]{:S(2)}, u32[]{:S(2)}) collective-permute-start(bf16[256,384]{1,0:T(8,128)(2,1)S(1)} %pad_maximum_fusion.1.own_ref), channel_id=1, source_target_pairs={{0,128},{64,192},{1,129},{65,193},{2,130},{66,194},{3,131},{67,195... | collective-permute-start | bytes 589832 | tf_op jit(solution)/shard_map/ppermute | solution.py:574
  271.9 1.3 collective-permute-start.13
  273.3 1.5 table.3.table_ref
  274.8 1.7 collective-permute-done.12.back2_ref
  276.4 2.7 collective-permute-done.13.back3_ref
  279.2 2.0 attend.3
  283.1 20.2 %all_to_all.54.parts_ref = bf16[8,8,3072]{2,1,0:T(8,128)(2,1)S(1)} all-to-all(bf16[8,8,3072]{2,1,0:T(8,128)(2,1)S(1)} %bitcast.75), channel_id=1, replica_groups=mesh['section'=4,'req'=2,'half'=2,'z'=8,'core'=2] {'z'}, dimensions={0} | all-to-all | bytes 786432 | tf_op jit(solution)/shard_map/all_to_all | solution.py:630
  303.8 17.1 %all_gather.30.x_ref = bf16[128,3072]{1,0:T(8,128)(2,1)S(1)} all-gather(bf16[8,3072]{1,0:T(8,128)(2,1)S(1)} %residual.6.x_ref), channel_id=1, replica_groups=mesh['section'=4,'req'=2,'half'=2,'z'=8,'core'=2] {'z','core'}, dimensions={0}, use_global_device_ids=true | all-gather | bytes 835584 | tf_op jit(solution)/shard_map/all_gather | solution.py:581
  320.9 5.5 %qkv.7 = (bf16[128,384]{1,0:T(8,128)(2,1)S(1)}, bf16[8,128,384]{2,1,0:T(8,128)(2,1)S(1)}, bf16[192,3072]{1,0:T(8,128)(2,1)S(1)}, f32[2,3072]{1,0:T(2,128)S(1)}) custom-call(bf16[128,3072]{1,0:T(8,128)(2,1)S(1)} %all_gather.30.x_ref, bf16[1,32,384]{2,1,0:T(8,128)(2,1)S(1)} %rec.1.rec_ref, f32[4,6,3072]{2,1,0:T(8,128)} %reshape.69.mod_hbm, ...), custom_call_target="tpu_custom_call" | custom-call | tf_op jit(solution)/shard_map/qkv/pallas_call | solution.py:584
  326.9 18.3 %all_to_all.55.fresh_ref = bf16[8,128,384]{2,1,0:T(8,128)(2,1)S(1)} all-to-all(bf16[8,128,384]{2,1,0:T(8,128)(2,1)S(1)} %get-tuple-element.71), channel_id=1, replica_groups=mesh['section'=4,'req'=2,'half'=2,'z'=8,'core'=2] {'section','half'}, dimensions={0} | all-to-all | bytes 1572864 | tf_op jit(solution)/shard_map/all_to_all | solution.py:601
  345.2 3.0 attend_all.3
  348.3 1.2 collective-permute-done.17.got_ref
  350.1 18.7 %all_to_all.56.parts_ref = bf16[8,8,3072]{2,1,0:T(8,128)(2,1)S(1)} all-to-all(bf16[8,8,3072]{2,1,0:T(8,128)(2,1)S(1)} %bitcast.76), channel_id=1, replica_groups=mesh['section'=4,'req'=2,'half'=2,'z'=8,'core'=2] {'z'}, dimensions={0} | all-to-all | bytes 786432 | tf_op jit(solution)/shard_map/all_to_all | solution.py:630
  369.5 12.0 %all_to_all.57 = bf16[8,4,3072]{2,1,0:T(4,128)(2,1)S(1)} all-to-all(bf16[8,4,3072]{2,1,0:T(4,128)(2,1)S(1)} %reshape.74), channel_id=1, replica_groups=mesh['section'=4,'req'=2,'half'=2,'z'=8,'core'=2] {'section','req'}, dimensions={0} | all-to-all | bytes 393216 | tf_op jit(solution)/shard_map/all_to_all | solution.py:637
  (116 shorter events, 23.4 us)
Async XLA Ops:
  6.5 42.6 %copy-start = (f32[1000,512]{1,0:T(8,128)S(1)}, f32[1000,512]{1,0:T(8,128)}, u32[]{:S(2)}) copy-start(f32[1000,512]{1,0:T(8,128)} %param.15) | copy-start | bytes 6144004
  6.5 104.1 %all-gather.5.cloned.1.call-start = ((), (), s32[]{:S(2)}) async-start(), calls=%async_computation.10 | async-start | bytes 5013504 | tf_op jit(solution)/shard_map/all_gather | solution.py:488
  28.9 5.7 %copy-start.9 = (bf16[1,1,2,3072]{3,2,1,0:T(2,128)(2,1)S(1)}, bf16[1,1,2,3072]{3,2,1,0:T(2,128)(2,1)}, u32[]{:S(2)}) copy-start(bf16[1,1,2,3072]{3,2,1,0:T(2,128)(2,1)} %param.21) | copy-start | bytes 36868
  30.0 154.6 %all-gather.7.cloned.1.call-start = ((), (), s32[]{:S(2)}) async-start(), calls=%async_computation.11 | async-start | bytes 5013504 | tf_op jit(solution)/shard_map/all_gather | solution.py:488
  30.8 221.0 %all-gather.9.cloned.1.call-start = ((), (), s32[]{:S(2)}) async-start(), calls=%async_computation.12 | async-start | bytes 5013504 | tf_op jit(solution)/shard_map/all_gather | solution.py:488
  32.4 21.7 %collective-permute-start = (bf16[4,2,3072]{2,0,1:T(4,128)(2,1)S(1)}, bf16[4,2,3072]{2,0,1:T(4,128)(2,1)S(1)}, u32[]{:S(2)}, u32[]{:S(2)}) collective-permute-start(bf16[4,2,3072]{2,0,1:T(4,128)(2,1)S(1)} %bitcast.91), channel_id=1, source_target_pairs={{0,32},{32,0},{1,33},{33,1},{2,34},{34,2},{3,35},{35,3},{4,36},{36... | collective-permute-start | bytes 147464 | tf_op jit(solution)/shard_map/ppermute | solution.py:447
  34.6 19.4 %collective-permute-start.1 = (bf16[1,2,3072]{2,1,0:T(2,128)(2,1)S(1)}, bf16[1,2,3072]{2,1,0:T(2,128)(2,1)S(1)}, u32[]{:S(2)}, u32[]{:S(2)}) collective-permute-start(bf16[1,2,3072]{2,1,0:T(2,128)(2,1)S(1)} %bitcast.95), channel_id=1, source_target_pairs={{0,32},{32,0},{1,33},{33,1},{2,34},{34,2},{3,35},{35,3},{4,36},{36... | collective-permute-start | bytes 36872 | tf_op jit(solution)/shard_map/ppermute | solution.py:447
  40.4 5.7 %copy-start.13 = (s32[2,64]{1,0:T(2,128)S(1)}, s32[2,64]{1,0:T(2,128)}, u32[]{:S(2)}) copy-start(s32[2,64]{1,0:T(2,128)} %param.22) | copy-start | bytes 1540
  40.4 6.2 %copy-start.12 = (s32[2,4]{1,0:T(2,128)S(1)}, s32[2,4]{1,0:T(2,128)}, u32[]{:S(2)}) copy-start(s32[2,4]{1,0:T(2,128)} %param.13) | copy-start | bytes 100
  40.4 11.7 %copy-start.4 = (bf16[1,512,288]{1,2,0:T(8,128)(2,1)S(1)}, bf16[1,512,288]{1,2,0:T(8,128)(2,1)}, u32[]{:S(2)}) copy-start(bf16[1,512,288]{1,2,0:T(8,128)(2,1)} %param.16) | copy-start | bytes 884740
  40.4 11.7 %copy-start.7 = (f32[1,128]{1,0:T(1,128)S(1)}, f32[1,128]{1,0:T(1,128)}, u32[]{:S(2)}) copy-start(f32[1,128]{1,0:T(1,128)} %constant.86.clone.rate_ref) | copy-start | bytes 1540
  40.4 13.5 %copy-start.14 = (f32[1,2,64]{2,1,0:T(2,128)S(1)}, f32[1,2,64]{2,1,0:T(2,128)}, u32[]{:S(2)}) copy-start(f32[1,2,64]{2,1,0:T(2,128)} %param.19) | copy-start | bytes 1540
  40.4 36.9 %all-to-all-start = ((bf16[8,384,384]{2,1,0:T(8,128)(2,1)}), bf16[8,384,384]{2,1,0:T(8,128)(2,1)}, u32[]{:S(2)}, u32[]{:S(2)}) async-start(bf16[8,384,384]{2,1,0:T(8,128)(2,1)} %broadcast_in_dim.47), calls=%async_computation | async-start | bytes 4718592 | tf_op jit(solution)/shard_map/all_to_all | solution.py:494
  45.4 275.5 %all-gather.11.cloned.1.call-start = ((), (), s32[]{:S(2)}) async-start(), calls=%async_computation.13 | async-start | bytes 5013504 | tf_op jit(solution)/shard_map/all_gather | solution.py:488
  46.5 5.5 %copy-start.10 = (s32[32]{0:T(128)}, s32[32]{0:T(128)S(1)}, u32[]{:S(2)}) copy-start(s32[32]{0:T(128)S(1)} %reshape.67) | copy-start | bytes 388
  53.1 0.7 copy-start.2
  102.6 1.1 copy-start.8
  116.1 0.6 copy-start.5
  116.7 1.0 copy-start.3
  116.7 5.7 %copy-start.11 = (s32[32]{0:T(128)S(1)}, s32[32]{0:T(128)}, u32[]{:S(2)}) copy-start(s32[32]{0:T(128)} %copy-done.10) | copy-start | bytes 388
  116.8 23.0 %collective-permute-start.2 = (bf16[192,3072]{1,0:T(8,128)(2,1)S(1)}, bf16[192,3072]{1,0:T(8,128)(2,1)S(1)}, u32[]{:S(2)}, u32[]{:S(2)}) collective-permute-start(bf16[192,3072]{1,0:T(8,128)(2,1)S(1)} %get-tuple-element.47.own_hbm), channel_id=1, source_target_pairs={{0,1},{1,0},{2,3},{3,2},{4,5},{5,4},{6,7},{7,6},{8,9},{9,8},{10,11... | collective-permute-start | bytes 3538952 | tf_op jit(solution)/shard_map/ppermute | solution.py:447
  117.7 22.0 %all-to-all-start.3 = ((bf16[8,160,384]{2,1,0:T(8,128)(2,1)}), bf16[8,160,384]{2,1,0:T(8,128)(2,1)S(1)}, u32[]{:S(2)}, u32[]{:S(2)}) async-start(bf16[8,160,384]{2,1,0:T(8,128)(2,1)} %copy-done.3), calls=%async_computation.3 | async-start | bytes 1966080 | tf_op jit(solution)/shard_map/all_to_all | solution.py:601
  143.3 1.3 collective-permute-start.3
  144.6 22.4 %copy-start.6 = (f32[2,3072]{1,0:T(2,128)S(1)}, f32[2,3072]{1,0:T(2,128)}, u32[]{:S(2)}) copy-start(f32[2,3072]{1,0:T(2,128)} %copy-done.5) | copy-start | bytes 73732
  190.2 6.5 %collective-permute-start.4 = (bf16[128,384]{1,0:T(8,128)(2,1)S(1)}, bf16[128,384]{1,0:T(8,128)(2,1)S(1)}, u32[]{:S(2)}, u32[]{:S(2)}) collective-permute-start(bf16[128,384]{1,0:T(8,128)(2,1)S(1)} %bitcast.80), channel_id=1, source_target_pairs={{0,16},{16,0},{1,17},{17,1},{2,18},{18,2},{3,19},{19,3},{4,20},{20... | collective-permute-start | bytes 294920 | tf_op jit(solution)/shard_map/ppermute | solution.py:447
  196.7 13.7 %collective-permute-start.8 = (bf16[192,3072]{1,0:T(8,128)(2,1)S(1)}, bf16[192,3072]{1,0:T(8,128)(2,1)S(1)}, u32[]{:S(2)}, u32[]{:S(2)}) collective-permute-start(bf16[192,3072]{1,0:T(8,128)(2,1)S(1)} %get-tuple-element.56.own_hbm), channel_id=1, source_target_pairs={{0,1},{1,0},{2,3},{3,2},{4,5},{5,4},{6,7},{7,6},{8,9},{9,8},{10,11... | collective-permute-start | bytes 3538952 | tf_op jit(solution)/shard_map/ppermute | solution.py:447
  196.8 8.9 %collective-permute-start.5 = (bf16[256,384]{1,0:T(8,128)(2,1)S(1)}, bf16[256,384]{1,0:T(8,128)(2,1)S(1)}, u32[]{:S(2)}, u32[]{:S(2)}) collective-permute-start(bf16[256,384]{1,0:T(8,128)(2,1)S(1)} %pad_maximum_fusion.own_ref), channel_id=1, source_target_pairs={{0,64},{64,128},{128,192},{1,65},{65,129},{129,193},{2,66},{66,130... | collective-permute-start | bytes 589832 | tf_op jit(solution)/shard_map/ppermute | solution.py:574
  199.4 10.2 %collective-permute-start.6 = (bf16[256,384]{1,0:T(8,128)(2,1)S(1)}, bf16[256,384]{1,0:T(8,128)(2,1)S(1)}, u32[]{:S(2)}, u32[]{:S(2)}) collective-permute-start(bf16[256,384]{1,0:T(8,128)(2,1)S(1)} %pad_maximum_fusion.own_ref), channel_id=1, source_target_pairs={{0,128},{64,192},{1,129},{65,193},{2,130},{66,194},{3,131},{67,195... | collective-permute-start | bytes 589832 | tf_op jit(solution)/shard_map/ppermute | solution.py:574
  202.6 7.9 %collective-permute-start.7 = (bf16[256,384]{1,0:T(8,128)(2,1)S(1)}, bf16[256,384]{1,0:T(8,128)(2,1)S(1)}, u32[]{:S(2)}, u32[]{:S(2)}) collective-permute-start(bf16[256,384]{1,0:T(8,128)(2,1)S(1)} %pad_maximum_fusion.own_ref), channel_id=1, source_target_pairs={{0,192},{1,193},{2,194},{3,195},{4,196},{5,197},{6,198},{7,199},{8... | collective-permute-start | bytes 589832 | tf_op jit(solution)/shard_map/ppermute | solution.py:574
  212.5 1.3 collective-permute-start.9
  257.3 5.2 %collective-permute-start.10 = (bf16[128,384]{1,0:T(8,128)(2,1)S(1)}, bf16[128,384]{1,0:T(8,128)(2,1)S(1)}, u32[]{:S(2)}, u32[]{:S(2)}) collective-permute-start(bf16[128,384]{1,0:T(8,128)(2,1)S(1)} %bitcast.82), channel_id=1, source_target_pairs={{0,16},{16,0},{1,17},{17,1},{2,18},{18,2},{3,19},{19,3},{4,20},{20... | collective-permute-start | bytes 294920 | tf_op jit(solution)/shard_map/ppermute | solution.py:447
  262.6 16.6 %collective-permute-start.14 = (bf16[192,3072]{1,0:T(8,128)(2,1)S(1)}, bf16[192,3072]{1,0:T(8,128)(2,1)S(1)}, u32[]{:S(2)}, u32[]{:S(2)}) collective-permute-start(bf16[192,3072]{1,0:T(8,128)(2,1)S(1)} %get-tuple-element.65.own_hbm), channel_id=1, source_target_pairs={{0,1},{1,0},{2,3},{3,2},{4,5},{5,4},{6,7},{7,6},{8,9},{9,8},{10,11... | collective-permute-start | bytes 3538952 | tf_op jit(solution)/shard_map/ppermute | solution.py:447
  262.7 12.1 %collective-permute-start.11 = (bf16[256,384]{1,0:T(8,128)(2,1)S(1)}, bf16[256,384]{1,0:T(8,128)(2,1)S(1)}, u32[]{:S(2)}, u32[]{:S(2)}) collective-permute-start(bf16[256,384]{1,0:T(8,128)(2,1)S(1)} %pad_maximum_fusion.1.own_ref), channel_id=1, source_target_pairs={{0,64},{64,128},{128,192},{1,65},{65,129},{129,193},{2,66},{66,130... | collective-permute-start | bytes 589832 | tf_op jit(solution)/shard_map/ppermute | solution.py:574
  264.0 12.5 %collective-permute-start.12 = (bf16[256,384]{1,0:T(8,128)(2,1)S(1)}, bf16[256,384]{1,0:T(8,128)(2,1)S(1)}, u32[]{:S(2)}, u32[]{:S(2)}) collective-permute-start(bf16[256,384]{1,0:T(8,128)(2,1)S(1)} %pad_maximum_fusion.1.own_ref), channel_id=1, source_target_pairs={{0,128},{64,192},{1,129},{65,193},{2,130},{66,194},{3,131},{67,195... | collective-permute-start | bytes 589832 | tf_op jit(solution)/shard_map/ppermute | solution.py:574
  271.9 7.2 %collective-permute-start.13 = (bf16[256,384]{1,0:T(8,128)(2,1)S(1)}, bf16[256,384]{1,0:T(8,128)(2,1)S(1)}, u32[]{:S(2)}, u32[]{:S(2)}) collective-permute-start(bf16[256,384]{1,0:T(8,128)(2,1)S(1)} %pad_maximum_fusion.1.own_ref), channel_id=1, source_target_pairs={{0,192},{1,193},{2,194},{3,195},{4,196},{5,197},{6,198},{7,199},{8... | collective-permute-start | bytes 589832 | tf_op jit(solution)/shard_map/ppermute | solution.py:574
  281.2 1.3 collective-permute-start.15
  326.4 18.7 %collective-permute-start.16 = (bf16[192,3072]{1,0:T(8,128)(2,1)S(1)}, bf16[192,3072]{1,0:T(8,128)(2,1)S(1)}, u32[]{:S(2)}, u32[]{:S(2)}) collective-permute-start(bf16[192,3072]{1,0:T(8,128)(2,1)S(1)} %get-tuple-element.72.own_hbm), channel_id=1, source_target_pairs={{0,1},{1,0},{2,3},{3,2},{4,5},{5,4},{6,7},{7,6},{8,9},{9,8},{10,11... | collective-permute-start | bytes 3538952 | tf_op jit(solution)/shard_map/ppermute | solution.py:447
  348.2 1.3 collective-permute-start.17
  349.5 32.9 %copy-start.1 = (f32[1000,512]{1,0:T(8,128)S(1)}, f32[1000,512]{1,0:T(8,128)}, u32[]{:S(2)}) copy-start(f32[1000,512]{1,0:T(8,128)} %param.15) | copy-start | bytes 6144004
Sparse Core Ops, SparseCore 0:
  30.2 80.4 all-gather.4
  113.1 63.4 all-gather.6
  179.1 63.3 all-gather.8
  244.9 62.9 all-gather.10
